TPU v7x, 32 devices: a whole 2x2x4 slice. The times are simulated.
32 devices in a mesh: dp: 8 (over y, x, core), mp: 4 (over z).
Axes of the slice: x: 2, y: 2, z: 4, core: 2. Of those that a mesh axis runs over, the one named last changes fastest.
Arguments:
- tokens: bfloat16 [8192, 1152], P(('dp', 'mp')), may hold values from -6 to 6
- conditioning: bfloat16 [32, 1152], P(('dp', 'mp')), may hold values from -6 to 6
- routes: int32 [32, 256], P(('dp', 'mp')), may hold values from 0 to 255, each once within a row
- keep_count: int32 [32], P(('dp', 'mp')), may hold values from 64 to 192, as said below
- cotangent: bfloat16 [8192, 1152], P(('dp', 'mp')), may hold values from -6 to 6
- ada_weight: bfloat16 [6912, 1152], replicated, may hold values from -0.1875 to 0.1875
- ada_bias: bfloat16 [6912], replicated, may hold values from -3 to 3
- qkv_weight: bfloat16 [3, 1152, 1152], P(None, 'mp'), may hold values from -0.1875 to 0.1875
- qv_bias: bfloat16 [2, 1152], P(None, 'mp'), may hold values from -3 to 3
- out_weight: bfloat16 [1152, 1152], P('mp'), may hold values from -1.75 to 1.75
- out_bias: bfloat16 [1152], replicated, may hold values from -3 to 3
- up_weight: bfloat16 [4608, 1152], P('mp'), may hold values from -0.1875 to 0.1875
- up_bias: bfloat16 [4608], P('mp'), may hold values from -3 to 3
- down_weight: bfloat16 [4608, 1152], P('mp'), may hold values from -0.1875 to 0.1875
- down_bias: bfloat16 [1152], replicated, may hold values from -3 to 3
Outputs:
- layer_out: bfloat16 [8192, 1152], P(('dp', 'mp'))
- tokens_grad: bfloat16 [8192, 1152], P(('dp', 'mp'))
- ada_weight_grad: float32 [6912, 1152], P(('dp', 'mp'))
- ada_bias_grad: float32 [6912], P(('dp', 'mp'))
- qkv_weight_grad: float32 [3, 1152, 1152], P(None, 'mp')
- qv_bias_grad: float32 [2, 1152], P(None, 'mp')
- out_weight_grad: float32 [1152, 1152], P('mp')
- out_bias_grad: float32 [1152], replicated
- up_weight_grad: float32 [4608, 1152], P('mp')
- up_bias_grad: float32 [4608], P('mp')
- down_weight_grad: float32 [4608, 1152], P('mp')
- down_bias_grad: float32 [1152], replicated
Inputs may be any that keep to these rules, and one draw needn't show every extreme that they name: `routes`: each row is a permutation of the image's 256 token positions. An image keeps the first keep_count of its routed slots; some image keeps exactly 192.
All inputs are finite; a program needn't handle non-finite values.
Results may differ from a plain program's by a relative error of at most 0.02.
The roundings to bfloat16 on the way count: a program that leaves them out, or rounds other values in their place, can miss the bound.
Values may be sent and summed in bfloat16 or wider, within the bound.
No kernel may reach another device: no remote copies, remote signals or barrier semaphores. Data moves between devices by JAX's collectives and lax.ppermute only.
A program may use at most 192 MiB of HBM per device.

v0:
```python
import math

import jax
import jax.numpy as jnp
from jax import lax
from jax.sharding import PartitionSpec as P

HEADS = 16


EPS = 1e-06


def norm_rows(rows):
    mean = jnp.mean(rows, axis=-1, keepdims=True)
    centred = rows - mean
    rstd = lax.rsqrt(jnp.mean(centred * centred, axis=-1, keepdims=True) + EPS)
    return (centred * rstd, rstd)


def norm_back(normed, rstd, grad):
    return rstd * (
        grad
        - jnp.mean(grad, axis=-1, keepdims=True)
        - normed * jnp.mean(grad * normed, axis=-1, keepdims=True)
    )


def place_rows(base, spots, rows):
    return base.at[spots].set(rows)


def right_dot(left, right):
    return lax.dot_general(
        left, right, (((1,), (1,)), ((), ())), preferred_element_type=jnp.float32
    )


def left_dot(left, right):
    return lax.dot_general(
        left, right, (((0,), (0,)), ((), ())), preferred_element_type=jnp.float32
    )


def per_device(
    tokens,
    conditioning,
    routes,
    keep_count,
    cotangent,
    ada_weight,
    ada_bias,
    qkv_weight,
    qv_bias,
    out_weight,
    out_bias,
    up_weight,
    up_bias,
    down_weight,
    down_bias,
):
    images = conditioning.shape[0]
    model_width = tokens.shape[1]
    patches = routes.shape[1]
    slot_count = 3 * patches // 4
    own_rows = images * slot_count
    head_cols = qkv_weight.shape[1]
    head_dim = model_width // HEADS
    heads_here = head_cols // head_dim
    score_scale = 1.0 / math.sqrt(head_dim)
    silu_cond = jax.nn.silu(conditioning.astype(jnp.float32)).astype(jnp.bfloat16)
    modulation = right_dot(silu_cond, ada_weight) + ada_bias.astype(jnp.float32)
    blocks = [
        modulation[:, index * model_width : (index + 1) * model_width][:, None, :]
        for index in range(6)
    ]
    shift_one, scale_one, gate_one, shift_two, scale_two, gate_two = blocks
    picks = routes[:, :slot_count]
    image_tokens = tokens.reshape(images, patches, model_width)
    routed = jnp.take_along_axis(image_tokens, picks[:, :, None], axis=1).astype(jnp.float32)
    live = (lax.broadcasted_iota(jnp.int32, (images, slot_count), 1) < keep_count[:, None]).astype(
        jnp.float32
    )
    live_col = live[:, :, None]
    normed_one, rstd_one = norm_rows(routed)
    mixed_one = (
        (normed_one * (1.0 + scale_one) + shift_one)
        .astype(jnp.bfloat16)
        .reshape(own_rows, model_width)
    )
    group_in, group_live = (
        lax.all_gather(mixed_one, "mp", axis=0, tiled=True),
        lax.all_gather(live.astype(jnp.bfloat16).reshape(own_rows), "mp", axis=0, tiled=True),
    )
    group_rows = group_in.shape[0]
    group_images = group_rows // slot_count
    key_live = group_live.reshape(group_images, 1, 1, slot_count) > 0
    w_flat = qkv_weight.reshape(3 * head_cols, model_width)
    qkv_rows = right_dot(group_in, w_flat)
    query = (qkv_rows[:, :head_cols] + qv_bias[0].astype(jnp.float32)).astype(jnp.bfloat16)
    key = qkv_rows[:, head_cols : 2 * head_cols].astype(jnp.bfloat16)
    value = (qkv_rows[:, 2 * head_cols :] + qv_bias[1].astype(jnp.float32)).astype(jnp.bfloat16)
    query_four = query.reshape(group_images, slot_count, heads_here, head_dim)
    key_four = key.reshape(group_images, slot_count, heads_here, head_dim)
    value_four = value.reshape(group_images, slot_count, heads_here, head_dim)
    scores = (
        jnp.einsum("bthd,bshd->bhts", query_four, key_four, preferred_element_type=jnp.float32)
        * score_scale
    )
    scores = jnp.where(key_live, scores, -1e30)
    top_score = jnp.max(scores, axis=-1, keepdims=True)
    raised = jnp.exp(scores - top_score)
    weights = raised / jnp.sum(raised, axis=-1, keepdims=True)
    weights_low = weights.astype(jnp.bfloat16)
    attended = jnp.einsum(
        "bhts,bshd->bthd", weights_low, value_four, preferred_element_type=jnp.float32
    )
    attended = attended.reshape(group_rows, head_cols).astype(jnp.bfloat16)
    branch_flat = lax.psum_scatter(
        jnp.dot(attended, out_weight, preferred_element_type=jnp.float32).astype(jnp.bfloat16),
        "mp",
        scatter_dimension=0,
        tiled=True,
    ).astype(jnp.float32)
    branch_one = (branch_flat + out_bias.astype(jnp.float32)).reshape(
        images, slot_count, model_width
    )
    hidden_one = routed + live_col * gate_one * branch_one
    normed_two, rstd_two = norm_rows(hidden_one)
    mixed_two = (
        (normed_two * (1.0 + scale_two) + shift_two)
        .astype(jnp.bfloat16)
        .reshape(own_rows, model_width)
    )
    group_two = lax.all_gather(mixed_two, "mp", axis=0, tiled=True)
    before = right_dot(group_two, up_weight) + up_bias.astype(jnp.float32)
    active = jax.nn.gelu(before, approximate=True).astype(jnp.bfloat16)
    branch_two = lax.psum_scatter(
        jnp.dot(active, down_weight, preferred_element_type=jnp.float32).astype(jnp.bfloat16),
        "mp",
        scatter_dimension=0,
        tiled=True,
    ).astype(jnp.float32) + down_bias.astype(jnp.float32)
    branch_two = branch_two.reshape(images, slot_count, model_width)
    hidden_two = hidden_one + live_col * gate_two * branch_two
    layer_out = jax.vmap(place_rows)(image_tokens.astype(jnp.float32), picks, hidden_two)
    layer_out = layer_out.reshape(images * patches, model_width).astype(jnp.bfloat16)
    grad_tokens = cotangent.astype(jnp.float32).reshape(images, patches, model_width)
    grad_two = jnp.take_along_axis(grad_tokens, picks[:, :, None], axis=1)
    gate_two_grad = jnp.sum(live_col * grad_two * branch_two, axis=1)
    branch_two_grad = (
        (live_col * gate_two * grad_two).astype(jnp.bfloat16).reshape(own_rows, model_width)
    )
    down_grad = lax.all_gather(branch_two_grad, "mp", axis=0, tiled=True)
    down_bias_grad = jnp.sum(down_grad.astype(jnp.float32), axis=0)
    down_weight_grad = left_dot(active, down_grad)
    active_grad = right_dot(down_grad, down_weight)
    _, gelu_pull = jax.vjp(lambda inner: jax.nn.gelu(inner, approximate=True), before)
    before_grad = gelu_pull(active_grad)[0].astype(jnp.bfloat16)
    up_bias_grad = jnp.sum(before_grad.astype(jnp.float32), axis=0)
    up_weight_grad = left_dot(before_grad, group_two)
    mixed_two_grad = (
        lax.psum_scatter(
            jnp.dot(before_grad, up_weight, preferred_element_type=jnp.float32).astype(
                jnp.bfloat16
            ),
            "mp",
            scatter_dimension=0,
            tiled=True,
        )
        .astype(jnp.float32)
        .reshape(images, slot_count, model_width)
    )
    shift_two_grad = jnp.sum(mixed_two_grad, axis=1)
    scale_two_grad = jnp.sum(mixed_two_grad * normed_two, axis=1)
    grad_one = grad_two + norm_back(normed_two, rstd_two, mixed_two_grad * (1.0 + scale_two))
    gate_one_grad = jnp.sum(live_col * grad_one * branch_one, axis=1)
    branch_one_grad = (
        (live_col * gate_one * grad_one).astype(jnp.bfloat16).reshape(own_rows, model_width)
    )
    proj_grad = lax.all_gather(branch_one_grad, "mp", axis=0, tiled=True)
    out_bias_grad = jnp.sum(proj_grad.astype(jnp.float32), axis=0)
    out_weight_grad = left_dot(attended, proj_grad)
    attended_grad = right_dot(proj_grad, out_weight).astype(jnp.bfloat16)
    attended_four = attended_grad.reshape(group_images, slot_count, heads_here, head_dim)
    weight_grad = jnp.einsum(
        "bthd,bshd->bhts", attended_four, value_four, preferred_element_type=jnp.float32
    )
    value_grad = jnp.einsum(
        "bhts,bthd->bshd", weights_low, attended_four, preferred_element_type=jnp.float32
    )
    row_total = jnp.sum(weights * weight_grad, axis=-1, keepdims=True)
    score_grad = (weights * (weight_grad - row_total)).astype(jnp.bfloat16)
    query_grad = (
        jnp.einsum("bhts,bshd->bthd", score_grad, key_four, preferred_element_type=jnp.float32)
        * score_scale
    )
    key_grad = (
        jnp.einsum("bhts,bthd->bshd", score_grad, query_four, preferred_element_type=jnp.float32)
        * score_scale
    )
    qkv_grad = jnp.concatenate(
        [
            query_grad.reshape(group_rows, head_cols),
            key_grad.reshape(group_rows, head_cols),
            value_grad.reshape(group_rows, head_cols),
        ],
        axis=1,
    ).astype(jnp.bfloat16)
    qkv_weight_grad = left_dot(qkv_grad, group_in).reshape(3, head_cols, model_width)
    column_sums = jnp.sum(qkv_grad.astype(jnp.float32), axis=0)
    qv_bias_grad = jnp.stack([column_sums[:head_cols], column_sums[2 * head_cols :]], axis=0)
    mixed_one_grad = (
        lax.psum_scatter(
            jnp.dot(qkv_grad, w_flat, preferred_element_type=jnp.float32).astype(jnp.bfloat16),
            "mp",
            scatter_dimension=0,
            tiled=True,
        )
        .astype(jnp.float32)
        .reshape(images, slot_count, model_width)
    )
    shift_one_grad = jnp.sum(mixed_one_grad, axis=1)
    scale_one_grad = jnp.sum(mixed_one_grad * normed_one, axis=1)
    routed_grad = grad_one + norm_back(normed_one, rstd_one, mixed_one_grad * (1.0 + scale_one))
    tokens_grad = jax.vmap(place_rows)(grad_tokens, picks, routed_grad)
    tokens_grad = tokens_grad.reshape(images * patches, model_width).astype(jnp.bfloat16)
    modulation_grad = jnp.concatenate(
        [
            shift_one_grad,
            scale_one_grad,
            gate_one_grad,
            shift_two_grad,
            scale_two_grad,
            gate_two_grad,
        ],
        axis=1,
    ).astype(jnp.bfloat16)
    group_grad, group_cond = (
        lax.all_gather(modulation_grad, "mp", axis=0, tiled=True),
        lax.all_gather(silu_cond, "mp", axis=0, tiled=True),
    )
    data_count = lax.axis_size("dp")
    model_count = lax.axis_size("mp")
    rows_each = modulation_grad.shape[1] // (data_count * model_count)
    grouped = group_grad.shape[0]
    arranged = group_grad.reshape(grouped, data_count, model_count, rows_each)
    chosen = lax.dynamic_index_in_dim(arranged, lax.axis_index("mp"), 2, keepdims=False)
    chosen = chosen.reshape(grouped, data_count * rows_each)
    part_weight = left_dot(chosen, group_cond)
    part_bias = jnp.sum(chosen.astype(jnp.float32), axis=0)
    ada_weight_grad, ada_bias_grad = (
        lax.psum_scatter(
            part_weight.astype(jnp.bfloat16), "dp", scatter_dimension=0, tiled=True
        ).astype(jnp.float32),
        lax.psum_scatter(
            part_bias.astype(jnp.bfloat16), "dp", scatter_dimension=0, tiled=True
        ).astype(jnp.float32),
    )
    summed = (
        lax.psum(qkv_weight_grad.astype(jnp.bfloat16), "dp").astype(jnp.float32),
        lax.psum(qv_bias_grad.astype(jnp.bfloat16), "dp").astype(jnp.float32),
        lax.psum(out_weight_grad.astype(jnp.bfloat16), "dp").astype(jnp.float32),
        lax.psum(out_bias_grad.astype(jnp.bfloat16), "dp").astype(jnp.float32),
        lax.psum(up_weight_grad.astype(jnp.bfloat16), "dp").astype(jnp.float32),
        lax.psum(up_bias_grad.astype(jnp.bfloat16), "dp").astype(jnp.float32),
        lax.psum(down_weight_grad.astype(jnp.bfloat16), "dp").astype(jnp.float32),
        lax.psum(down_bias_grad.astype(jnp.bfloat16), "dp").astype(jnp.float32),
    )
    return (
        layer_out,
        tokens_grad,
        ada_weight_grad,
        ada_bias_grad,
        summed[0],
        summed[1],
        summed[2],
        summed[3],
        summed[4],
        summed[5],
        summed[6],
        summed[7],
    )


def solution(mesh):
    in_specs = (
        P(("dp", "mp"), None),
        P(("dp", "mp"), None),
        P(("dp", "mp"), None),
        P(("dp", "mp")),
        P(("dp", "mp"), None),
        P(),
        P(),
        P(None, "mp", None),
        P(None, "mp"),
        P("mp", None),
        P(),
        P("mp", None),
        P("mp"),
        P("mp", None),
        P(),
    )
    out_specs = (
        P(("dp", "mp"), None),
        P(("dp", "mp"), None),
        P(("dp", "mp"), None),
        P(("dp", "mp")),
        P(None, "mp", None),
        P(None, "mp"),
        P("mp", None),
        P(),
        P("mp", None),
        P("mp"),
        P("mp", None),
        P(),
    )
    return jax.shard_map(
        per_device, mesh=mesh, in_specs=in_specs, out_specs=out_specs, check_vma=False
    )
```

profile of v0, /device:TPU:0, one launch (start us, length us, event | category | flops | bytes accessed | tf_op | source)
XLA Modules:
  0.0 598.8 jit_solution(2476086887556479806)
XLA Ops:
  9.4 9.8 %convolution_reduce_fusion = f32[6912]{0:T(1024)S(1)} fusion(bf16[6912,1152]{1,0:T(8,128)(2,1)} %param.20, bf16[1,1152]{1,0:T(2,128)(2,1)} %param.16), kind=kOutput, calls=%fused_computation.49 | convolution fusion | flops 15932160 | bytes 15955200 | tf_op jit(solution)/shard_map/dot_general | solution.py:34
  26.8 13.7 %all-reduce = bf16[768]{0:T(1024)(128)(2,1)S(1)} all-reduce(bf16[768]{0:T(1024)(128)(2,1)S(1)} %dynamic-update-slice), channel_id=1, replica_groups=mesh['dp'=8,'mp'=4] {'mp'}, use_global_device_ids=true, to_apply=%add | all-reduce | flops 768 | bytes 3072
  41.1 26.6 %all-gather.7.cloned.1.call-done = bf16[768,1152]{1,0:T(8,128)(2,1)} async-done(((bf16[192,1152]{1,0:T(8,128)(2,1)}), bf16[768,1152]{1,0:T(8,128)(2,1)}) %all-gather.7.cloned.1.call-update) | async-done | bytes 1769488 | tf_op jit(solution)/shard_map/all_gather | solution.py:92
  67.8 4.0 fusion.88
  86.9 3.7 convolution_convert_fusion.6
  93.9 3.7 gather_fusion.1
  98.2 29.8 %reduce-scatter.8.cloned.1.call-done = bf16[192,1152]{1,0:T(8,128)(2,1)} async-done(((bf16[768,1152]{1,0:T(8,128)(2,1)}), bf16[192,1152]{1,0:T(8,128)(2,1)}) %reduce-scatter.8.cloned.1.call-update) | async-done | bytes 442384 | tf_op jit(solution)/shard_map/reduce_scatter | solution.py:119
  130.1 3.1 fusion.48
  137.9 34.7 %all-gather.11.cloned.1.call-done = bf16[768,1152]{1,0:T(8,128)(2,1)} async-done(((bf16[192,1152]{1,0:T(8,128)(2,1)}), bf16[768,1152]{1,0:T(8,128)(2,1)}) %all-gather.11.cloned.1.call-update) | async-done | bytes 1769488 | tf_op jit(solution)/shard_map/all_gather | solution.py:154
  172.6 6.8 %fusion.89 = f32[768,1152]{1,0:T(8,128)} fusion(bf16[768,1152]{1,0:T(8,128)(2,1)} %all-gather.11.cloned.1.call-done, bf16[1152,1152]{1,0:T(8,128)(2,1)} %param.28), kind=kOutput, calls=%fused_computation.177 | convolution fusion | flops 2038431744 | bytes 7962624 | tf_op jit(solution)/shard_map/dot_general | solution.py:34
  179.3 34.3 %all-gather.9.cloned.1.call-done = bf16[768,1152]{1,0:T(8,128)(2,1)} async-done(((bf16[192,1152]{1,0:T(8,128)(2,1)}), bf16[768,1152]{1,0:T(8,128)(2,1)}) %all-gather.9.cloned.1.call-update) | async-done | bytes 1769488 | tf_op jit(solution)/shard_map/all_gather | solution.py:135
  213.7 9.1 %fusion.82 = (bf16[1152]{0:T(1024)(128)(2,1)}, bf16[768,1152]{1,0:T(8,128)(2,1)S(1)}, f32[768,1152]{1,0:T(8,128)}) fusion(f32[768,1152]{1,0:T(8,128)} %fusion.89, f32[1152]{0:T(1024)} %convert_element_type.242, bf16[768,1152]{1,0:T(8,128)(2,1)} %all-gather.9.cloned.1.call-done, bf16[1152,1152]{1,0:T(8,128)(2,1)S(1)} %copy-done), kind=kOutput, calls=%fused_computation.172 | convolution fusion | flops 2057894784 | bytes 13277952 | tf_op jit(solution)/shard_map/dot_general | solution.py:34
  224.0 3.8 convolution_convert_fusion.4
  228.0 7.3 %convolution_convert_fusion.5 = bf16[768,1152]{1,0:T(8,128)(2,1)} fusion(bf16[1152,1152]{1,0:T(8,128)(2,1)} %param.28, f32[768,1152]{1,0:T(8,128)} %get-tuple-element.52), kind=kOutput, calls=%fused_computation.21 | convolution fusion | flops 2047279104 | bytes 7962624 | tf_op jit(solution)/shard_map/dot_general | solution.py:139
  235.5 29.8 %reduce-scatter.12.cloned.1.call-done = bf16[192,1152]{1,0:T(8,128)(2,1)} async-done(((bf16[768,1152]{1,0:T(8,128)(2,1)}), bf16[192,1152]{1,0:T(8,128)(2,1)}) %reduce-scatter.12.cloned.1.call-update) | async-done | bytes 442384 | tf_op jit(solution)/shard_map/reduce_scatter | solution.py:163
  265.3 40.2 %reduce-scatter.10.cloned.1.call-done = bf16[192,1152]{1,0:T(8,128)(2,1)} async-done(((bf16[768,1152]{1,0:T(8,128)(2,1)}), bf16[192,1152]{1,0:T(8,128)(2,1)}) %reduce-scatter.10.cloned.1.call-update) | async-done | bytes 442384 | tf_op jit(solution)/shard_map/reduce_scatter | solution.py:138
  309.3 39.3 %all-gather.13.cloned.1.call-done = bf16[768,1152]{1,0:T(8,128)(2,1)} async-done(((bf16[192,1152]{1,0:T(8,128)(2,1)}), bf16[768,1152]{1,0:T(8,128)(2,1)}) %all-gather.13.cloned.1.call-update) | async-done | bytes 1769488 | tf_op jit(solution)/shard_map/all_gather | solution.py:181
  351.5 2.7 fusion.15
  368.6 3.4 convolution_convert_fusion.7
  372.3 6.2 %convolution_convert_fusion.1 = bf16[1152,1152]{1,0:T(8,128)(2,1)} fusion(bf16[768,1152]{1,0:T(8,128)(2,1)} %copy-done.56, bf16[768,1152]{1,0:T(8,128)(2,1)} %all-gather.9.cloned.1.call-done), kind=kOutput, calls=%fused_computation.6 | convolution fusion | flops 2039758848 | bytes 6193152 | tf_op jit(solution)/shard_map/dot_general | solution.py:40
  378.5 4.3 convolution_convert_fusion
  384.4 3.2 convolution_convert_fusion.3
  388.3 13.7 %all-gather.1 = bf16[4,1,1152]{2,1,0:T(2,128)(2,1)S(1)} all-gather(bf16[1,1,1152]{2,1,0:T(2,128)(2,1)S(1)} %convert_bitcast_fusion), channel_id=1, replica_groups=mesh['dp'=8,'mp'=4] {'mp'}, dimensions={0}, use_global_device_ids=true | all-gather | bytes 11520 | tf_op jit(solution)/shard_map/all_gather | solution.py:241
  402.0 7.8 %reduce-scatter.14.cloned.1.call-done = bf16[192,1152]{1,0:T(8,128)(2,1)} async-done(((bf16[768,1152]{1,0:T(8,128)(2,1)}), bf16[192,1152]{1,0:T(8,128)(2,1)}) %reduce-scatter.14.cloned.1.call-update) | async-done | bytes 442384 | tf_op jit(solution)/shard_map/reduce_scatter | solution.py:214
  412.6 13.6 %all-gather = bf16[4,1,6912]{2,1,0:T(2,128)(2,1)S(1)} all-gather(bf16[1,1,6912]{2,1,0:T(2,128)(2,1)S(1)} %bitcast.84), channel_id=1, replica_groups=mesh['dp'=8,'mp'=4] {'mp'}, dimensions={0}, use_global_device_ids=true | all-gather | bytes 69120 | tf_op jit(solution)/shard_map/all_gather | solution.py:240
  426.9 3.1 convolution_convert_fusion.2
  435.3 4.1 scatter_custom_fusion
  448.4 23.4 %all-reduce.3 = (bf16[1728]{0:T(1024)(128)(2,1)S(1)}, bf16[2,288]{1,0:T(2,128)(2,1)S(1)}, bf16[1152]{0:T(1024)(128)(2,1)S(1)}, bf16[1152]{0:T(1024)(128)(2,1)S(1)}, bf16[1152]{0:T(1024)(128)(2,1)S(1)}) all-reduce(bf16[1728]{0:T(1024)(128)(2,1)S(1)} %reduce_sum.220, ...), channel_id=7, replica_groups=mesh['dp'=8,'mp'=4] {'dp'}, use_global_device_ids=true, to_apply=%region_25.26.clone | all-reduce | flops 5760 | bytes 23040
  474.8 61.6 %all-reduce.7.cloned.1.call-done = (bf16[3,288,1152]{2,1,0:T(8,128)(2,1)}, bf16[288,1152]{1,0:T(8,128)(2,1)}, bf16[1152,1152]{1,0:T(8,128)(2,1)}, bf16[1152,1152]{1,0:T(8,128)(2,1)}) async-done(((bf16[3,288,1152]{2,1,0:T(8,128)(2,1)}, bf16[288,1152]{1,0:T(8,128)(2,1)}, bf16[1152,1152]{1,0:T(8,128)(2,1)}, bf16[1152,1152]{1,0:T(8,128)(2,1)}), (bf16[3,288,1152]{2,1,0:T(8,128)(2,1)}, ...) | async-done | bytes 7962640 | tf_op jit(solution)/shard_map/psum | solution.py:261
  541.9 2.9 convert_element_type.272
  544.8 3.0 convert_element_type.275
  547.8 41.6 %reduce-scatter.16.cloned.1.call-done = bf16[216,1152]{1,0:T(8,128)(2,1)} async-done(((bf16[1728,1152]{1,0:T(8,128)(2,1)}), bf16[216,1152]{1,0:T(8,128)(2,1)}) %reduce-scatter.16.cloned.1.call-update) | async-done | bytes 497680
  (232 shorter events, 87.3 us)
Async XLA Ops:
  7.2 206.5 %copy-start = (bf16[1152,1152]{1,0:T(8,128)(2,1)S(1)}, bf16[1152,1152]{1,0:T(8,128)(2,1)}, u32[]{:S(2)}) copy-start(bf16[1152,1152]{1,0:T(8,128)(2,1)} %param.26) | copy-start | bytes 7962628
  7.2 60.6 %all-gather.7.cloned.1.call-start = ((), (), s32[]{:S(2)}) async-start(), calls=%async_computation.5 | async-start | bytes 2211840 | tf_op jit(solution)/shard_map/all_gather | solution.py:92
  9.3 13.7 %copy-start.29 = (pred[192]{0:T(512)(128)(4,1)}, pred[192]{0:T(512)(128)(4,1)S(1)}, u32[]{:S(2)}) copy-start(pred[192]{0:T(512)(128)(4,1)S(1)} %compare_and_fusion) | copy-start | bytes 580
  9.3 10.5 %copy-start.45 = (s32[1024]{0:T(1024)}, s32[1024]{0:T(1024)S(1)}, u32[]{:S(2)}) copy-start(s32[1024]{0:T(1024)S(1)} %pad_clamp_fusion) | copy-start | bytes 12292
  9.4 9.8 %copy-start.44 = (bf16[6912]{0:T(1024)(128)(2,1)S(1)}, bf16[6912]{0:T(1024)(128)(2,1)}, u32[]{:S(2)}) copy-start(bf16[6912]{0:T(1024)(128)(2,1)} %param.21) | copy-start | bytes 41476
  19.9 21.3 %copy-start.46 = (bf16[2,288]{1,0:T(2,128)(2,1)S(1)}, bf16[2,288]{1,0:T(2,128)(2,1)}, u32[]{:S(2)}) copy-start(bf16[2,288]{1,0:T(2,128)(2,1)} %param.23) | copy-start | bytes 3460
  22.7 45.1 %copy-start.33 = (f32[192]{0:T(256)}, f32[192]{0:T(256)S(1)}, u32[]{:S(2)}) copy-start(f32[192]{0:T(256)S(1)} %broadcast_multiply_fusion.5) | copy-start | bytes 2308
  23.0 44.7 %copy-start.38 = (f32[192]{0:T(256)}, f32[192]{0:T(256)S(1)}, u32[]{:S(2)}) copy-start(f32[192]{0:T(256)S(1)} %add_rsqrt_fusion.1) | copy-start | bytes 2308
  24.6 103.4 %reduce-scatter.8.cloned.1.call-start = ((), (), s32[]{:S(2)}) async-start(), calls=%async_computation.6 | async-start | bytes 2211840 | tf_op jit(solution)/shard_map/reduce_scatter | solution.py:119
  90.6 82.0 %all-gather.11.cloned.1.call-start = ((), (), s32[]{:S(2)}) async-start(), calls=%async_computation.9 | async-start | bytes 2211840 | tf_op jit(solution)/shard_map/all_gather | solution.py:154
  133.2 80.5 %all-gather.9.cloned.1.call-start = ((), (), s32[]{:S(2)}) async-start(), calls=%async_computation.7 | async-start | bytes 2211840 | tf_op jit(solution)/shard_map/all_gather | solution.py:135
  136.5 128.8 %reduce-scatter.12.cloned.1.call-start = ((), (), s32[]{:S(2)}) async-start(), calls=%async_computation.10 | async-start | bytes 2211840 | tf_op jit(solution)/shard_map/reduce_scatter | solution.py:163
  227.8 77.7 %reduce-scatter.10.cloned.1.call-start = ((), (), s32[]{:S(2)}) async-start(), calls=%async_computation.8 | async-start | bytes 2211840 | tf_op jit(solution)/shard_map/reduce_scatter | solution.py:138
  227.9 7.6 %copy-start.47 = (bf16[1152]{0:T(1024)(128)(2,1)S(1)}, bf16[1152]{0:T(1024)(128)(2,1)}, u32[]{:S(2)}) copy-start(bf16[1152]{0:T(1024)(128)(2,1)} %param.29) | copy-start | bytes 6916
  227.9 77.6 %copy-start.5 = (f32[192,1152]{1,0:T(8,128)S(1)}, f32[192,1152]{1,0:T(8,128)}, u32[]{:S(2)}) copy-start(f32[192,1152]{1,0:T(8,128)} %gather_fusion.1) | copy-start | bytes 2654212
  227.9 77.6 %copy-start.27 = (f32[1152]{0:T(1024)S(1)}, f32[1152]{0:T(1024)}, u32[]{:S(2)}) copy-start(f32[1152]{0:T(1024)} %get-tuple-element.22) | copy-start | bytes 13828
  227.9 77.6 %copy-start.30 = (pred[192]{0:T(512)(128)(4,1)S(1)}, pred[192]{0:T(512)(128)(4,1)}, u32[]{:S(2)}) copy-start(pred[192]{0:T(512)(128)(4,1)} %copy-done.29) | copy-start | bytes 580
  227.9 77.6 %copy-start.31 = (f32[192]{0:T(256)S(1)}, f32[192]{0:T(256)}, u32[]{:S(2)}) copy-start(f32[192]{0:T(256)} %compare_convert_fusion) | copy-start | bytes 2308
  227.9 77.6 %copy-start.36 = (f32[192]{0:T(256)S(1)}, f32[192]{0:T(256)}, u32[]{:S(2)}) copy-start(f32[192]{0:T(256)} %copy-done.35) | copy-start | bytes 2308
  228.0 77.6 %copy-start.41 = (f32[192]{0:T(256)S(1)}, f32[192]{0:T(256)}, u32[]{:S(2)}) copy-start(f32[192]{0:T(256)} %copy-done.40) | copy-start | bytes 2308
  235.3 113.3 %all-gather.13.cloned.1.call-start = ((), (), s32[]{:S(2)}) async-start(), calls=%async_computation.11 | async-start | bytes 2211840 | tf_op jit(solution)/shard_map/all_gather | solution.py:181
  265.3 42.3 %copy-start.9 = (bf16[192,1152]{1,0:T(8,128)(2,1)S(1)}, bf16[192,1152]{1,0:T(8,128)(2,1)}, u32[]{:S(2)}) copy-start(bf16[192,1152]{1,0:T(8,128)(2,1)} %reduce-scatter.12.cloned.1.call-done) | copy-start | bytes 1327108
  309.2 42.3 %copy-start.43 = (f32[4,4,192]{2,1,0:T(4,128)S(1)}, f32[4,4,192]{2,1,0:T(4,128)}, u32[]{:S(2)}) copy-start(f32[4,4,192]{2,1,0:T(4,128)} %copy-done.42) | copy-start | bytes 36868
  309.2 100.6 %reduce-scatter.14.cloned.1.call-start = ((), (), s32[]{:S(2)}) async-start(), calls=%async_computation.12 | async-start | bytes 2211840 | tf_op jit(solution)/shard_map/reduce_scatter | solution.py:214
  368.6 15.8 %copy-start.15 = (bf16[768,864]{0,1:T(8,128)(2,1)}, bf16[768,864]{0,1:T(8,128)(2,1)S(1)}, u32[]{:S(2)}) copy-start(bf16[768,864]{0,1:T(8,128)(2,1)S(1)} %constant_dynamic-update-slice_fusion) | copy-start | bytes 3981316
  372.0 164.4 %all-reduce.7.cloned.1.call-start = ((), (), s32[]{:S(2)}) async-start(), calls=%async_computation.14 | async-start | bytes 15925248 | tf_op jit(solution)/shard_map/psum | solution.py:261
  387.6 14.4 %copy-start.10 = (bf16[192,1152]{1,0:T(8,128)(2,1)S(1)}, bf16[192,1152]{1,0:T(8,128)(2,1)}, u32[]{:S(2)}) copy-start(bf16[192,1152]{1,0:T(8,128)(2,1)} %reduce-scatter.12.cloned.1.call-done) | copy-start | bytes 1327108
  387.6 23.4 %copy-start.26 = (f32[1152]{0:T(1024)S(1)}, f32[1152]{0:T(1024)}, u32[]{:S(2)}) copy-start(f32[1152]{0:T(1024)} %copy-done.25) | copy-start | bytes 13828
  387.6 23.4 %copy-start.34 = (f32[192]{0:T(256)S(1)}, f32[192]{0:T(256)}, u32[]{:S(2)}) copy-start(f32[192]{0:T(256)} %copy-done.33) | copy-start | bytes 2308
  387.6 23.4 %copy-start.39 = (f32[192]{0:T(256)S(1)}, f32[192]{0:T(256)}, u32[]{:S(2)}) copy-start(f32[192]{0:T(256)} %copy-done.38) | copy-start | bytes 2308
  387.6 201.8 %reduce-scatter.16.cloned.1.call-start = ((), (), s32[]{:S(2)}) async-start(), calls=%async_computation.13 | async-start | bytes 4478976
  544.8 46.7 %copy-start.1 = (bf16[1152,1152]{1,0:T(8,128)(2,1)S(1)}, bf16[1152,1152]{1,0:T(8,128)(2,1)}, u32[]{:S(2)}) copy-start(bf16[1152,1152]{1,0:T(8,128)(2,1)} %param.26) | copy-start | bytes 7962628
  (35 other events, 119.9 us)
Sparse Core Ops, SparseCore 0:
  24.7 43.0 all-gather.6
  90.7 37.2 reduce-scatter.7
  133.3 39.2 all-gather.10
  174.6 39.0 all-gather.8
  228.0 37.2 reduce-scatter.11
  268.0 37.4 reduce-scatter.9
  309.3 39.2 all-gather.12
  372.1 37.6 reduce-scatter.13
  415.1 121.3 all-reduce.6
  539.7 49.6 reduce-scatter.15
where the time goes:
time: 608 us; the launch traced here: 599 us
  waiting for transfers between devices  346 us (57%)
  matrix products  76.9 us (13%)
  blocking collectives  64.3 us (11%)
  other arithmetic  58.1 us (10%)
  local copies, waits for them, and re-layouts  34.9 us (6%)
  between operations  17.3 us (3%)
    psum x1, waiting for transfers between devices, per_device(): lax.psum(qkv_weight_grad.astype(jnp.bfloat16), 'dp').astype(jnp.float32)  61.6 us
    unnamed x11, waiting for transfers between devices  41.8 us
    reduce_scatter x1, waiting for transfers between devices, per_device(): lax.psum_scatter(jnp.dot(active, down_weight, preferred_element_type=jnp....  40.2 us
    all_gather x1, waiting for transfers between devices, per_device(): proj_grad = lax.all_gather(branch_one_grad, 'mp', axis=0, tiled=True)  39.3 us
    unnamed x2, blocking collectives  37 us
    all_gather x1, waiting for transfers between devices, per_device(): down_grad = lax.all_gather(branch_two_grad, 'mp', axis=0, tiled=True)  34.7 us
    all_gather x1, waiting for transfers between devices, per_device(): group_two = lax.all_gather(mixed_two, 'mp', axis=0, tiled=True)  34.3 us
    dot_general x5, matrix products, right_dot(): lax.dot_general(left, right, (((1,), (1,)), ((), ())), preferred_element_...  32.1 us
  transfers between devices with their start and end apart: 10, of which 10 were waited for; matrix products, arithmetic and copies ran while one was open for 13% of the time, Pallas kernels for 0%

commit v1 on v0

v1 whole, which is shorter than its diff:
```python
import functools
import math

import jax
import jax.numpy as jnp
from jax import lax
from jax.experimental import pallas as pl
from jax.experimental.pallas import tpu as pltpu
from jax.sharding import PartitionSpec as P

HEADS = 16
EPS = 1e-06
F32 = jnp.float32
BF16 = jnp.bfloat16
GELU_A = math.sqrt(2.0 / math.pi)
GELU_B = 0.044715


def norm_rows(rows):
    mean = jnp.mean(rows, axis=-1, keepdims=True)
    centred = rows - mean
    rstd = lax.rsqrt(jnp.mean(centred * centred, axis=-1, keepdims=True) + EPS)
    return centred * rstd, rstd


def norm_back(normed, rstd, grad):
    return rstd * (
        grad
        - jnp.mean(grad, axis=-1, keepdims=True)
        - normed * jnp.mean(grad * normed, axis=-1, keepdims=True)
    )


def mm(left, right, dims=((1,), (0,))):
    return lax.dot_general(left, right, (dims, ((), ())), preferred_element_type=F32)


NT = ((1,), (1,))
TN = ((0,), (0,))


def block(shape):
    rank = len(shape)
    return pl.BlockSpec((1,) + tuple(shape[1:]), lambda i: (i,) + (0,) * (rank - 1))


def whole(shape):
    rank = len(shape)
    return pl.BlockSpec(tuple(shape), lambda i: (0,) * rank)


def call(body, name, grid, ins, outs):
    return pl.pallas_call(
        body,
        grid=(grid,),
        in_specs=[block(a.shape) if step else whole(a.shape) for a, step in ins],
        out_specs=[block(shape) for shape, _ in outs],
        out_shape=[jax.ShapeDtypeStruct(shape, dtype) for shape, dtype in outs],
        name=name,
    )(*[a for a, _ in ins])


def gather_body(picks, tokens, cotangent, routed, grad_two):
    slots, patches = routed.shape[1], tokens.shape[1]
    hot = (lax.broadcasted_iota(jnp.int32, (slots, patches), 1) == picks[0]).astype(F32)
    hot = hot.astype(BF16)
    routed[0] = mm(hot, tokens[0]).astype(BF16)
    grad_two[0] = mm(hot, cotangent[0]).astype(BF16)


def mod_row(mod, index):
    return mod[0][index : index + 1, :]


def live_rows(keep, slots):
    return (lax.broadcasted_iota(jnp.int32, (slots, 1), 0).astype(F32) < keep[0][:, :1]).astype(F32)


def live_keys(keep, slots):
    return lax.broadcasted_iota(jnp.int32, (1, slots), 1).astype(F32) < keep[0][:, :1]


def head_mask(head, head_dim, cols):
    lane = lax.broadcasted_iota(jnp.int32, (1, cols), 1)
    inside = jnp.logical_and(lane >= head * head_dim, lane < (head + 1) * head_dim)
    return inside.astype(F32).astype(BF16)


def softmax_of(query, key, alive, scale):
    scores = mm(query, key, NT) * scale
    scores = jnp.where(alive, scores, -1e30)
    raised = jnp.exp(scores - jnp.max(scores, axis=-1, keepdims=True))
    return raised / jnp.sum(raised, axis=-1, keepdims=True)


def attend_body(head_dim, routed, mod, keep, weight, bias, out_weight, mixed, qkv, attended, branch):
    slots, cols = routed.shape[1], weight.shape[1]
    scale = 1.0 / math.sqrt(head_dim)
    normed, _ = norm_rows(routed[0].astype(F32))
    rows = (normed * (1.0 + mod_row(mod, 1)) + mod_row(mod, 0)).astype(BF16)
    mixed[0] = rows
    query = (mm(rows, weight[0], NT) + bias[0:1, :]).astype(BF16)
    key = mm(rows, weight[1], NT).astype(BF16)
    value = (mm(rows, weight[2], NT) + bias[1:2, :]).astype(BF16)
    qkv[0, 0] = query
    qkv[0, 1] = key
    qkv[0, 2] = value
    alive = live_keys(keep, slots)
    total = jnp.zeros((slots, cols), F32)
    for head in range(cols // head_dim):
        mask = head_mask(head, head_dim, cols)
        low = softmax_of(query * mask, key, alive, scale).astype(BF16)
        total = total + mm(low, value * mask)
    total = total.astype(BF16)
    attended[0] = total
    branch[0] = mm(total, out_weight[...]).astype(BF16)


def attend_back_body(
    head_dim, grad, qkv, routed, keep, weight, out_weight, qkv_grad, mixed_grad, stats, bias_sums
):
    slots, cols = routed.shape[1], weight.shape[1]
    scale = 1.0 / math.sqrt(head_dim)
    rows_grad = grad[0]
    attended_grad = mm(rows_grad, out_weight[...], NT).astype(BF16)
    query, key, value = qkv[0, 0], qkv[0, 1], qkv[0, 2]
    alive = live_keys(keep, slots)
    query_grad = jnp.zeros((slots, cols), F32)
    key_grad = jnp.zeros((slots, cols), F32)
    value_grad = jnp.zeros((slots, cols), F32)
    for head in range(cols // head_dim):
        mask = head_mask(head, head_dim, cols)
        own_query = query * mask
        weights = softmax_of(own_query, key, alive, scale)
        own_grad = attended_grad * mask
        weight_grad = mm(own_grad, value, NT)
        value_grad = value_grad + mm(weights.astype(BF16), own_grad, TN)
        row_total = jnp.sum(weights * weight_grad, axis=-1, keepdims=True)
        score_grad = (weights * (weight_grad - row_total)).astype(BF16)
        query_grad = query_grad + mm(score_grad, key * mask)
        key_grad = key_grad + mm(score_grad, own_query, TN)
    query_grad = (query_grad * scale).astype(BF16)
    key_grad = (key_grad * scale).astype(BF16)
    value_grad = value_grad.astype(BF16)
    qkv_grad[0, 0] = query_grad
    qkv_grad[0, 1] = key_grad
    qkv_grad[0, 2] = value_grad
    rows = mm(query_grad, weight[0]) + mm(key_grad, weight[1]) + mm(value_grad, weight[2])
    mixed_grad[0] = rows.astype(BF16)
    normed, _ = norm_rows(routed[0].astype(F32))
    stats[0, 0:1, :] = jnp.sum(rows, axis=0, keepdims=True)
    stats[0, 1:2, :] = jnp.sum(rows * normed, axis=0, keepdims=True)
    stats[0, 2:3, :] = jnp.sum(rows_grad.astype(F32), axis=0, keepdims=True)
    bias_sums[0, 0:1, :] = jnp.sum(query_grad.astype(F32), axis=0, keepdims=True)
    bias_sums[0, 1:2, :] = jnp.sum(value_grad.astype(F32), axis=0, keepdims=True)


def forward_body(
    mixed, grad_two, mod, keep, up, up_bias, down,
    active, before_grad, down_grad, branch, mixed_grad, up_sum, down_sum,
):
    slots = mixed.shape[1]
    gate = live_rows(keep, slots) * mod_row(mod, 5)
    rows_grad = (gate * grad_two[0].astype(F32)).astype(BF16)
    down_grad[0] = rows_grad
    down_sum[0] = jnp.sum(rows_grad.astype(F32), axis=0, keepdims=True)
    before = mm(mixed[0], up[...], NT) + up_bias[...]
    square = before * before
    tanh = jnp.tanh(GELU_A * (before + GELU_B * (before * square)))
    half = 0.5 * (1.0 + tanh)
    act = (before * half).astype(BF16)
    active[0] = act
    slope = half + 0.5 * before * (1.0 - tanh * tanh) * (GELU_A * (1.0 + 3.0 * GELU_B * square))
    inner = (mm(rows_grad, down[...], NT) * slope).astype(BF16)
    before_grad[0] = inner
    up_sum[0] = jnp.sum(inner.astype(F32), axis=0, keepdims=True)
    mixed_grad[0] = mm(inner, up[...]).astype(BF16)
    branch[0] = mm(act, down[...]).astype(BF16)


def middle_body(branch, out_bias, routed, mod, keep, hidden, mixed):
    slots = routed.shape[1]
    branch_one = branch[0].astype(F32) + out_bias[...]
    rows = routed[0].astype(F32) + live_rows(keep, slots) * mod_row(mod, 2) * branch_one
    hidden[0] = rows
    normed, _ = norm_rows(rows)
    mixed[0] = (normed * (1.0 + mod_row(mod, 4)) + mod_row(mod, 3)).astype(BF16)


def middle_back_body(
    mixed_grad, hidden, branch, out_bias, grad_two, mod, keep, grad_one, branch_grad, stats
):
    slots = hidden.shape[1]
    rows = mixed_grad[0].astype(F32)
    normed, rstd = norm_rows(hidden[0])
    grad = grad_two[0].astype(F32) + norm_back(normed, rstd, rows * (1.0 + mod_row(mod, 4)))
    grad_one[0] = grad
    live = live_rows(keep, slots)
    branch_one = branch[0].astype(F32) + out_bias[...]
    stats[0, 0:1, :] = jnp.sum(live * grad * branch_one, axis=0, keepdims=True)
    stats[0, 1:2, :] = jnp.sum(rows, axis=0, keepdims=True)
    stats[0, 2:3, :] = jnp.sum(rows * normed, axis=0, keepdims=True)
    branch_grad[0] = (live * mod_row(mod, 2) * grad).astype(BF16)


def place(picks, base, rows):
    patches, slots = base.shape[0], rows.shape[0]
    hot = (lax.broadcasted_iota(jnp.int32, (patches, slots), 0) == picks).astype(F32)
    taken = jnp.max(hot, axis=1, keepdims=True) > 0
    return jnp.where(taken, mm(hot.astype(BF16), rows.astype(BF16)), base.astype(F32)).astype(BF16)


def out_body(branch, hidden, down_bias, mod, keep, grad_two, picks, tokens, layer_out, gate_grad):
    slots = hidden.shape[1]
    live = live_rows(keep, slots)
    branch_two = branch[0].astype(F32) + down_bias[...]
    gate_grad[0] = jnp.sum(live * grad_two[0].astype(F32) * branch_two, axis=0, keepdims=True)
    rows = hidden[0] + live * mod_row(mod, 5) * branch_two
    layer_out[0] = place(picks[0], tokens[0], rows)


def first_back_body(mixed_grad, routed, mod, grad_one, picks, cotangent, tokens_grad):
    normed, rstd = norm_rows(routed[0].astype(F32))
    rows = mixed_grad[0].astype(F32) * (1.0 + mod_row(mod, 1))
    tokens_grad[0] = place(picks[0], cotangent[0], grad_one[0] + norm_back(normed, rstd, rows))


def dp_bits():
    count = lax.axis_size("dp").bit_length() - 1
    return list(range(count))


def partner(bit):
    return [(i, i ^ (1 << bit)) for i in range(lax.axis_size("dp"))]


def scatter_sum(part, bits):
    index = lax.axis_index("dp")
    for bit in bits:
        side = (index >> bit) & 1
        halves = part.reshape(2, part.shape[0] // 2, part.shape[1])
        own = lax.dynamic_index_in_dim(halves, side, 0, keepdims=False)
        other = lax.dynamic_index_in_dim(halves, 1 - side, 0, keepdims=False)
        got = lax.ppermute(other, "dp", partner(bit))
        part = (own.astype(F32) + got.astype(F32)).astype(BF16)
    return part


def gather_rows(part, bits):
    index = lax.axis_index("dp")
    for bit in reversed(bits):
        side = (index >> bit) & 1
        got = lax.ppermute(part, "dp", partner(bit))
        part = jnp.where(
            side == 0, jnp.concatenate([part, got], 0), jnp.concatenate([got, part], 0)
        )
    return part


def shift(value, step):
    count = lax.axis_size("mp")
    return lax.ppermute(value, "mp", [(i, (i + step) % count) for i in range(count)])


def small_gather(value):
    count, here = lax.axis_size("mp"), lax.axis_index("mp")
    rows = jnp.stack([value] + [shift(value, step) for step in range(1, count)])
    return jnp.take(rows, (here - jnp.arange(count)) % count, axis=0)


def small_scatter_sum(parts):
    count, here = lax.axis_size("mp"), lax.axis_index("mp")
    total = lax.dynamic_index_in_dim(parts, here, 0, keepdims=False)
    for step in range(1, count):
        to = (here + step) % count
        total = total + shift(lax.dynamic_index_in_dim(parts, to, 0, keepdims=False), step)
    return total


def sum_pair(first, second):
    bits = dp_bits()
    turned = bits[:1] + bits[2:] + bits[1:2]
    first = scatter_sum(first, bits)
    second = scatter_sum(second, turned)
    return gather_rows(first, bits), gather_rows(second, turned)


def per_device(
    tokens, conditioning, routes, keep_count, cotangent, ada_weight, ada_bias, qkv_weight,
    qv_bias, out_weight, out_bias, up_weight, up_bias, down_weight, down_bias,
):
    images = conditioning.shape[0]
    width = tokens.shape[1]
    patches = routes.shape[1]
    slots = 3 * patches // 4
    cols = qkv_weight.shape[1]
    head_dim = width // HEADS
    hidden_units = up_weight.shape[0]
    members = lax.axis_size("mp")
    groups = lax.axis_size("dp")
    group = members * images
    here = lax.axis_index("mp")

    image_tokens = tokens.reshape(images, patches, width)
    image_cot = cotangent.reshape(images, patches, width)
    picks = routes[:, :slots]
    picks_col = picks.reshape(images, slots, 1)
    picks_row = picks.reshape(images, 1, slots)
    rows_shape = (images, slots, width)
    group_shape = (group, slots, width)

    routed, grad_two = call(
        gather_body, "gather", images,
        [(picks_col, True), (image_tokens, True), (image_cot, True)],
        [(rows_shape, BF16), (rows_shape, BF16)],
    )
    group_routed = lax.all_gather(routed, "mp", axis=0, tiled=True)
    group_two = lax.all_gather(grad_two, "mp", axis=0, tiled=True)

    small = jnp.concatenate(
        [conditioning, jnp.broadcast_to(keep_count.astype(BF16)[:, None], (images, 128))], axis=1
    )
    small = small_gather(small).reshape(group, width + 128)
    silu_cond = jax.nn.silu(small[:, :width].astype(F32)).astype(BF16)
    modulation = mm(silu_cond, ada_weight, NT) + ada_bias.astype(F32)
    modulation = modulation.reshape(group, 6, width)
    keep = small[:, None, width:].astype(F32)
    own_mod = lax.dynamic_slice_in_dim(modulation, here * images, images, 0)
    own_keep = jnp.broadcast_to(keep_count.astype(F32)[:, None, None], (images, 1, 128))
    out_bias_row = out_bias.astype(F32)[None]
    down_bias_row = down_bias.astype(F32)[None]

    mixed_one, qkv, attended, branch = call(
        functools.partial(attend_body, head_dim), "attend", group,
        [
            (group_routed, True), (modulation, True), (keep, True), (qkv_weight, False),
            (qv_bias.astype(F32), False), (out_weight, False),
        ],
        [
            (group_shape, BF16), ((group, 3, slots, cols), BF16), ((group, slots, cols), BF16),
            (group_shape, BF16),
        ],
    )
    branch_one = lax.psum_scatter(branch, "mp", scatter_dimension=0, tiled=True)
    hidden_one, mixed_two = call(
        middle_body, "middle", images,
        [
            (branch_one, True), (out_bias_row, False), (routed, True), (own_mod, True),
            (own_keep, True),
        ],
        [(rows_shape, F32), (rows_shape, BF16)],
    )
    group_mixed = lax.all_gather(mixed_two, "mp", axis=0, tiled=True)
    unit_shape = (group, slots, hidden_units)
    active, before_grad, down_grad, branch, mixed_grad, up_sum, down_sum = call(
        forward_body, "forward", group,
        [
            (group_mixed, True), (group_two, True), (modulation, True), (keep, True),
            (up_weight, False), (up_bias.astype(F32)[None], False), (down_weight, False),
        ],
        [
            (unit_shape, BF16), (unit_shape, BF16), (group_shape, BF16), (group_shape, BF16),
            (group_shape, BF16), ((group, 1, hidden_units), F32), ((group, 1, width), F32),
        ],
    )
    mixed_two_grad = lax.psum_scatter(mixed_grad, "mp", scatter_dimension=0, tiled=True)
    branch_two = lax.psum_scatter(branch, "mp", scatter_dimension=0, tiled=True)

    flat = (group * slots, hidden_units)
    wide = (group * slots, width)
    up_part = mm(before_grad.reshape(flat), group_mixed.reshape(wide), TN).astype(BF16)
    down_part = mm(active.reshape(flat), down_grad.reshape(wide), TN).astype(BF16)
    up_weight_grad, down_weight_grad = sum_pair(up_part, down_part)

    grad_one, branch_grad, middle_stats = call(
        middle_back_body, "middle_back", images,
        [
            (mixed_two_grad, True), (hidden_one, True), (branch_one, True), (out_bias_row, False),
            (grad_two, True), (own_mod, True), (own_keep, True),
        ],
        [(rows_shape, F32), (rows_shape, BF16), ((images, 3, width), F32)],
    )
    group_grad = lax.all_gather(branch_grad, "mp", axis=0, tiled=True)
    layer_out, gate_grad = call(
        out_body, "out", images,
        [
            (branch_two, True), (hidden_one, True), (down_bias_row, False), (own_mod, True),
            (own_keep, True), (grad_two, True), (picks_row, True), (image_tokens, True),
        ],
        [((images, patches, width), BF16), ((images, 1, width), F32)],
    )
    qkv_grad, mixed_grad, attend_stats, bias_sums = call(
        functools.partial(attend_back_body, head_dim), "attend_back", group,
        [
            (group_grad, True), (qkv, True), (group_routed, True), (keep, True),
            (qkv_weight, False), (out_weight, False),
        ],
        [
            ((group, 3, slots, cols), BF16), (group_shape, BF16), ((group, 3, width), F32),
            ((group, 2, cols), F32),
        ],
    )
    mixed_one_grad = lax.psum_scatter(mixed_grad, "mp", scatter_dimension=0, tiled=True)

    qkv_part = jnp.einsum(
        "gtsc,gsd->tcd", qkv_grad, mixed_one, preferred_element_type=F32
    ).reshape(3 * cols, width)
    out_part = mm(attended.reshape(-1, cols), group_grad.reshape(wide), TN)
    part = jnp.concatenate([qkv_part.astype(BF16), out_part.astype(BF16)], axis=0)
    part = jnp.concatenate(sum_pair(part[: 2 * cols], part[2 * cols :]), axis=0)
    qkv_weight_grad = part[: 3 * cols].reshape(3, cols, width)
    out_weight_grad = part[3 * cols :]

    own_rows = jnp.concatenate([middle_stats, gate_grad], axis=1)
    placed = lax.dynamic_update_slice(
        jnp.zeros((group, 4, width), F32), own_rows, (here * images, 0, 0)
    )
    mod_grad = jnp.concatenate([attend_stats[:, :2], placed], axis=1)
    each = 6 * width // (groups * members)
    mod_grad = mod_grad.reshape(group, groups, members, each)
    mod_grad = small_scatter_sum(mod_grad.transpose(2, 0, 1, 3)).astype(BF16)
    pieces = [
        mod_grad.reshape(-1),
        silu_cond.reshape(-1),
        jnp.sum(bias_sums, axis=0).astype(BF16).reshape(-1),
        jnp.sum(attend_stats[:, 2], axis=0).astype(BF16),
        jnp.sum(up_sum, axis=0).astype(BF16).reshape(-1),
        jnp.sum(down_sum, axis=0).astype(BF16).reshape(-1),
    ]
    sizes = [piece.shape[0] for piece in pieces]
    packed = jnp.concatenate(pieces)
    packed = jnp.pad(packed, (0, -packed.shape[0] % 2048)).reshape(-1, 128)
    packed = lax.all_gather(packed, "dp", axis=0, tiled=False).reshape(groups, -1)
    starts = [sum(sizes[:i]) for i in range(len(sizes))]
    views = [packed[:, s : s + n] for s, n in zip(starts, sizes)]
    mod_all = views[0].reshape(groups, group, groups, each)
    mod_all = lax.dynamic_index_in_dim(mod_all, lax.axis_index("dp"), 2, keepdims=False)
    mod_all = mod_all.reshape(groups * group, each)
    cond_all = views[1].reshape(groups * group, width)
    ada_weight_grad = mm(mod_all, cond_all, TN)
    ada_bias_grad = jnp.sum(mod_all.astype(F32), axis=0)
    qv_sum, out_sum, up_bias_grad, down_bias_grad = [
        jnp.sum(view.astype(F32), axis=0) for view in views[2:]
    ]

    tokens_grad = call(
        first_back_body, "first_back", images,
        [
            (mixed_one_grad, True), (routed, True), (own_mod, True), (grad_one, True),
            (picks_row, True), (image_cot, True),
        ],
        [((images, patches, width), BF16)],
    )[0]
    return (
        layer_out.reshape(images * patches, width),
        tokens_grad.reshape(images * patches, width),
        ada_weight_grad,
        ada_bias_grad,
        qkv_weight_grad.astype(F32),
        qv_sum.reshape(2, cols),
        out_weight_grad.astype(F32),
        out_sum,
        up_weight_grad.astype(F32),
        up_bias_grad,
        down_weight_grad.astype(F32),
        down_bias_grad,
    )


def solution(mesh):
    both = ("dp", "mp")
    in_specs = (
        P(both, None), P(both, None), P(both, None), P(both), P(both, None), P(), P(),
        P(None, "mp", None), P(None, "mp"), P("mp", None), P(), P("mp", None), P("mp"),
        P("mp", None), P(),
    )
    out_specs = (
        P(both, None), P(both, None), P(both, None), P(both), P(None, "mp", None), P(None, "mp"),
        P("mp", None), P(), P("mp", None), P("mp"), P("mp", None), P(),
    )
    return jax.shard_map(
        per_device, mesh=mesh, in_specs=in_specs, out_specs=out_specs, check_vma=False
    )
```

time: 608 us -> 437 us (0.72); the launches traced: 599 us -> 436 us
  waiting for transfers between devices: 346 us -> 239 us
  Pallas kernels: 0 us -> 62.4 us
  matrix products: 76.9 us -> 21.8 us
  blocking collectives: 64.3 us -> 10.5 us
  starting transfers between devices: 1.26 us -> 31.5 us
  other arithmetic: 58.1 us -> 33.1 us
  local copies, waits for them, and re-layouts: 34.9 us -> 21.7 us
    ppermute x0 -> x30, waiting for transfers between devices: none -> 92.7 us  [the longest x12 47.9 us: scatter_sum(): got = lax.ppermute(other, 'dp', partner(bit))]
    reduce_scatter x4, waiting for transfers between devices: 108 us -> 34.7 us  [the longest x1 34.6 us: per_device(): branch_one = lax.psum_scatter(branch, 'mp', scatter_dimension=0, tiled=True)]
    pallas_call x0 -> x8, Pallas kernels: none -> 62.4 us  [call(): pl.pallas_call(body, grid=(grid,), in_specs=[block(a.shape) if step else...]
    psum x1 -> x0, waiting for transfers between devices: 61.6 us -> none  [per_device(): lax.psum(qkv_weight_grad.astype(jnp.bfloat16), 'dp').astype(jnp.float32)]
    dot_general x20 -> x6, matrix products: 76.9 us -> 21.8 us  [the longest x5 18.4 us: mm(): lax.dot_general(left, right, (dims, ((), ())), preferred_element_type=F32)]
    unnamed x11 -> x8, waiting for transfers between devices: 41.8 us -> 0.8 us
    unnamed x2 -> x0, blocking collectives: 37 us -> none
    ppermute x0 -> x30, starting transfers between devices: none -> 30.8 us  [the longest x12 11.2 us: gather_rows(): got = lax.ppermute(part, 'dp', partner(bit))]
  transfers between devices with their start and end apart: 10 -> 38, of which waited for: 10 -> 22; matrix products, arithmetic and copies ran while one was open for 13% -> 15% of each run, Pallas kernels for 0% -> 2%
where the time goes in v1:
time: 437 us; the launch traced here: 436 us
  waiting for transfers between devices  239 us (55%)
  Pallas kernels  62.4 us (14%)
  other arithmetic  33.1 us (8%)
  starting transfers between devices  31.5 us (7%)
  matrix products  21.8 us (5%)
  local copies, waits for them, and re-layouts  21.7 us (5%)
  between operations  15.5 us (4%)
  blocking collectives  10.5 us (2%)
    pallas_call x8, Pallas kernels, call(): pl.pallas_call(body, grid=(grid,), in_specs=[block(a.shape) if step else...  62.4 us
    ppermute x12, waiting for transfers between devices, scatter_sum(): got = lax.ppermute(other, 'dp', partner(bit))  47.9 us
    all_gather x1, waiting for transfers between devices, per_device(): group_mixed = lax.all_gather(mixed_two, 'mp', axis=0, tiled=True)  41.1 us
    all_gather x1, waiting for transfers between devices, per_device(): group_two = lax.all_gather(grad_two, 'mp', axis=0, tiled=True)  37.7 us
    ppermute x12, waiting for transfers between devices, gather_rows(): got = lax.ppermute(part, 'dp', partner(bit))  36.8 us
    reduce_scatter x1, waiting for transfers between devices, per_device(): branch_one = lax.psum_scatter(branch, 'mp', scatter_dimension=0, tiled=True)  34.6 us
    all_gather x1, waiting for transfers between devices, per_device(): group_routed = lax.all_gather(routed, 'mp', axis=0, tiled=True)  20.2 us
    dot_general x5, matrix products, mm(): lax.dot_general(left, right, (dims, ((), ())), preferred_element_type=F32)  18.4 us
  transfers between devices with their start and end apart: 38, of which 22 were waited for; matrix products, arithmetic and copies ran while one was open for 15% of the time, Pallas kernels for 2%

profile of v1, /device:TPU:0, one launch (start us, length us, event | category | flops | bytes accessed | tf_op | source)
XLA Modules:
  0.0 436.0 jit_solution(3069085764496466711)
XLA Ops:
  9.3 2.5 gather.12
  12.6 5.1 %collective-permute-start.2 = (bf16[1,1280]{1,0:T(2,128)(2,1)S(1)}, bf16[1,1280]{1,0:T(2,128)(2,1)S(1)}, u32[]{:S(2)}, u32[]{:S(2)}) collective-permute-start(bf16[1,1280]{1,0:T(2,128)(2,1)S(1)} %get-tuple-element.68), channel_id=1, source_target_pairs={{0,3},{1,0},{2,1},{3,2},{4,7},{5,4},{6,5},{7,6},{8,11},{9,8},{10,9... | collective-permute-start | bytes 7688 | tf_op jit(solution)/shard_map/ppermute | solution.py:262
  19.4 2.8 collective-permute-done.1
  23.8 9.7 %convolution_add_fusion = f32[4,6912]{1,0:T(4,128)S(1)} fusion(bf16[6912,1152]{1,0:T(8,128)(2,1)} %param.20, f32[6912]{0:T(1024)S(1)} %convert_element_type.246, bf16[4,1280]{1,0:T(4,128)(2,1)S(1)} %broadcast_select_fusion), kind=kOutput, calls=%fused_computation.3 | convolution fusion | flops 63756288 | bytes 16073728 | tf_op jit(solution)/shard_map/dot_general | solution.py:35
  34.9 20.2 %all-gather.5.cloned.1.call-done.routed = bf16[4,192,1152]{2,1,0:T(8,128)(2,1)} async-done(((bf16[1,192,1152]{2,1,0:T(8,128)(2,1)}), bf16[4,192,1152]{2,1,0:T(8,128)(2,1)}) %all-gather.5.cloned.1.call-update) | async-done | bytes 1769488 | tf_op jit(solution)/shard_map/all_gather | solution.py:317
  55.1 12.8 %attend.1 = (bf16[4,192,1152]{2,1,0:T(8,128)(2,1)}, bf16[4,3,192,288]{3,2,1,0:T(8,128)(2,1)}, bf16[4,192,288]{2,1,0:T(8,128)(2,1)}, bf16[4,192,1152]{2,1,0:T(8,128)(2,1)}) custom-call(bf16[4,192,1152]{2,1,0:T(8,128)(2,1)} %all-gather.5.cloned.1.call-done.routed, f32[4,6,1152]{2,1,0:T(8,128)} %reshape.240.mod, f32[4,1,128]{2,1,0:T(1,128)} %bitcast.180, ...), custom_call_target="tpu_custom_call" | custom-call | tf_op jit(solution)/shard_map/attend/pallas_call | solution.py:53
  70.7 34.6 %reduce-scatter.5.cloned.1.call-done.branch = bf16[1,192,1152]{2,1,0:T(8,128)(2,1)} async-done(((bf16[4,192,1152]{2,1,0:T(8,128)(2,1)}), bf16[1,192,1152]{2,1,0:T(8,128)(2,1)}) %reduce-scatter.5.cloned.1.call-update) | async-done | bytes 442384 | tf_op jit(solution)/shard_map/reduce_scatter | solution.py:344
  109.0 37.7 %all-gather.9.cloned.1.call-done.grad_two = bf16[4,192,1152]{2,1,0:T(8,128)(2,1)} async-done(((bf16[1,192,1152]{2,1,0:T(8,128)(2,1)}), bf16[4,192,1152]{2,1,0:T(8,128)(2,1)}) %all-gather.9.cloned.1.call-update) | async-done | bytes 1769488 | tf_op jit(solution)/shard_map/all_gather | solution.py:318
  146.7 41.1 %all-gather.7.cloned.1.call-done.mixed = bf16[4,192,1152]{2,1,0:T(8,128)(2,1)} async-done(((bf16[1,192,1152]{2,1,0:T(8,128)(2,1)}), bf16[4,192,1152]{2,1,0:T(8,128)(2,1)}) %all-gather.7.cloned.1.call-update) | async-done | bytes 1769488 | tf_op jit(solution)/shard_map/all_gather | solution.py:353
  187.9 16.8 %forward.1 = (bf16[4,192,1152]{2,1,0:T(8,128)(2,1)}, bf16[4,192,1152]{2,1,0:T(8,128)(2,1)}, bf16[4,192,1152]{2,1,0:T(8,128)(2,1)}, bf16[4,192,1152]{2,1,0:T(8,12...) custom-call(bf16[4,192,1152]{2,1,0:T(8,128)(2,1)} %all-gather.7.cloned.1.call-done.mixed, ...), custom_call_target="tpu_custom_call" | custom-call | tf_op jit(solution)/shard_map/forward/pallas_call | solution.py:53
  206.1 4.1 fusion
  222.8 13.8 %collective-permute-done.19 = bf16[288,1152]{1,0:T(8,128)(2,1)} collective-permute-done((bf16[288,1152]{1,0:T(8,128)(2,1)S(1)}, bf16[288,1152]{1,0:T(8,128)(2,1)}, u32[]{:S(2)}, u32[]{:S(2)}) %collective-permute-start.19) | collective-permute-done | bytes 663584 | tf_op jit(solution)/shard_map/ppermute | solution.py:244
  240.1 8.5 %collective-permute-done.20 = bf16[144,1152]{1,0:T(8,128)(2,1)S(1)} collective-permute-done((bf16[144,1152]{1,0:T(8,128)(2,1)S(1)}, bf16[144,1152]{1,0:T(8,128)(2,1)S(1)}, u32[]{:S(2)}, u32[]{:S(2)}) %collective-permute-start.20) | collective-permute-done | bytes 331808 | tf_op jit(solution)/shard_map/ppermute | solution.py:244
  250.2 12.7 %collective-permute-done.25 = bf16[288,1152]{1,0:T(8,128)(2,1)} collective-permute-done((bf16[288,1152]{1,0:T(8,128)(2,1)S(1)}, bf16[288,1152]{1,0:T(8,128)(2,1)}, u32[]{:S(2)}, u32[]{:S(2)}) %collective-permute-start.25) | collective-permute-done | bytes 663584 | tf_op jit(solution)/shard_map/ppermute | solution.py:244
  265.8 2.8 collective-permute-done.21
  274.3 18.5 %collective-permute-done.27 = bf16[144,1152]{1,0:T(8,128)(2,1)S(1)} collective-permute-done((bf16[144,1152]{1,0:T(8,128)(2,1)S(1)}, bf16[144,1152]{1,0:T(8,128)(2,1)S(1)}, u32[]{:S(2)}, u32[]{:S(2)}) %collective-permute-start.27) | collective-permute-done | bytes 331808 | tf_op jit(solution)/shard_map/ppermute | solution.py:253
  295.8 3.5 middle_back.1
  299.5 9.4 %collective-permute-done.28 = bf16[288,1152]{1,0:T(8,128)(2,1)} collective-permute-done((bf16[288,1152]{1,0:T(8,128)(2,1)S(1)}, bf16[288,1152]{1,0:T(8,128)(2,1)}, u32[]{:S(2)}, u32[]{:S(2)}) %collective-permute-start.28) | collective-permute-done | bytes 663584 | tf_op jit(solution)/shard_map/ppermute | solution.py:253
  312.6 3.1 out.1
  316.4 4.6 %fusion.2 = f32[1152,1152]{1,0:T(8,128)} fusion(bf16[576,1152]{1,0:T(8,128)(2,1)} %collective-permute-done.23, bf16[576,1152]{1,0:T(8,128)(2,1)S(1)} %maximum_select_fusion.4, pred[]{:T(512)S(6)} %eq.11), kind=kLoop, calls=%fused_computation.9 | loop fusion | flops 13271040 | bytes 7962625 | tf_op jit(solution)/shard_map/convert_element_type | solution.py:463
  321.0 4.6 %fusion.3 = f32[1152,1152]{1,0:T(8,128)} fusion(bf16[576,1152]{1,0:T(8,128)(2,1)} %collective-permute-done.29, bf16[576,1152]{1,0:T(8,128)(2,1)S(1)} %maximum_select_fusion.5, pred[]{:T(512)S(6)} %eq.11), kind=kLoop, calls=%fused_computation.11 | loop fusion | flops 13271040 | bytes 7962625 | tf_op jit(solution)/shard_map/convert_element_type | solution.py:465
  325.7 12.1 %all-gather.11.cloned.1.call-done.grad = bf16[4,192,1152]{2,1,0:T(8,128)(2,1)} async-done(((bf16[1,192,1152]{2,1,0:T(8,128)(2,1)}), bf16[4,192,1152]{2,1,0:T(8,128)(2,1)}) %all-gather.11.cloned.1.call-update) | async-done | bytes 1769488 | tf_op jit(solution)/shard_map/all_gather | solution.py:383
  337.8 17.8 %attend_back.1 = (bf16[4,3,192,288]{3,2,1,0:T(8,128)(2,1)}, bf16[4,192,1152]{2,1,0:T(8,128)(2,1)}, f32[4,3,1152]{2,1,0:T(4,128)}, f32[4,2,288]{2,1,0:T(2,128)}) custom-call(bf16[4,192,1152]{2,1,0:T(8,128)(2,1)} %all-gather.11.cloned.1.call-done.grad, bf16[4,3,192,288]{3,2,1,0:T(8,128)(2,1)} %get-tuple-element.45.qkv, ...), custom_call_target="tpu_custom_call" | custom-call | tf_op jit(solution)/shard_map/attend_back/pallas_call | solution.py:53
  357.2 3.4 bitcast_convert_fusion
  369.3 4.1 collective-permute-done.4
  374.3 2.9 concatenate.93
  382.8 5.4 %collective-permute-done.13 = bf16[144,1152]{1,0:T(8,128)(2,1)S(1)} collective-permute-done((bf16[144,1152]{1,0:T(8,128)(2,1)S(1)}, bf16[144,1152]{1,0:T(8,128)(2,1)S(1)}, u32[]{:S(2)}, u32[]{:S(2)}) %collective-permute-start.13) | collective-permute-done | bytes 331808 | tf_op jit(solution)/shard_map/ppermute | solution.py:244
  391.5 2.8 collective-permute-done.14
  397.0 2.8 collective-permute-done.15
  400.9 3.2 collective-permute-done.9
  405.7 10.5 %all_gather.19 = bf16[8,128,128]{2,1,0:T(8,128)(2,1)S(1)} all-gather(bf16[1,128,128]{2,1,0:T(8,128)(2,1)S(1)} %pad_bitcast_fusion), channel_id=1, replica_groups=mesh['dp'=8,'mp'=4] {'dp'}, dimensions={0}, use_global_device_ids=true | all-gather | bytes 294912 | tf_op jit(solution)/shard_map/all_gather | solution.py:433
  425.8 3.3 first_back.1
  (193 shorter events, 82.9 us)
Async XLA Ops:
  7.2 47.9 %all-gather.5.cloned.1.call-start = ((), (), s32[]{:S(2)}) async-start(), calls=%async_computation.4 | async-start | bytes 2211840 | tf_op jit(solution)/shard_map/all_gather | solution.py:317
  11.9 93.5 %reduce-scatter.5.cloned.1.call-start = ((), (), s32[]{:S(2)}) async-start(), calls=%async_computation.5 | async-start | bytes 2211840 | tf_op jit(solution)/shard_map/reduce_scatter | solution.py:344
  12.6 6.8 %collective-permute-start.2 = (bf16[1,1280]{1,0:T(2,128)(2,1)S(1)}, bf16[1,1280]{1,0:T(2,128)(2,1)S(1)}, u32[]{:S(2)}, u32[]{:S(2)}) collective-permute-start(bf16[1,1280]{1,0:T(2,128)(2,1)S(1)} %get-tuple-element.68), channel_id=1, source_target_pairs={{0,3},{1,0},{2,1},{3,2},{4,7},{5,4},{6,5},{7,6},{8,11},{9,8},{10,9... | collective-permute-start | bytes 7688 | tf_op jit(solution)/shard_map/ppermute | solution.py:262
  17.7 5.4 %collective-permute-start = (bf16[1,1280]{1,0:T(2,128)(2,1)S(1)}, bf16[1,1280]{1,0:T(2,128)(2,1)S(1)}, u32[]{:S(2)}, u32[]{:S(2)}) collective-permute-start(bf16[1,1280]{1,0:T(2,128)(2,1)S(1)} %get-tuple-element.68), channel_id=1, source_target_pairs={{0,1},{1,2},{2,3},{3,0},{4,5},{5,6},{6,7},{7,4},{8,9},{9,10},{10,1... | collective-permute-start | bytes 7688 | tf_op jit(solution)/shard_map/ppermute | solution.py:262
  67.9 78.8 %all-gather.9.cloned.1.call-start = ((), (), s32[]{:S(2)}) async-start(), calls=%async_computation.7 | async-start | bytes 2211840 | tf_op jit(solution)/shard_map/all_gather | solution.py:318
  68.7 119.2 %all-gather.7.cloned.1.call-start = ((), (), s32[]{:S(2)}) async-start(), calls=%async_computation.6 | async-start | bytes 2211840 | tf_op jit(solution)/shard_map/all_gather | solution.py:353
  108.4 187.4 %reduce-scatter.9.cloned.1.call-start = ((), (), s32[]{:S(2)}) async-start(), calls=%async_computation.9 | async-start | bytes 2211840 | tf_op jit(solution)/shard_map/reduce_scatter | solution.py:366
  204.7 107.9 %reduce-scatter.7.cloned.1.call-start = ((), (), s32[]{:S(2)}) async-start(), calls=%async_computation.8 | async-start | bytes 2211840 | tf_op jit(solution)/shard_map/reduce_scatter | solution.py:367
  210.4 6.5 %collective-permute-start.18 = (bf16[576,1152]{1,0:T(8,128)(2,1)S(1)}, bf16[576,1152]{1,0:T(8,128)(2,1)}, u32[]{:S(2)}, u32[]{:S(2)}) collective-permute-start(bf16[576,1152]{1,0:T(8,128)(2,1)S(1)} %dynamic-slice_bitcast_fusion.1), channel_id=1, source_target_pairs={{0,4},{4,0},{8,12},{12,8},{16,20},{20,16},{24,28},{28,24},{1,5},{5... | collective-permute-start | bytes 3981320 | tf_op jit(solution)/shard_map/ppermute | solution.py:244
  219.1 17.5 %collective-permute-start.19 = (bf16[288,1152]{1,0:T(8,128)(2,1)S(1)}, bf16[288,1152]{1,0:T(8,128)(2,1)}, u32[]{:S(2)}, u32[]{:S(2)}) collective-permute-start(bf16[288,1152]{1,0:T(8,128)(2,1)S(1)} %dynamic-slice_bitcast_fusion.3), channel_id=1, source_target_pairs={{0,8},{4,12},{8,0},{12,4},{16,24},{20,28},{24,16},{28,20},{1,9},{5... | collective-permute-start | bytes 1990664 | tf_op jit(solution)/shard_map/ppermute | solution.py:244
  220.6 117.2 %all-gather.11.cloned.1.call-start = ((), (), s32[]{:S(2)}) async-start(), calls=%async_computation.10 | async-start | bytes 2211840 | tf_op jit(solution)/shard_map/all_gather | solution.py:383
  237.9 10.7 %collective-permute-start.20 = (bf16[144,1152]{1,0:T(8,128)(2,1)S(1)}, bf16[144,1152]{1,0:T(8,128)(2,1)S(1)}, u32[]{:S(2)}, u32[]{:S(2)}) collective-permute-start(bf16[144,1152]{1,0:T(8,128)(2,1)S(1)} %dynamic-slice_bitcast_fusion.7), channel_id=1, source_target_pairs={{0,16},{4,20},{8,24},{12,28},{16,0},{20,4},{24,8},{28,12},{1,17},{... | collective-permute-start | bytes 995336 | tf_op jit(solution)/shard_map/ppermute | solution.py:244
  239.5 23.5 %collective-permute-start.25 = (bf16[288,1152]{1,0:T(8,128)(2,1)S(1)}, bf16[288,1152]{1,0:T(8,128)(2,1)}, u32[]{:S(2)}, u32[]{:S(2)}) collective-permute-start(bf16[288,1152]{1,0:T(8,128)(2,1)S(1)} %dynamic-slice_bitcast_fusion.2), channel_id=1, source_target_pairs={{0,16},{4,20},{8,24},{12,28},{16,0},{20,4},{24,8},{28,12},{1,17},{... | collective-permute-start | bytes 1990664 | tf_op jit(solution)/shard_map/ppermute | solution.py:244
  248.7 19.9 %collective-permute-start.21 = (bf16[144,1152]{1,0:T(8,128)(2,1)S(1)}, bf16[144,1152]{1,0:T(8,128)(2,1)S(1)}, u32[]{:S(2)}, u32[]{:S(2)}) collective-permute-start(bf16[144,1152]{1,0:T(8,128)(2,1)S(1)} %fusion.13), channel_id=1, source_target_pairs={{0,16},{4,20},{8,24},{12,28},{16,0},{20,4},{24,8},{28,12},{1,17},{... | collective-permute-start | bytes 995336 | tf_op jit(solution)/shard_map/ppermute | solution.py:253
  264.2 8.4 %collective-permute-start.26 = (bf16[144,1152]{1,0:T(8,128)(2,1)S(1)}, bf16[144,1152]{1,0:T(8,128)(2,1)S(1)}, u32[]{:S(2)}, u32[]{:S(2)}) collective-permute-start(bf16[144,1152]{1,0:T(8,128)(2,1)S(1)} %dynamic-slice_bitcast_fusion.6), channel_id=1, source_target_pairs={{0,8},{4,12},{8,0},{12,4},{16,24},{20,28},{24,16},{28,20},{1,9},{5... | collective-permute-start | bytes 995336 | tf_op jit(solution)/shard_map/ppermute | solution.py:244
  268.8 25.8 %collective-permute-start.22 = (bf16[288,1152]{1,0:T(8,128)(2,1)S(1)}, bf16[288,1152]{1,0:T(8,128)(2,1)S(1)}, u32[]{:S(2)}, u32[]{:S(2)}) collective-permute-start(bf16[288,1152]{1,0:T(8,128)(2,1)S(1)} %maximum_select_fusion.8), channel_id=1, source_target_pairs={{0,8},{4,12},{8,0},{12,4},{16,24},{20,28},{24,16},{28,20},{1,9},{5... | collective-permute-start | bytes 1990664 | tf_op jit(solution)/shard_map/ppermute | solution.py:253
  272.7 20.1 %collective-permute-start.27 = (bf16[144,1152]{1,0:T(8,128)(2,1)S(1)}, bf16[144,1152]{1,0:T(8,128)(2,1)S(1)}, u32[]{:S(2)}, u32[]{:S(2)}) collective-permute-start(bf16[144,1152]{1,0:T(8,128)(2,1)S(1)} %fusion.12), channel_id=1, source_target_pairs={{0,8},{4,12},{8,0},{12,4},{16,24},{20,28},{24,16},{28,20},{1,9},{5... | collective-permute-start | bytes 995336 | tf_op jit(solution)/shard_map/ppermute | solution.py:253
  293.0 16.0 %collective-permute-start.28 = (bf16[288,1152]{1,0:T(8,128)(2,1)S(1)}, bf16[288,1152]{1,0:T(8,128)(2,1)}, u32[]{:S(2)}, u32[]{:S(2)}) collective-permute-start(bf16[288,1152]{1,0:T(8,128)(2,1)S(1)} %maximum_select_fusion.9), channel_id=1, source_target_pairs={{0,16},{4,20},{8,24},{12,28},{16,0},{20,4},{24,8},{28,12},{1,17},{... | collective-permute-start | bytes 1990664 | tf_op jit(solution)/shard_map/ppermute | solution.py:253
  295.0 21.4 %collective-permute-start.23 = (bf16[576,1152]{1,0:T(8,128)(2,1)S(1)}, bf16[576,1152]{1,0:T(8,128)(2,1)}, u32[]{:S(2)}, u32[]{:S(2)}) collective-permute-start(bf16[576,1152]{1,0:T(8,128)(2,1)S(1)} %maximum_select_fusion.4), channel_id=1, source_target_pairs={{0,4},{4,0},{8,12},{12,8},{16,20},{20,16},{24,28},{28,24},{1,5},{5... | collective-permute-start | bytes 3981320 | tf_op jit(solution)/shard_map/ppermute | solution.py:253
  299.3 126.5 %reduce-scatter.11.cloned.1.call-start = ((), (), s32[]{:S(2)}) async-start(), calls=%async_computation.11 | async-start | bytes 2211840 | tf_op jit(solution)/shard_map/reduce_scatter | solution.py:403
  310.6 10.4 %collective-permute-start.29 = (bf16[576,1152]{1,0:T(8,128)(2,1)S(1)}, bf16[576,1152]{1,0:T(8,128)(2,1)}, u32[]{:S(2)}, u32[]{:S(2)}) collective-permute-start(bf16[576,1152]{1,0:T(8,128)(2,1)S(1)} %maximum_select_fusion.5), channel_id=1, source_target_pairs={{0,4},{4,0},{8,12},{12,8},{16,20},{20,16},{24,28},{28,24},{1,5},{5... | collective-permute-start | bytes 3981320 | tf_op jit(solution)/shard_map/ppermute | solution.py:253
  363.2 13.9 %collective-permute-start.12 = (bf16[288,1152]{1,0:T(8,128)(2,1)S(1)}, bf16[288,1152]{1,0:T(8,128)(2,1)}, u32[]{:S(2)}, u32[]{:S(2)}) collective-permute-start(bf16[288,1152]{1,0:T(8,128)(2,1)S(1)} %dynamic-slice_bitcast_fusion.4), channel_id=1, source_target_pairs={{0,4},{4,0},{8,12},{12,8},{16,20},{20,16},{24,28},{28,24},{1,5},{5... | collective-permute-start | bytes 1990664 | tf_op jit(solution)/shard_map/ppermute | solution.py:244
  363.4 5.9 %collective-permute-start.5 = (f32[4,8,216]{2,1,0:T(8,128)S(1)}, f32[4,8,216]{2,1,0:T(8,128)S(1)}, u32[]{:S(2)}, u32[]{:S(2)}) collective-permute-start(f32[4,8,216]{2,1,0:T(8,128)S(1)} %bitcast.183), channel_id=1, source_target_pairs={{0,3},{1,0},{2,1},{3,2},{4,7},{5,4},{6,5},{7,6},{8,11},{9,8},{10,9... | collective-permute-start | bytes 82952 | tf_op jit(solution)/shard_map/ppermute | solution.py:262
  364.7 8.7 %collective-permute-start.4 = (f32[4,8,216]{2,1,0:T(8,128)S(1)}, f32[4,8,216]{2,1,0:T(8,128)}, u32[]{:S(2)}, u32[]{:S(2)}) collective-permute-start(f32[4,8,216]{2,1,0:T(8,128)S(1)} %bitcast.184), channel_id=1, source_target_pairs={{0,2},{1,3},{2,0},{3,1},{4,6},{5,7},{6,4},{7,5},{8,10},{9,11},{10,... | collective-permute-start | bytes 82952 | tf_op jit(solution)/shard_map/ppermute | solution.py:262
  365.4 7.9 %collective-permute-start.3 = (f32[4,8,216]{2,1,0:T(8,128)S(1)}, f32[4,8,216]{2,1,0:T(8,128)}, u32[]{:S(2)}, u32[]{:S(2)}) collective-permute-start(f32[4,8,216]{2,1,0:T(8,128)S(1)} %bitcast.185), channel_id=1, source_target_pairs={{0,1},{1,2},{2,3},{3,0},{4,5},{5,6},{6,7},{7,4},{8,9},{9,10},{10,1... | collective-permute-start | bytes 82952 | tf_op jit(solution)/shard_map/ppermute | solution.py:262
  369.1 10.9 %collective-permute-start.6 = (bf16[288,1152]{1,0:T(8,128)(2,1)}, bf16[288,1152]{1,0:T(8,128)(2,1)}, u32[]{:S(2)}, u32[]{:S(2)}) collective-permute-start(bf16[288,1152]{1,0:T(8,128)(2,1)} %dynamic-slice_bitcast_fusion.5), channel_id=1, source_target_pairs={{0,4},{4,0},{8,12},{12,8},{16,20},{20,16},{24,28},{28,24},{1,5},{5... | collective-permute-start | bytes 1990664 | tf_op jit(solution)/shard_map/ppermute | solution.py:244
  378.4 9.8 %collective-permute-start.13 = (bf16[144,1152]{1,0:T(8,128)(2,1)S(1)}, bf16[144,1152]{1,0:T(8,128)(2,1)S(1)}, u32[]{:S(2)}, u32[]{:S(2)}) collective-permute-start(bf16[144,1152]{1,0:T(8,128)(2,1)S(1)} %dynamic-slice_bitcast_fusion.8), channel_id=1, source_target_pairs={{0,16},{4,20},{8,24},{12,28},{16,0},{20,4},{24,8},{28,12},{1,17},{... | collective-permute-start | bytes 995336 | tf_op jit(solution)/shard_map/ppermute | solution.py:244
  381.3 10.1 %collective-permute-start.7 = (bf16[144,1152]{1,0:T(8,128)(2,1)S(1)}, bf16[144,1152]{1,0:T(8,128)(2,1)S(1)}, u32[]{:S(2)}, u32[]{:S(2)}) collective-permute-start(bf16[144,1152]{1,0:T(8,128)(2,1)S(1)} %dynamic-slice_bitcast_fusion.9), channel_id=1, source_target_pairs={{0,8},{4,12},{8,0},{12,4},{16,24},{20,28},{24,16},{28,20},{1,9},{5... | collective-permute-start | bytes 995336 | tf_op jit(solution)/shard_map/ppermute | solution.py:244
  388.3 6.0 %collective-permute-start.14 = (bf16[72,1152]{1,0:T(8,128)(2,1)S(1)}, bf16[72,1152]{1,0:T(8,128)(2,1)S(1)}, u32[]{:S(2)}, u32[]{:S(2)}) collective-permute-start(bf16[72,1152]{1,0:T(8,128)(2,1)S(1)} %dynamic-slice_bitcast_fusion.10), channel_id=1, source_target_pairs={{0,8},{4,12},{8,0},{12,4},{16,24},{20,28},{24,16},{28,20},{1,9},{5... | collective-permute-start | bytes 497672 | tf_op jit(solution)/shard_map/ppermute | solution.py:244
  396.9 7.2 %collective-permute-start.9 = (bf16[72,1152]{1,0:T(8,128)(2,1)S(1)}, bf16[72,1152]{1,0:T(8,128)(2,1)S(1)}, u32[]{:S(2)}, u32[]{:S(2)}) collective-permute-start(bf16[72,1152]{1,0:T(8,128)(2,1)S(1)} %fusion.17), channel_id=1, source_target_pairs={{0,16},{4,20},{8,24},{12,28},{16,0},{20,4},{24,8},{28,12},{1,17},{... | collective-permute-start | bytes 497672 | tf_op jit(solution)/shard_map/ppermute | solution.py:253
  399.9 16.6 %collective-permute-start.16 = (bf16[144,1152]{1,0:T(8,128)(2,1)S(1)}, bf16[144,1152]{1,0:T(8,128)(2,1)S(1)}, u32[]{:S(2)}, u32[]{:S(2)}) collective-permute-start(bf16[144,1152]{1,0:T(8,128)(2,1)S(1)} %maximum_select_fusion.11), channel_id=1, source_target_pairs={{0,16},{4,20},{8,24},{12,28},{16,0},{20,4},{24,8},{28,12},{1,17},{... | collective-permute-start | bytes 995336 | tf_op jit(solution)/shard_map/ppermute | solution.py:253
  404.2 12.9 %collective-permute-start.10 = (bf16[144,1152]{1,0:T(8,128)(2,1)S(1)}, bf16[144,1152]{1,0:T(8,128)(2,1)S(1)}, u32[]{:S(2)}, u32[]{:S(2)}) collective-permute-start(bf16[144,1152]{1,0:T(8,128)(2,1)S(1)} %maximum_select_fusion.10), channel_id=1, source_target_pairs={{0,8},{4,12},{8,0},{12,4},{16,24},{20,28},{24,16},{28,20},{1,9},{5... | collective-permute-start | bytes 995336 | tf_op jit(solution)/shard_map/ppermute | solution.py:253
  (24 other events, 167.3 us)
Sparse Core Ops, SparseCore 0:
  12.0 43.0 all-gather.4
  68.0 37.2 reduce-scatter.4
  107.5 39.2 all-gather.8
  148.7 39.0 all-gather.6
  204.8 37.3 reduce-scatter.8
  244.4 37.4 reduce-scatter.6
  299.4 38.3 all-gather.10
  355.8 39.3 reduce-scatter.10

commit v2 on v1

--- a/solution.py
+++ b/solution.py
@@ -5,8 +5,8 @@
 import jax.numpy as jnp
 from jax import lax
 from jax.experimental import pallas as pl
-from jax.experimental.pallas import tpu as pltpu
 from jax.sharding import PartitionSpec as P
+
 
 HEADS = 16
 EPS = 1e-06
@@ -49,14 +49,13 @@
     return pl.BlockSpec(tuple(shape), lambda i: (0,) * rank)
 
 
-def call(body, name, grid, ins, outs):
+def call(body, grid, ins, outs):
     return pl.pallas_call(
         body,
         grid=(grid,),
         in_specs=[block(a.shape) if step else whole(a.shape) for a, step in ins],
         out_specs=[block(shape) for shape, _ in outs],
         out_shape=[jax.ShapeDtypeStruct(shape, dtype) for shape, dtype in outs],
-        name=name,
     )(*[a for a, _ in ins])
 
 
@@ -234,27 +233,34 @@
     return [(i, i ^ (1 << bit)) for i in range(lax.axis_size("dp"))]
 
 
-def scatter_sum(part, bits):
-    index = lax.axis_index("dp")
-    for bit in bits:
-        side = (index >> bit) & 1
-        halves = part.reshape(2, part.shape[0] // 2, part.shape[1])
-        own = lax.dynamic_index_in_dim(halves, side, 0, keepdims=False)
-        other = lax.dynamic_index_in_dim(halves, 1 - side, 0, keepdims=False)
-        got = lax.ppermute(other, "dp", partner(bit))
-        part = (own.astype(F32) + got.astype(F32)).astype(BF16)
-    return part
-
-
-def gather_rows(part, bits):
-    index = lax.axis_index("dp")
-    for bit in reversed(bits):
-        side = (index >> bit) & 1
-        got = lax.ppermute(part, "dp", partner(bit))
-        part = jnp.where(
-            side == 0, jnp.concatenate([part, got], 0), jnp.concatenate([got, part], 0)
-        )
-    return part
+def halve(part, bit):
+    side = (lax.axis_index("dp") >> bit) & 1
+    halves = part.reshape(2, part.shape[0] // 2, part.shape[1])
+    own = lax.dynamic_index_in_dim(halves, side, 0, keepdims=False)
+    other = lax.dynamic_index_in_dim(halves, 1 - side, 0, keepdims=False)
+    return own, lax.ppermute(other, "dp", partner(bit))
+
+
+def add_low(own, got):
+    return (own.astype(F32) + got.astype(F32)).astype(BF16)
+
+
+def double(part, bit):
+    return part, lax.ppermute(part, "dp", partner(bit))
+
+
+def join(own, got, bit):
+    side = (lax.axis_index("dp") >> bit) & 1
+    return jnp.where(side == 0, jnp.concatenate([own, got], 0), jnp.concatenate([got, own], 0))
+
+
+def after(value, *others):
+    return lax.optimization_barrier((value,) + others)[0]
+
+
+def orders():
+    bits = dp_bits()
+    return bits, bits[:1] + bits[2:] + bits[1:2]
 
 
 def shift(value, step):
@@ -277,12 +283,21 @@
     return total
 
 
-def sum_pair(first, second):
-    bits = dp_bits()
-    turned = bits[:1] + bits[2:] + bits[1:2]
-    first = scatter_sum(first, bits)
-    second = scatter_sum(second, turned)
-    return gather_rows(first, bits), gather_rows(second, turned)
+def sum_pair(parts):
+    pairs = list(zip(parts, orders()))
+    for level in range(len(dp_bits())):
+        pairs = [(add_low(*halve(part, bits[level])), bits) for part, bits in pairs]
+    for level in reversed(range(len(dp_bits()))):
+        pairs = [(join(*double(part, bits[level]), bits[level]), bits) for part, bits in pairs]
+    return [part for part, _ in pairs]
+
+
+def all_rows(rows):
+    return lax.all_gather(rows, "mp", axis=0, tiled=True)
+
+
+def own_sum(rows):
+    return lax.psum_scatter(rows, "mp", scatter_dimension=0, tiled=True)
 
 
 def per_device(
@@ -310,12 +325,12 @@
     group_shape = (group, slots, width)
 
     routed, grad_two = call(
-        gather_body, "gather", images,
+        gather_body, images,
         [(picks_col, True), (image_tokens, True), (image_cot, True)],
         [(rows_shape, BF16), (rows_shape, BF16)],
     )
-    group_routed = lax.all_gather(routed, "mp", axis=0, tiled=True)
-    group_two = lax.all_gather(grad_two, "mp", axis=0, tiled=True)
+    group_routed = all_rows(routed)
+    group_two = all_rows(grad_two)
 
     small = jnp.concatenate(
         [conditioning, jnp.broadcast_to(keep_count.astype(BF16)[:, None], (images, 128))], axis=1
@@ -331,7 +346,7 @@
     down_bias_row = down_bias.astype(F32)[None]
 
     mixed_one, qkv, attended, branch = call(
-        functools.partial(attend_body, head_dim), "attend", group,
+        functools.partial(attend_body, head_dim), group,
         [
             (group_routed, True), (modulation, True), (keep, True), (qkv_weight, False),
             (qv_bias.astype(F32), False), (out_weight, False),
@@ -341,19 +356,19 @@
             (group_shape, BF16),
         ],
     )
-    branch_one = lax.psum_scatter(branch, "mp", scatter_dimension=0, tiled=True)
+    branch_one = own_sum(branch)
     hidden_one, mixed_two = call(
-        middle_body, "middle", images,
+        middle_body, images,
         [
             (branch_one, True), (out_bias_row, False), (routed, True), (own_mod, True),
             (own_keep, True),
         ],
         [(rows_shape, F32), (rows_shape, BF16)],
     )
-    group_mixed = lax.all_gather(mixed_two, "mp", axis=0, tiled=True)
+    group_mixed = all_rows(mixed_two)
     unit_shape = (group, slots, hidden_units)
     active, before_grad, down_grad, branch, mixed_grad, up_sum, down_sum = call(
-        forward_body, "forward", group,
+        forward_body, group,
         [
             (group_mixed, True), (group_two, True), (modulation, True), (keep, True),
             (up_weight, False), (up_bias.astype(F32)[None], False), (down_weight, False),
@@ -363,26 +378,35 @@
             (group_shape, BF16), ((group, 1, hidden_units), F32), ((group, 1, width), F32),
         ],
     )
-    mixed_two_grad = lax.psum_scatter(mixed_grad, "mp", scatter_dimension=0, tiled=True)
-    branch_two = lax.psum_scatter(branch, "mp", scatter_dimension=0, tiled=True)
+    mixed_two_grad = own_sum(mixed_grad)
 
     flat = (group * slots, hidden_units)
     wide = (group * slots, width)
     up_part = mm(before_grad.reshape(flat), group_mixed.reshape(wide), TN).astype(BF16)
     down_part = mm(active.reshape(flat), down_grad.reshape(wide), TN).astype(BF16)
-    up_weight_grad, down_weight_grad = sum_pair(up_part, down_part)
+    levels = len(dp_bits())
+    ways = orders()
+    sums = [add_low(*halve(part, way[0])) for part, way in zip((up_part, down_part), ways)]
+    flights = [halve(part, way[1]) for part, way in zip(sums, ways)]
 
     grad_one, branch_grad, middle_stats = call(
-        middle_back_body, "middle_back", images,
+        middle_back_body, images,
         [
             (mixed_two_grad, True), (hidden_one, True), (branch_one, True), (out_bias_row, False),
             (grad_two, True), (own_mod, True), (own_keep, True),
         ],
         [(rows_shape, F32), (rows_shape, BF16), ((images, 3, width), F32)],
     )
-    group_grad = lax.all_gather(branch_grad, "mp", axis=0, tiled=True)
+    group_grad = all_rows(branch_grad)
+    sums = [add_low(after(own, branch_grad), got) for own, got in flights]
+    for level in range(2, levels):
+        sums = [add_low(*halve(part, way[level])) for part, way in zip(sums, ways)]
+    for level in reversed(range(2, levels)):
+        sums = [join(*double(part, way[level]), way[level]) for part, way in zip(sums, ways)]
+    flights = [double(part, way[1]) for part, way in zip(sums, ways)]
+    branch_two = own_sum(branch)
     layer_out, gate_grad = call(
-        out_body, "out", images,
+        out_body, images,
         [
             (branch_two, True), (hidden_one, True), (down_bias_row, False), (own_mod, True),
             (own_keep, True), (grad_two, True), (picks_row, True), (image_tokens, True),
@@ -390,7 +414,7 @@
         [((images, patches, width), BF16), ((images, 1, width), F32)],
     )
     qkv_grad, mixed_grad, attend_stats, bias_sums = call(
-        functools.partial(attend_back_body, head_dim), "attend_back", group,
+        functools.partial(attend_back_body, head_dim), group,
         [
             (group_grad, True), (qkv, True), (group_routed, True), (keep, True),
             (qkv_weight, False), (out_weight, False),
@@ -400,14 +424,18 @@
             ((group, 2, cols), F32),
         ],
     )
-    mixed_one_grad = lax.psum_scatter(mixed_grad, "mp", scatter_dimension=0, tiled=True)
+    mixed_one_grad = own_sum(mixed_grad)
+    sums = [join(after(own, attend_stats), got, way[1]) for (own, got), way in zip(flights, ways)]
+    up_weight_grad, down_weight_grad = [
+        join(*double(part, way[0]), way[0]) for part, way in zip(sums, ways)
+    ]
 
     qkv_part = jnp.einsum(
         "gtsc,gsd->tcd", qkv_grad, mixed_one, preferred_element_type=F32
     ).reshape(3 * cols, width)
     out_part = mm(attended.reshape(-1, cols), group_grad.reshape(wide), TN)
     part = jnp.concatenate([qkv_part.astype(BF16), out_part.astype(BF16)], axis=0)
-    part = jnp.concatenate(sum_pair(part[: 2 * cols], part[2 * cols :]), axis=0)
+    part = jnp.concatenate(sum_pair((part[: 2 * cols], part[2 * cols :])), axis=0)
     qkv_weight_grad = part[: 3 * cols].reshape(3, cols, width)
     out_weight_grad = part[3 * cols :]
 
@@ -444,10 +472,10 @@
     ]
 
     tokens_grad = call(
-        first_back_body, "first_back", images,
+        first_back_body, images,
         [
             (mixed_one_grad, True), (routed, True), (own_mod, True), (grad_one, True),
-            (picks_row, True), (image_cot, True),
+            (after(picks_row, ada_weight_grad), True), (image_cot, True),
         ],
         [((images, patches, width), BF16)],
     )[0]
@@ -478,6 +506,7 @@
         P(both, None), P(both, None), P(both, None), P(both), P(None, "mp", None), P(None, "mp"),
         P("mp", None), P(), P("mp", None), P("mp"), P("mp", None), P(),
     )
+
     return jax.shard_map(
         per_device, mesh=mesh, in_specs=in_specs, out_specs=out_specs, check_vma=False
     )

time: 437 us -> 430 us (0.984)
    ppermute x24, waiting for transfers between devices: 84.7 us -> 25.5 us  [the longest x12 13.8 us: double(): return (part, lax.ppermute(part, 'dp', partner(bit)))]
    reduce_scatter x4, waiting for transfers between devices: 34.7 us -> 82.7 us  [own_sum(): return lax.psum_scatter(rows, 'mp', scatter_dimension=0, tiled=True)]
    all_gather x4, waiting for transfers between devices: 111 us -> 123 us  [all_rows(): return lax.all_gather(rows, 'mp', axis=0, tiled=True)]
    unnamed x40 -> x44, local copies, waits for them, and re-layouts: 7.86 us -> 2.67 us
  transfers between devices with their start and end apart: 38 -> 38, of which waited for: 22 -> 18; matrix products, arithmetic and copies ran while one was open for 15% -> 16% of each run, Pallas kernels for 2% -> 6%
where the time goes in v2:
time: 430 us; the launch traced here: 429 us
  waiting for transfers between devices  237 us (55%)
  Pallas kernels  62.4 us (15%)
  starting transfers between devices  32.3 us (8%)
  other arithmetic  32 us (7%)
  matrix products  22.5 us (5%)
  local copies, waits for them, and re-layouts  18.1 us (4%)
  between operations  15.4 us (4%)
  blocking collectives  9.53 us (2%)
    all_gather x4, waiting for transfers between devices, all_rows(): return lax.all_gather(rows, 'mp', axis=0, tiled=True)  123 us
    reduce_scatter x4, waiting for transfers between devices, own_sum(): return lax.psum_scatter(rows, 'mp', scatter_dimension=0, tiled=True)  82.7 us
    pallas_call x8, Pallas kernels, call(): pl.pallas_call(body, grid=(grid,), in_specs=[block(a.shape) if step else...  62.4 us
    dot_general x5, matrix products, mm(): lax.dot_general(left, right, (dims, ((), ())), preferred_element_type=F32)  18.4 us
    ppermute x12, waiting for transfers between devices, double(): return (part, lax.ppermute(part, 'dp', partner(bit)))  13.8 us
    ppermute x12, waiting for transfers between devices, halve(): return (own, lax.ppermute(other, 'dp', partner(bit)))  11.7 us
    ppermute x6, starting transfers between devices, shift(): lax.ppermute(value, 'mp', [(i, (i + step) % count) for i in range(count)])  11.3 us
    ppermute x12, starting transfers between devices, halve(): return (own, lax.ppermute(other, 'dp', partner(bit)))  10.7 us
  transfers between devices with their start and end apart: 38, of which 18 were waited for; matrix products, arithmetic and copies ran while one was open for 16% of the time, Pallas kernels for 6%

profile of v2, /device:TPU:0, one launch (start us, length us, event | category | flops | bytes accessed | tf_op | source)
XLA Modules:
  0.0 428.9 jit_solution(10402494562487646158)
XLA Ops:
  9.3 2.6 shard_map.238
  12.6 5.1 %collective-permute-start.2 = (bf16[1,1280]{1,0:T(2,128)(2,1)S(1)}, bf16[1,1280]{1,0:T(2,128)(2,1)S(1)}, u32[]{:S(2)}, u32[]{:S(2)}) collective-permute-start(bf16[1,1280]{1,0:T(2,128)(2,1)S(1)} %get-tuple-element.82), channel_id=1, source_target_pairs={{0,3},{1,0},{2,1},{3,2},{4,7},{5,4},{6,5},{7,6},{8,11},{9,8},{10,9... | collective-permute-start | bytes 7688 | tf_op jit(solution)/shard_map/ppermute | solution.py:268
  19.4 2.8 collective-permute-done.1
  23.9 9.7 %convolution_add_fusion = f32[4,6912]{1,0:T(4,128)S(1)} fusion(bf16[6912,1152]{1,0:T(8,128)(2,1)} %param.20, f32[6912]{0:T(1024)S(1)} %convert_element_type.240, bf16[4,1280]{1,0:T(4,128)(2,1)S(1)} %broadcast_select_fusion), kind=kOutput, calls=%fused_computation.3 | convolution fusion | flops 63756288 | bytes 16073728 | tf_op jit(solution)/shard_map/dot_general | solution.py:35
  34.9 20.2 %all-gather.5.cloned.1.call-done.routed = bf16[4,192,1152]{2,1,0:T(8,128)(2,1)} async-done(((bf16[1,192,1152]{2,1,0:T(8,128)(2,1)}), bf16[4,192,1152]{2,1,0:T(8,128)(2,1)}) %all-gather.5.cloned.1.call-update) | async-done | bytes 1769488 | tf_op jit(solution)/shard_map/all_gather | solution.py:296
  55.1 12.8 %shard_map.239 = (bf16[4,192,1152]{2,1,0:T(8,128)(2,1)}, bf16[4,3,192,288]{3,2,1,0:T(8,128)(2,1)}, bf16[4,192,288]{2,1,0:T(8,128)(2,1)}, bf16[4,192,1152]{2,1,0:T(8,128)(2,1)}) custom-call(bf16[4,192,1152]{2,1,0:T(8,128)(2,1)} %all-gather.5.cloned.1.call-done.routed, f32[4,6,1152]{2,1,0:T(8,128)} %reshape.236.mod, f32[4,1,128]{2,1,0:T(1,128)} %bitcast.176, ...), custom_call_target="tpu_custom_call" | custom-call | tf_op jit(solution)/shard_map/pallas_call | solution.py:53
  70.7 34.7 %reduce-scatter.5.cloned.1.call-done.branch = bf16[1,192,1152]{2,1,0:T(8,128)(2,1)} async-done(((bf16[4,192,1152]{2,1,0:T(8,128)(2,1)}), bf16[1,192,1152]{2,1,0:T(8,128)(2,1)}) %reduce-scatter.5.cloned.1.call-update) | async-done | bytes 442384 | tf_op jit(solution)/shard_map/reduce_scatter | solution.py:300
  105.9 2.5 shard_map.240
  109.1 37.1 %all-gather.9.cloned.1.call-done.grad_two = bf16[4,192,1152]{2,1,0:T(8,128)(2,1)} async-done(((bf16[1,192,1152]{2,1,0:T(8,128)(2,1)}), bf16[4,192,1152]{2,1,0:T(8,128)(2,1)}) %all-gather.9.cloned.1.call-update) | async-done | bytes 1769488 | tf_op jit(solution)/shard_map/all_gather | solution.py:296
  146.2 41.1 %all-gather.7.cloned.1.call-done.mixed = bf16[4,192,1152]{2,1,0:T(8,128)(2,1)} async-done(((bf16[1,192,1152]{2,1,0:T(8,128)(2,1)}), bf16[4,192,1152]{2,1,0:T(8,128)(2,1)}) %all-gather.7.cloned.1.call-update) | async-done | bytes 1769488 | tf_op jit(solution)/shard_map/all_gather | solution.py:296
  187.3 16.8 %shard_map.241 = (bf16[4,192,1152]{2,1,0:T(8,128)(2,1)}, bf16[4,192,1152]{2,1,0:T(8,128)(2,1)}, bf16[4,192,1152]{2,1,0:T(8,128)(2,1)}, bf16[4,192,1152]{2,1,0:T(...) custom-call(bf16[4,192,1152]{2,1,0:T(8,128)(2,1)} %all-gather.7.cloned.1.call-done.mixed, ...), custom_call_target="tpu_custom_call" | custom-call | tf_op jit(solution)/shard_map/pallas_call | solution.py:53
  205.7 4.1 fusion
  212.6 2.5 fusion.1
  224.9 16.8 %reduce-scatter.9.cloned.1.call-done.mixed_grad = bf16[1,192,1152]{2,1,0:T(8,128)(2,1)} async-done(((bf16[4,192,1152]{2,1,0:T(8,128)(2,1)}), bf16[1,192,1152]{2,1,0:T(8,128)(2,1)}) %reduce-scatter.9.cloned.1.call-update) | async-done | bytes 442384 | tf_op jit(solution)/shard_map/reduce_scatter | solution.py:300
  241.7 3.5 shard_map.243
  250.1 31.3 %reduce-scatter.7.cloned.1.call-done.branch = bf16[1,192,1152]{2,1,0:T(8,128)(2,1)} async-done(((bf16[4,192,1152]{2,1,0:T(8,128)(2,1)}), bf16[1,192,1152]{2,1,0:T(8,128)(2,1)}) %reduce-scatter.7.cloned.1.call-update) | async-done | bytes 442384 | tf_op jit(solution)/shard_map/reduce_scatter | solution.py:300
  281.4 3.1 shard_map.242
  287.8 6.0 %collective-permute-done.21 = bf16[144,1152]{1,0:T(8,128)(2,1)S(1)} collective-permute-done((bf16[144,1152]{1,0:T(8,128)(2,1)S(1)}, bf16[144,1152]{1,0:T(8,128)(2,1)S(1)}, u32[]{:S(2)}, u32[]{:S(2)}) %collective-permute-start.21) | collective-permute-done | bytes 331808 | tf_op jit(solution)/shard_map/ppermute | solution.py:249
  297.9 24.8 %all-gather.11.cloned.1.call-done.grad = bf16[4,192,1152]{2,1,0:T(8,128)(2,1)} async-done(((bf16[1,192,1152]{2,1,0:T(8,128)(2,1)}), bf16[4,192,1152]{2,1,0:T(8,128)(2,1)}) %all-gather.11.cloned.1.call-update) | async-done | bytes 1769488 | tf_op jit(solution)/shard_map/all_gather | solution.py:296
  322.8 17.8 %shard_map.244 = (bf16[4,3,192,288]{3,2,1,0:T(8,128)(2,1)}, bf16[4,192,1152]{2,1,0:T(8,128)(2,1)}, f32[4,3,1152]{2,1,0:T(4,128)}, f32[4,2,288]{2,1,0:T(2,128)}) custom-call(bf16[4,192,1152]{2,1,0:T(8,128)(2,1)} %all-gather.11.cloned.1.call-done.grad, bf16[4,3,192,288]{3,2,1,0:T(8,128)(2,1)} %get-tuple-element.50.qkv, ...), custom_call_target="tpu_custom_call" | custom-call | tf_op jit(solution)/shard_map/pallas_call | solution.py:53
  343.8 4.1 bitcast_convert_fusion
  350.1 3.3 collective-permute-start.5
  357.6 2.1 maximum_select_fusion.5
  361.2 9.5 %all_gather.19 = bf16[8,128,128]{2,1,0:T(8,128)(2,1)S(1)} all-gather(bf16[1,128,128]{2,1,0:T(8,128)(2,1)S(1)} %pad_bitcast_fusion), channel_id=1, replica_groups=mesh['dp'=8,'mp'=4] {'dp'}, dimensions={0}, use_global_device_ids=true | all-gather | bytes 294912 | tf_op jit(solution)/shard_map/all_gather | solution.py:461
  379.8 6.6 %collective-permute-done.13 = bf16[144,1152]{1,0:T(8,128)(2,1)S(1)} collective-permute-done((bf16[144,1152]{1,0:T(8,128)(2,1)S(1)}, bf16[144,1152]{1,0:T(8,128)(2,1)S(1)}, u32[]{:S(2)}, u32[]{:S(2)}) %collective-permute-start.13) | collective-permute-done | bytes 331808 | tf_op jit(solution)/shard_map/ppermute | solution.py:241
  389.8 2.8 collective-permute-done.14
  395.3 2.8 collective-permute-done.15
  399.3 2.8 collective-permute-done.9
  402.2 4.6 %fusion.2 = f32[1152,1152]{1,0:T(8,128)} fusion(bf16[576,1152]{1,0:T(8,128)(2,1)} %collective-permute-done.23, bf16[576,1152]{1,0:T(8,128)(2,1)S(1)} %maximum_select_fusion.4, pred[]{:T(512)S(6)} %eq.11), kind=kLoop, calls=%fused_computation.9 | loop fusion | flops 13271040 | bytes 7962625 | tf_op jit(solution)/shard_map/convert_element_type | solution.py:491
  409.6 4.6 %fusion.3 = f32[1152,1152]{1,0:T(8,128)} fusion(bf16[576,1152]{1,0:T(8,128)(2,1)} %collective-permute-done.29, bf16[576,1152]{1,0:T(8,128)(2,1)S(1)} %maximum_select_fusion.5, pred[]{:T(512)S(6)} %eq.11), kind=kLoop, calls=%fused_computation.11 | loop fusion | flops 13271040 | bytes 7962625 | tf_op jit(solution)/shard_map/convert_element_type | solution.py:493
  415.4 2.2 convert.21
  418.8 3.3 shard_map.245
  (197 shorter events, 69.3 us)
Async XLA Ops:
  7.2 47.9 %all-gather.5.cloned.1.call-start = ((), (), s32[]{:S(2)}) async-start(), calls=%async_computation.4 | async-start | bytes 2211840 | tf_op jit(solution)/shard_map/all_gather | solution.py:296
  11.9 93.5 %reduce-scatter.5.cloned.1.call-start = ((), (), s32[]{:S(2)}) async-start(), calls=%async_computation.5 | async-start | bytes 2211840 | tf_op jit(solution)/shard_map/reduce_scatter | solution.py:300
  12.6 6.8 %collective-permute-start.2 = (bf16[1,1280]{1,0:T(2,128)(2,1)S(1)}, bf16[1,1280]{1,0:T(2,128)(2,1)S(1)}, u32[]{:S(2)}, u32[]{:S(2)}) collective-permute-start(bf16[1,1280]{1,0:T(2,128)(2,1)S(1)} %get-tuple-element.82), channel_id=1, source_target_pairs={{0,3},{1,0},{2,1},{3,2},{4,7},{5,4},{6,5},{7,6},{8,11},{9,8},{10,9... | collective-permute-start | bytes 7688 | tf_op jit(solution)/shard_map/ppermute | solution.py:268
  68.0 78.3 %all-gather.9.cloned.1.call-start = ((), (), s32[]{:S(2)}) async-start(), calls=%async_computation.7 | async-start | bytes 2211840 | tf_op jit(solution)/shard_map/all_gather | solution.py:296
  68.7 118.6 %all-gather.7.cloned.1.call-start = ((), (), s32[]{:S(2)}) async-start(), calls=%async_computation.6 | async-start | bytes 2211840 | tf_op jit(solution)/shard_map/all_gather | solution.py:296
  108.4 133.3 %reduce-scatter.9.cloned.1.call-start = ((), (), s32[]{:S(2)}) async-start(), calls=%async_computation.9 | async-start | bytes 2211840 | tf_op jit(solution)/shard_map/reduce_scatter | solution.py:300
  204.2 77.2 %reduce-scatter.7.cloned.1.call-start = ((), (), s32[]{:S(2)}) async-start(), calls=%async_computation.8 | async-start | bytes 2211840 | tf_op jit(solution)/shard_map/reduce_scatter | solution.py:300
  204.8 118.0 %all-gather.11.cloned.1.call-start = ((), (), s32[]{:S(2)}) async-start(), calls=%async_computation.10 | async-start | bytes 2211840 | tf_op jit(solution)/shard_map/all_gather | solution.py:296
  211.0 6.1 %collective-permute-start.18 = (bf16[576,1152]{1,0:T(8,128)(2,1)}, bf16[576,1152]{1,0:T(8,128)(2,1)}, u32[]{:S(2)}, u32[]{:S(2)}) collective-permute-start(bf16[576,1152]{1,0:T(8,128)(2,1)} %dynamic-slice_bitcast_fusion.1), channel_id=1, source_target_pairs={{0,4},{4,0},{8,12},{12,8},{16,20},{20,16},{24,28},{28,24},{1,5},{5... | collective-permute-start | bytes 3981320 | tf_op jit(solution)/shard_map/ppermute | solution.py:241
  220.1 25.3 %collective-permute-start.19 = (bf16[288,1152]{1,0:T(8,128)(2,1)}, bf16[288,1152]{1,0:T(8,128)(2,1)}, u32[]{:S(2)}, u32[]{:S(2)}) collective-permute-start(bf16[288,1152]{1,0:T(8,128)(2,1)} %get-tuple-element.76), channel_id=1, source_target_pairs={{0,8},{4,12},{8,0},{12,4},{16,24},{20,28},{24,16},{28,20},{1,9},{5... | collective-permute-start | bytes 1990664 | tf_op jit(solution)/shard_map/ppermute | solution.py:241
  223.4 24.9 %collective-permute-start.25 = (bf16[288,1152]{1,0:T(8,128)(2,1)S(1)}, bf16[288,1152]{1,0:T(8,128)(2,1)S(1)}, u32[]{:S(2)}, u32[]{:S(2)}) collective-permute-start(bf16[288,1152]{1,0:T(8,128)(2,1)S(1)} %get-tuple-element.74), channel_id=1, source_target_pairs={{0,16},{4,20},{8,24},{12,28},{16,0},{20,4},{24,8},{28,12},{1,17},{... | collective-permute-start | bytes 1990664 | tf_op jit(solution)/shard_map/ppermute | solution.py:241
  245.2 173.6 %reduce-scatter.11.cloned.1.call-start = ((), (), s32[]{:S(2)}) async-start(), calls=%async_computation.11 | async-start | bytes 2211840 | tf_op jit(solution)/shard_map/reduce_scatter | solution.py:300
  246.8 37.7 %collective-permute-start.20 = (bf16[144,1152]{1,0:T(8,128)(2,1)S(1)}, bf16[144,1152]{1,0:T(8,128)(2,1)S(1)}, u32[]{:S(2)}, u32[]{:S(2)}) collective-permute-start(bf16[144,1152]{1,0:T(8,128)(2,1)S(1)} %dynamic-slice_bitcast_fusion.9), channel_id=1, source_target_pairs={{0,16},{4,20},{8,24},{12,28},{16,0},{20,4},{24,8},{28,12},{1,17},{... | collective-permute-start | bytes 995336 | tf_op jit(solution)/shard_map/ppermute | solution.py:241
  248.5 37.6 %collective-permute-start.26 = (bf16[144,1152]{1,0:T(8,128)(2,1)S(1)}, bf16[144,1152]{1,0:T(8,128)(2,1)S(1)}, u32[]{:S(2)}, u32[]{:S(2)}) collective-permute-start(bf16[144,1152]{1,0:T(8,128)(2,1)S(1)} %dynamic-slice_bitcast_fusion.8), channel_id=1, source_target_pairs={{0,8},{4,12},{8,0},{12,4},{16,24},{20,28},{24,16},{28,20},{1,9},{5... | collective-permute-start | bytes 995336 | tf_op jit(solution)/shard_map/ppermute | solution.py:241
  284.6 9.2 %collective-permute-start.21 = (bf16[144,1152]{1,0:T(8,128)(2,1)S(1)}, bf16[144,1152]{1,0:T(8,128)(2,1)S(1)}, u32[]{:S(2)}, u32[]{:S(2)}) collective-permute-start(bf16[144,1152]{1,0:T(8,128)(2,1)S(1)} %fusion.11), channel_id=1, source_target_pairs={{0,16},{4,20},{8,24},{12,28},{16,0},{20,4},{24,8},{28,12},{1,17},{... | collective-permute-start | bytes 995336 | tf_op jit(solution)/shard_map/ppermute | solution.py:249
  286.2 9.3 %collective-permute-start.27 = (bf16[144,1152]{1,0:T(8,128)(2,1)S(1)}, bf16[144,1152]{1,0:T(8,128)(2,1)S(1)}, u32[]{:S(2)}, u32[]{:S(2)}) collective-permute-start(bf16[144,1152]{1,0:T(8,128)(2,1)S(1)} %fusion.10), channel_id=1, source_target_pairs={{0,8},{4,12},{8,0},{12,4},{16,24},{20,28},{24,16},{28,20},{1,9},{5... | collective-permute-start | bytes 995336 | tf_op jit(solution)/shard_map/ppermute | solution.py:249
  293.9 61.4 %collective-permute-start.22 = (bf16[288,1152]{1,0:T(8,128)(2,1)S(1)}, bf16[288,1152]{1,0:T(8,128)(2,1)}, u32[]{:S(2)}, u32[]{:S(2)}) collective-permute-start(bf16[288,1152]{1,0:T(8,128)(2,1)S(1)} %maximum_select_fusion.8), channel_id=1, source_target_pairs={{0,8},{4,12},{8,0},{12,4},{16,24},{20,28},{24,16},{28,20},{1,9},{5... | collective-permute-start | bytes 1990664 | tf_op jit(solution)/shard_map/ppermute | solution.py:249
  296.4 60.6 %collective-permute-start.28 = (bf16[288,1152]{1,0:T(8,128)(2,1)}, bf16[288,1152]{1,0:T(8,128)(2,1)}, u32[]{:S(2)}, u32[]{:S(2)}) collective-permute-start(bf16[288,1152]{1,0:T(8,128)(2,1)} %maximum_select_fusion.9), channel_id=1, source_target_pairs={{0,16},{4,20},{8,24},{12,28},{16,0},{20,4},{24,8},{28,12},{1,17},{... | collective-permute-start | bytes 1990664 | tf_op jit(solution)/shard_map/ppermute | solution.py:249
  341.9 17.8 %collective-permute-start.4 = (f32[4,8,216]{2,1,0:T(8,128)S(1)}, f32[4,8,216]{2,1,0:T(8,128)S(1)}, u32[]{:S(2)}, u32[]{:S(2)}) collective-permute-start(f32[4,8,216]{2,1,0:T(8,128)S(1)} %bitcast.180), channel_id=1, source_target_pairs={{0,2},{1,3},{2,0},{3,1},{4,6},{5,7},{6,4},{7,5},{8,10},{9,11},{10,... | collective-permute-start | bytes 82952 | tf_op jit(solution)/shard_map/ppermute | solution.py:268
  343.3 17.0 %collective-permute-start.3 = (f32[4,8,216]{2,1,0:T(8,128)S(1)}, f32[4,8,216]{2,1,0:T(8,128)S(1)}, u32[]{:S(2)}, u32[]{:S(2)}) collective-permute-start(f32[4,8,216]{2,1,0:T(8,128)S(1)} %bitcast.179), channel_id=1, source_target_pairs={{0,1},{1,2},{2,3},{3,0},{4,5},{5,6},{6,7},{7,4},{8,9},{9,10},{10,1... | collective-permute-start | bytes 82952 | tf_op jit(solution)/shard_map/ppermute | solution.py:268
  350.1 9.6 %collective-permute-start.5 = (f32[4,8,216]{2,1,0:T(8,128)S(1)}, f32[4,8,216]{2,1,0:T(8,128)}, u32[]{:S(2)}, u32[]{:S(2)}) collective-permute-start(f32[4,8,216]{2,1,0:T(8,128)S(1)} %bitcast.181), channel_id=1, source_target_pairs={{0,3},{1,0},{2,1},{3,2},{4,7},{5,4},{6,5},{7,6},{8,11},{9,8},{10,9... | collective-permute-start | bytes 82952 | tf_op jit(solution)/shard_map/ppermute | solution.py:268
  355.3 19.5 %collective-permute-start.12 = (bf16[288,1152]{1,0:T(8,128)(2,1)}, bf16[288,1152]{1,0:T(8,128)(2,1)}, u32[]{:S(2)}, u32[]{:S(2)}) collective-permute-start(bf16[288,1152]{1,0:T(8,128)(2,1)} %dynamic-slice_bitcast_fusion.6), channel_id=1, source_target_pairs={{0,4},{4,0},{8,12},{12,8},{16,20},{20,16},{24,28},{28,24},{1,5},{5... | collective-permute-start | bytes 1990664 | tf_op jit(solution)/shard_map/ppermute | solution.py:241
  357.0 20.9 %collective-permute-start.6 = (bf16[288,1152]{1,0:T(8,128)(2,1)}, bf16[288,1152]{1,0:T(8,128)(2,1)}, u32[]{:S(2)}, u32[]{:S(2)}) collective-permute-start(bf16[288,1152]{1,0:T(8,128)(2,1)} %dynamic-slice_bitcast_fusion.7), channel_id=1, source_target_pairs={{0,4},{4,0},{8,12},{12,8},{16,20},{20,16},{24,28},{28,24},{1,5},{5... | collective-permute-start | bytes 1990664 | tf_op jit(solution)/shard_map/ppermute | solution.py:241
  359.7 42.6 %collective-permute-start.23 = (bf16[576,1152]{1,0:T(8,128)(2,1)S(1)}, bf16[576,1152]{1,0:T(8,128)(2,1)}, u32[]{:S(2)}, u32[]{:S(2)}) collective-permute-start(bf16[576,1152]{1,0:T(8,128)(2,1)S(1)} %maximum_select_fusion.4), channel_id=1, source_target_pairs={{0,4},{4,0},{8,12},{12,8},{16,20},{20,16},{24,28},{28,24},{1,5},{5... | collective-permute-start | bytes 3981320 | tf_op jit(solution)/shard_map/ppermute | solution.py:249
  359.8 49.8 %collective-permute-start.29 = (bf16[576,1152]{1,0:T(8,128)(2,1)S(1)}, bf16[576,1152]{1,0:T(8,128)(2,1)}, u32[]{:S(2)}, u32[]{:S(2)}) collective-permute-start(bf16[576,1152]{1,0:T(8,128)(2,1)S(1)} %maximum_select_fusion.5), channel_id=1, source_target_pairs={{0,4},{4,0},{8,12},{12,8},{16,20},{20,16},{24,28},{28,24},{1,5},{5... | collective-permute-start | bytes 3981320 | tf_op jit(solution)/shard_map/ppermute | solution.py:249
  376.3 10.1 %collective-permute-start.13 = (bf16[144,1152]{1,0:T(8,128)(2,1)S(1)}, bf16[144,1152]{1,0:T(8,128)(2,1)S(1)}, u32[]{:S(2)}, u32[]{:S(2)}) collective-permute-start(bf16[144,1152]{1,0:T(8,128)(2,1)S(1)} %dynamic-slice_bitcast_fusion.10), channel_id=1, source_target_pairs={{0,16},{4,20},{8,24},{12,28},{16,0},{20,4},{24,8},{28,12},{1,17},{... | collective-permute-start | bytes 995336 | tf_op jit(solution)/shard_map/ppermute | solution.py:241
  379.2 10.2 %collective-permute-start.7 = (bf16[144,1152]{1,0:T(8,128)(2,1)S(1)}, bf16[144,1152]{1,0:T(8,128)(2,1)S(1)}, u32[]{:S(2)}, u32[]{:S(2)}) collective-permute-start(bf16[144,1152]{1,0:T(8,128)(2,1)S(1)} %dynamic-slice_bitcast_fusion.11), channel_id=1, source_target_pairs={{0,8},{4,12},{8,0},{12,4},{16,24},{20,28},{24,16},{28,20},{1,9},{5... | collective-permute-start | bytes 995336 | tf_op jit(solution)/shard_map/ppermute | solution.py:241
  386.6 6.0 %collective-permute-start.14 = (bf16[72,1152]{1,0:T(8,128)(2,1)S(1)}, bf16[72,1152]{1,0:T(8,128)(2,1)S(1)}, u32[]{:S(2)}, u32[]{:S(2)}) collective-permute-start(bf16[72,1152]{1,0:T(8,128)(2,1)S(1)} %dynamic-slice_bitcast_fusion.12), channel_id=1, source_target_pairs={{0,8},{4,12},{8,0},{12,4},{16,24},{20,28},{24,16},{28,20},{1,9},{5... | collective-permute-start | bytes 497672 | tf_op jit(solution)/shard_map/ppermute | solution.py:241
  394.9 7.2 %collective-permute-start.9 = (bf16[72,1152]{1,0:T(8,128)(2,1)S(1)}, bf16[72,1152]{1,0:T(8,128)(2,1)S(1)}, u32[]{:S(2)}, u32[]{:S(2)}) collective-permute-start(bf16[72,1152]{1,0:T(8,128)(2,1)S(1)} %fusion.15), channel_id=1, source_target_pairs={{0,16},{4,20},{8,24},{12,28},{16,0},{20,4},{24,8},{28,12},{1,17},{... | collective-permute-start | bytes 497672 | tf_op jit(solution)/shard_map/ppermute | solution.py:249
  398.1 9.3 %collective-permute-start.16 = (bf16[144,1152]{1,0:T(8,128)(2,1)S(1)}, bf16[144,1152]{1,0:T(8,128)(2,1)S(1)}, u32[]{:S(2)}, u32[]{:S(2)}) collective-permute-start(bf16[144,1152]{1,0:T(8,128)(2,1)S(1)} %maximum_select_fusion.11), channel_id=1, source_target_pairs={{0,16},{4,20},{8,24},{12,28},{16,0},{20,4},{24,8},{28,12},{1,17},{... | collective-permute-start | bytes 995336 | tf_op jit(solution)/shard_map/ppermute | solution.py:249
  402.2 7.2 %collective-permute-start.10 = (bf16[144,1152]{1,0:T(8,128)(2,1)S(1)}, bf16[144,1152]{1,0:T(8,128)(2,1)S(1)}, u32[]{:S(2)}, u32[]{:S(2)}) collective-permute-start(bf16[144,1152]{1,0:T(8,128)(2,1)S(1)} %maximum_select_fusion.10), channel_id=1, source_target_pairs={{0,8},{4,12},{8,0},{12,4},{16,24},{20,28},{24,16},{28,20},{1,9},{5... | collective-permute-start | bytes 995336 | tf_op jit(solution)/shard_map/ppermute | solution.py:249
  407.6 6.6 %collective-permute-start.17 = (bf16[288,1152]{1,0:T(8,128)(2,1)S(1)}, bf16[288,1152]{1,0:T(8,128)(2,1)S(1)}, u32[]{:S(2)}, u32[]{:S(2)}) collective-permute-start(bf16[288,1152]{1,0:T(8,128)(2,1)S(1)} %maximum_select_fusion.7), channel_id=1, source_target_pairs={{0,4},{4,0},{8,12},{12,8},{16,20},{20,16},{24,28},{28,24},{1,5},{5... | collective-permute-start | bytes 1990664 | tf_op jit(solution)/shard_map/ppermute | solution.py:249
  (26 other events, 156.2 us)
Sparse Core Ops, SparseCore 0:
  12.0 43.0 all-gather.4
  68.1 37.2 reduce-scatter.4
  107.0 39.2 all-gather.8
  148.2 39.0 all-gather.6
  204.3 37.3 reduce-scatter.8
  243.9 37.4 reduce-scatter.6
  283.5 39.2 all-gather.10
  341.6 38.0 reduce-scatter.10

commit v3 on v2

--- a/solution.py
+++ b/solution.py
@@ -5,6 +5,7 @@
 import jax.numpy as jnp
 from jax import lax
 from jax.experimental import pallas as pl
+from jax.experimental.pallas import tpu as pltpu
 from jax.sharding import PartitionSpec as P
 
 
@@ -49,12 +50,15 @@
     return pl.BlockSpec(tuple(shape), lambda i: (0,) * rank)
 
 
-def call(body, grid, ins, outs):
+def call(body, grid, ins, outs, fixed=0, scratch=()):
+    moving = len(outs) - fixed
     return pl.pallas_call(
         body,
         grid=(grid,),
         in_specs=[block(a.shape) if step else whole(a.shape) for a, step in ins],
-        out_specs=[block(shape) for shape, _ in outs],
+        out_specs=[block(shape) for shape, _ in outs[:moving]]
+        + [whole(shape) for shape, _ in outs[moving:]],
+        scratch_shapes=list(scratch),
         out_shape=[jax.ShapeDtypeStruct(shape, dtype) for shape, dtype in outs],
     )(*[a for a, _ in ins])
 
@@ -116,7 +120,8 @@
 
 
 def attend_back_body(
-    head_dim, grad, qkv, routed, keep, weight, out_weight, qkv_grad, mixed_grad, stats, bias_sums
+    head_dim, grad, qkv, routed, mixed, attended, keep, weight, out_weight,
+    mixed_grad, stats, bias_sums, part, total,
 ):
     slots, cols = routed.shape[1], weight.shape[1]
     scale = 1.0 / math.sqrt(head_dim)
@@ -141,9 +146,21 @@
     query_grad = (query_grad * scale).astype(BF16)
     key_grad = (key_grad * scale).astype(BF16)
     value_grad = value_grad.astype(BF16)
-    qkv_grad[0, 0] = query_grad
-    qkv_grad[0, 1] = key_grad
-    qkv_grad[0, 2] = value_grad
+    step = pl.program_id(0)
+
+    @pl.when(step == 0)
+    def _():
+        total[...] = jnp.zeros_like(total)
+
+    total[0] += mm(query_grad, mixed[0], TN)
+    total[1] += mm(key_grad, mixed[0], TN)
+    total[2] += mm(value_grad, mixed[0], TN)
+    total[3] += mm(attended[0], rows_grad, TN)
+
+    @pl.when(step == pl.num_programs(0) - 1)
+    def _():
+        part[...] = total[...].astype(BF16)
+
     rows = mm(query_grad, weight[0]) + mm(key_grad, weight[1]) + mm(value_grad, weight[2])
     mixed_grad[0] = rows.astype(BF16)
     normed, _ = norm_rows(routed[0].astype(F32))
@@ -154,27 +171,42 @@
     bias_sums[0, 1:2, :] = jnp.sum(value_grad.astype(F32), axis=0, keepdims=True)
 
 
-def forward_body(
-    mixed, grad_two, mod, keep, up, up_bias, down,
-    active, before_grad, down_grad, branch, mixed_grad, up_sum, down_sum,
-):
-    slots = mixed.shape[1]
-    gate = live_rows(keep, slots) * mod_row(mod, 5)
-    rows_grad = (gate * grad_two[0].astype(F32)).astype(BF16)
-    down_grad[0] = rows_grad
-    down_sum[0] = jnp.sum(rows_grad.astype(F32), axis=0, keepdims=True)
-    before = mm(mixed[0], up[...], NT) + up_bias[...]
-    square = before * before
-    tanh = jnp.tanh(GELU_A * (before + GELU_B * (before * square)))
-    half = 0.5 * (1.0 + tanh)
-    act = (before * half).astype(BF16)
-    active[0] = act
-    slope = half + 0.5 * before * (1.0 - tanh * tanh) * (GELU_A * (1.0 + 3.0 * GELU_B * square))
-    inner = (mm(rows_grad, down[...], NT) * slope).astype(BF16)
-    before_grad[0] = inner
-    up_sum[0] = jnp.sum(inner.astype(F32), axis=0, keepdims=True)
-    mixed_grad[0] = mm(inner, up[...]).astype(BF16)
-    branch[0] = mm(act, down[...]).astype(BF16)
+def down_back_body(grad_two, mod, keep, down, down_grad, active_grad, down_sum):
+    gate = live_rows(keep, grad_two.shape[1]) * mod_row(mod, 5)
+    rows = (gate * grad_two[0].astype(F32)).astype(BF16)
+    down_grad[0] = rows
+    down_sum[0] = jnp.sum(rows.astype(F32), axis=0, keepdims=True)
+    active_grad[0] = mm(rows, down[...], NT)
+
+
+def forward_body(mixed, active_grad, up, up_bias, active, before_grad, mixed_grad, up_sum):
+    units = up.shape[0]
+    step = 384 if units % 384 == 0 else units
+    rows = mixed[0]
+    total = None
+    for start in range(0, units, step):
+        at = slice(start, start + step)
+        before = mm(rows, up[at, :], NT) + up_bias[:, at]
+        square = before * before
+        tanh = jnp.tanh(GELU_A * (before + GELU_B * (before * square)))
+        half = 0.5 * (1.0 + tanh)
+        active[0, :, at] = (before * half).astype(BF16)
+        slope = half + 0.5 * before * (1.0 - tanh * tanh) * (
+            GELU_A * (1.0 + 3.0 * GELU_B * square)
+        )
+        inner = (active_grad[0, :, at] * slope).astype(BF16)
+        before_grad[0, :, at] = inner
+        up_sum[0, :, at] = jnp.sum(inner.astype(F32), axis=0, keepdims=True)
+        piece = mm(inner, up[at, :])
+        total = piece if total is None else total + piece
+    mixed_grad[0] = total.astype(BF16)
+
+
+def branch_body(active, grad_two, keep, down, bias, branch, gate_grad):
+    rows = mm(active[0], down[...])
+    branch[0] = rows.astype(BF16)
+    grad = live_rows(keep, grad_two.shape[1]) * grad_two[0].astype(F32)
+    gate_grad[0] = jnp.sum(grad * (rows + bias[...]), axis=0, keepdims=True)
 
 
 def middle_body(branch, out_bias, routed, mod, keep, hidden, mixed):
@@ -209,12 +241,9 @@
     return jnp.where(taken, mm(hot.astype(BF16), rows.astype(BF16)), base.astype(F32)).astype(BF16)
 
 
-def out_body(branch, hidden, down_bias, mod, keep, grad_two, picks, tokens, layer_out, gate_grad):
-    slots = hidden.shape[1]
-    live = live_rows(keep, slots)
+def out_body(branch, hidden, down_bias, mod, keep, picks, tokens, layer_out):
     branch_two = branch[0].astype(F32) + down_bias[...]
-    gate_grad[0] = jnp.sum(live * grad_two[0].astype(F32) * branch_two, axis=0, keepdims=True)
-    rows = hidden[0] + live * mod_row(mod, 5) * branch_two
+    rows = hidden[0] + live_rows(keep, hidden.shape[1]) * mod_row(mod, 5) * branch_two
     layer_out[0] = place(picks[0], tokens[0], rows)
 
 
@@ -256,6 +285,19 @@
 
 def after(value, *others):
     return lax.optimization_barrier((value,) + others)[0]
+
+
+def halve_all(parts, level):
+    ways = orders()
+    flights = [halve(part, way[level]) for part, way in zip(parts, ways)]
+    return [add_low(own, got) for own, got in lax.optimization_barrier(flights)]
+
+
+def join_all(parts, level):
+    ways = orders()
+    flights = [double(part, way[level]) for part, way in zip(parts, ways)]
+    flights = lax.optimization_barrier(flights)
+    return [join(own, got, way[level]) for (own, got), way in zip(flights, ways)]
 
 
 def orders():
@@ -281,15 +323,6 @@
         to = (here + step) % count
         total = total + shift(lax.dynamic_index_in_dim(parts, to, 0, keepdims=False), step)
     return total
-
-
-def sum_pair(parts):
-    pairs = list(zip(parts, orders()))
-    for level in range(len(dp_bits())):
-        pairs = [(add_low(*halve(part, bits[level])), bits) for part, bits in pairs]
-    for level in reversed(range(len(dp_bits()))):
-        pairs = [(join(*double(part, bits[level]), bits[level]), bits) for part, bits in pairs]
-    return [part for part, _ in pairs]
 
 
 def all_rows(rows):
@@ -367,83 +400,91 @@
     )
     group_mixed = all_rows(mixed_two)
     unit_shape = (group, slots, hidden_units)
-    active, before_grad, down_grad, branch, mixed_grad, up_sum, down_sum = call(
+    down_grad, active_grad, down_sum = call(
+        down_back_body, group,
+        [(group_two, True), (modulation, True), (keep, True), (down_weight, False)],
+        [(group_shape, BF16), (unit_shape, F32), ((group, 1, width), F32)],
+    )
+    active, before_grad, mixed_grad, up_sum = call(
         forward_body, group,
         [
-            (group_mixed, True), (group_two, True), (modulation, True), (keep, True),
-            (up_weight, False), (up_bias.astype(F32)[None], False), (down_weight, False),
-        ],
-        [
-            (unit_shape, BF16), (unit_shape, BF16), (group_shape, BF16), (group_shape, BF16),
-            (group_shape, BF16), ((group, 1, hidden_units), F32), ((group, 1, width), F32),
+            (group_mixed, True), (active_grad, True), (up_weight, False),
+            (up_bias.astype(F32)[None], False),
+        ],
+        [
+            (unit_shape, BF16), (unit_shape, BF16), (group_shape, BF16),
+            ((group, 1, hidden_units), F32),
         ],
     )
     mixed_two_grad = own_sum(mixed_grad)
-
     flat = (group * slots, hidden_units)
     wide = (group * slots, width)
     up_part = mm(before_grad.reshape(flat), group_mixed.reshape(wide), TN).astype(BF16)
     down_part = mm(active.reshape(flat), down_grad.reshape(wide), TN).astype(BF16)
     levels = len(dp_bits())
-    ways = orders()
-    sums = [add_low(*halve(part, way[0])) for part, way in zip((up_part, down_part), ways)]
-    flights = [halve(part, way[1]) for part, way in zip(sums, ways)]
+    sums = halve_all((up_part, down_part), 0)
+    branch, gate_grad = call(
+        branch_body, group,
+        [
+            (active, True), (group_two, True), (after(keep, *sums), True), (down_weight, False),
+            (jnp.where(here == 0, down_bias_row, 0.0), False),
+        ],
+        [(group_shape, BF16), ((group, 1, width), F32)],
+    )
+    sums = halve_all(sums, 1)
 
     grad_one, branch_grad, middle_stats = call(
         middle_back_body, images,
         [
             (mixed_two_grad, True), (hidden_one, True), (branch_one, True), (out_bias_row, False),
-            (grad_two, True), (own_mod, True), (own_keep, True),
+            (grad_two, True), (own_mod, True), (after(own_keep, gate_grad, *sums), True),
         ],
         [(rows_shape, F32), (rows_shape, BF16), ((images, 3, width), F32)],
     )
     group_grad = all_rows(branch_grad)
-    sums = [add_low(after(own, branch_grad), got) for own, got in flights]
+    branch_two = own_sum(branch)
     for level in range(2, levels):
-        sums = [add_low(*halve(part, way[level])) for part, way in zip(sums, ways)]
-    for level in reversed(range(2, levels)):
-        sums = [join(*double(part, way[level]), way[level]) for part, way in zip(sums, ways)]
-    flights = [double(part, way[1]) for part, way in zip(sums, ways)]
-    branch_two = own_sum(branch)
-    layer_out, gate_grad = call(
+        sums = halve_all(sums, level)
+    for level in reversed(range(1, levels)):
+        sums = join_all(sums, level)
+    up_weight_grad, down_weight_grad = [part.astype(F32) for part in join_all(sums, 0)]
+    mixed_grad, attend_stats, bias_sums, part = call(
+        functools.partial(attend_back_body, head_dim), group,
+        [
+            (group_grad, True), (qkv, True), (group_routed, True), (mixed_one, True),
+            (attended, True), (after(keep, up_weight_grad, down_weight_grad), True),
+            (qkv_weight, False), (out_weight, False),
+        ],
+        [
+            (group_shape, BF16), ((group, 3, width), F32), ((group, 2, cols), F32),
+            ((4, cols, width), BF16),
+        ],
+        fixed=1,
+        scratch=[pltpu.VMEM((4, cols, width), F32)],
+    )
+    (layer_out,) = call(
         out_body, images,
         [
             (branch_two, True), (hidden_one, True), (down_bias_row, False), (own_mod, True),
-            (own_keep, True), (grad_two, True), (picks_row, True), (image_tokens, True),
-        ],
-        [((images, patches, width), BF16), ((images, 1, width), F32)],
-    )
-    qkv_grad, mixed_grad, attend_stats, bias_sums = call(
-        functools.partial(attend_back_body, head_dim), group,
-        [
-            (group_grad, True), (qkv, True), (group_routed, True), (keep, True),
-            (qkv_weight, False), (out_weight, False),
-        ],
-        [
-            ((group, 3, slots, cols), BF16), (group_shape, BF16), ((group, 3, width), F32),
-            ((group, 2, cols), F32),
-        ],
+            (after(own_keep, attend_stats), True), (picks_row, True), (image_tokens, True),
+        ],
+        [((images, patches, width), BF16)],
     )
     mixed_one_grad = own_sum(mixed_grad)
-    sums = [join(after(own, attend_stats), got, way[1]) for (own, got), way in zip(flights, ways)]
-    up_weight_grad, down_weight_grad = [
-        join(*double(part, way[0]), way[0]) for part, way in zip(sums, ways)
-    ]
-
-    qkv_part = jnp.einsum(
-        "gtsc,gsd->tcd", qkv_grad, mixed_one, preferred_element_type=F32
-    ).reshape(3 * cols, width)
-    out_part = mm(attended.reshape(-1, cols), group_grad.reshape(wide), TN)
-    part = jnp.concatenate([qkv_part.astype(BF16), out_part.astype(BF16)], axis=0)
-    part = jnp.concatenate(sum_pair((part[: 2 * cols], part[2 * cols :])), axis=0)
+    part = part.reshape(2, 2 * cols, width)
+    firsts = [part[0], part[1]]
+    for level in range(levels):
+        firsts = halve_all(firsts, level)
+    for level in reversed(range(levels)):
+        firsts = join_all(firsts, level)
+    part = jnp.concatenate(firsts, axis=0).astype(F32)
     qkv_weight_grad = part[: 3 * cols].reshape(3, cols, width)
     out_weight_grad = part[3 * cols :]
 
-    own_rows = jnp.concatenate([middle_stats, gate_grad], axis=1)
     placed = lax.dynamic_update_slice(
-        jnp.zeros((group, 4, width), F32), own_rows, (here * images, 0, 0)
-    )
-    mod_grad = jnp.concatenate([attend_stats[:, :2], placed], axis=1)
+        jnp.zeros((group, 3, width), F32), middle_stats, (here * images, 0, 0)
+    )
+    mod_grad = jnp.concatenate([attend_stats[:, :2], placed, gate_grad], axis=1)
     each = 6 * width // (groups * members)
     mod_grad = mod_grad.reshape(group, groups, members, each)
     mod_grad = small_scatter_sum(mod_grad.transpose(2, 0, 1, 3)).astype(BF16)
@@ -484,13 +525,13 @@
         tokens_grad.reshape(images * patches, width),
         ada_weight_grad,
         ada_bias_grad,
-        qkv_weight_grad.astype(F32),
+        qkv_weight_grad,
         qv_sum.reshape(2, cols),
-        out_weight_grad.astype(F32),
+        out_weight_grad,
         out_sum,
-        up_weight_grad.astype(F32),
+        up_weight_grad,
         up_bias_grad,
-        down_weight_grad.astype(F32),
+        down_weight_grad,
         down_bias_grad,
     )
 

time: 430 us -> 436 us (1.014)
  Pallas kernels: 62.4 us -> 73.5 us
  other arithmetic: 32 us -> 21 us
  waiting for transfers between devices: 237 us -> 242 us
  matrix products: 22.5 us -> 17.7 us
    ppermute x12, waiting for transfers between devices: 11.7 us -> 41.2 us  [halve(): return (own, lax.ppermute(other, 'dp', partner(bit)))]
    reduce_scatter x4, waiting for transfers between devices: 82.7 us -> 55.4 us  [own_sum(): return lax.psum_scatter(rows, 'mp', scatter_dimension=0, tiled=True)]
    pallas_call x8 -> x9, Pallas kernels: 62.4 us -> 73.5 us  [call(): pl.pallas_call(body, grid=(grid,), in_specs=[block(a.shape) if step else...]
    ppermute x12, waiting for transfers between devices: 13.8 us -> 23.5 us  [double(): return (part, lax.ppermute(part, 'dp', partner(bit)))]
    convert_element_type x4 -> x3, other arithmetic: 12.6 us -> 9.75 us  [the longest x2 9.4 us: per_device(): part.astype(F32)]
    dot_general x5 -> x4, matrix products: 18.4 us -> 17.7 us  [mm(): lax.dot_general(left, right, (dims, ((), ())), preferred_element_type=F32)]
  transfers between devices with their start and end apart: 38 -> 38, of which waited for: 18 -> 26; matrix products, arithmetic and copies ran while one was open for 16% -> 10% of each run, Pallas kernels for 6% -> 5%
where the time goes in v3:
time: 436 us; the launch traced here: 435 us
  waiting for transfers between devices  242 us (56%)
  Pallas kernels  73.5 us (17%)
  starting transfers between devices  34.7 us (8%)
  local copies, waits for them, and re-layouts  21.1 us (5%)
  other arithmetic  21 us (5%)
  matrix products  17.7 us (4%)
  between operations  15.4 us (4%)
  blocking collectives  9.71 us (2%)
    all_gather x4, waiting for transfers between devices, all_rows(): return lax.all_gather(rows, 'mp', axis=0, tiled=True)  120 us
    pallas_call x9, Pallas kernels, call(): pl.pallas_call(body, grid=(grid,), in_specs=[block(a.shape) if step else...  73.5 us
    reduce_scatter x4, waiting for transfers between devices, own_sum(): return lax.psum_scatter(rows, 'mp', scatter_dimension=0, tiled=True)  55.4 us
    ppermute x12, waiting for transfers between devices, halve(): return (own, lax.ppermute(other, 'dp', partner(bit)))  41.2 us
    ppermute x12, waiting for transfers between devices, double(): return (part, lax.ppermute(part, 'dp', partner(bit)))  23.5 us
    dot_general x4, matrix products, mm(): lax.dot_general(left, right, (dims, ((), ())), preferred_element_type=F32)  17.7 us
    ppermute x6, starting transfers between devices, shift(): lax.ppermute(value, 'mp', [(i, (i + step) % count) for i in range(count)])  12.2 us
    ppermute x12, starting transfers between devices, halve(): return (own, lax.ppermute(other, 'dp', partner(bit)))  11.6 us
  transfers between devices with their start and end apart: 38, of which 26 were waited for; matrix products, arithmetic and copies ran while one was open for 10% of the time, Pallas kernels for 5%

profile of v3, /device:TPU:0, one launch (start us, length us, event | category | flops | bytes accessed | tf_op | source)
XLA Modules:
  0.0 435.2 jit_solution(2938786137199866461)
XLA Ops:
  9.3 2.5 shard_map.238
  12.6 4.1 collective-permute-start.1
  22.8 9.8 %convolution_add_fusion = f32[4,6912]{1,0:T(4,128)S(1)} fusion(bf16[6912,1152]{1,0:T(8,128)(2,1)} %param.20, f32[6912]{0:T(1024)S(1)} %convert_element_type.197, bf16[4,1280]{1,0:T(4,128)(2,1)S(1)} %broadcast_select_fusion), kind=kOutput, calls=%fused_computation.3 | convolution fusion | flops 63756288 | bytes 16073728 | tf_op jit(solution)/shard_map/dot_general | solution.py:36
  33.9 21.1 %all-gather.5.cloned.1.call-done.routed = bf16[4,192,1152]{2,1,0:T(8,128)(2,1)} async-done(((bf16[1,192,1152]{2,1,0:T(8,128)(2,1)}), bf16[4,192,1152]{2,1,0:T(8,128)(2,1)}) %all-gather.5.cloned.1.call-update) | async-done | bytes 1769488 | tf_op jit(solution)/shard_map/all_gather | solution.py:329
  55.0 12.8 %shard_map.239 = (bf16[4,192,1152]{2,1,0:T(8,128)(2,1)}, bf16[4,3,192,288]{3,2,1,0:T(8,128)(2,1)}, bf16[4,192,288]{2,1,0:T(8,128)(2,1)}, bf16[4,192,1152]{2,1,0:T(8,128)(2,1)}) custom-call(bf16[4,192,1152]{2,1,0:T(8,128)(2,1)} %all-gather.5.cloned.1.call-done.routed, f32[4,6,1152]{2,1,0:T(8,128)} %reshape.215.mod, f32[4,1,128]{2,1,0:T(1,128)} %bitcast.139, ...), custom_call_target="tpu_custom_call" | custom-call | tf_op jit(solution)/shard_map/pallas_call | solution.py:55
  70.6 34.7 %reduce-scatter.5.cloned.1.call-done.branch = bf16[1,192,1152]{2,1,0:T(8,128)(2,1)} async-done(((bf16[4,192,1152]{2,1,0:T(8,128)(2,1)}), bf16[1,192,1152]{2,1,0:T(8,128)(2,1)}) %reduce-scatter.5.cloned.1.call-update) | async-done | bytes 442384 | tf_op jit(solution)/shard_map/reduce_scatter | solution.py:333
  105.8 2.5 shard_map.240
  109.2 37.5 %all-gather.9.cloned.1.call-done.grad_two = bf16[4,192,1152]{2,1,0:T(8,128)(2,1)} async-done(((bf16[1,192,1152]{2,1,0:T(8,128)(2,1)}), bf16[4,192,1152]{2,1,0:T(8,128)(2,1)}) %all-gather.9.cloned.1.call-update) | async-done | bytes 1769488 | tf_op jit(solution)/shard_map/all_gather | solution.py:329
  146.7 7.4 %shard_map.241 = (bf16[4,192,1152]{2,1,0:T(8,128)(2,1)}, f32[4,192,1152]{2,1,0:T(8,128)}, f32[4,1,1152]{2,1,0:T(1,128)}) custom-call(bf16[4,192,1152]{2,1,0:T(8,128)(2,1)} %all-gather.9.cloned.1.call-done.grad_two, f32[4,6,1152]{2,1,0:T(8,128)} %reshape.215.mod, f32[4,1,128]{2,1,0:T(1,128)} %bitcast.140, bf16[1152,1152]{1,0:T(8,128)(2,1)} %down.3), custom_call_target="tpu_custom_call" | custom-call | tf_op jit(solution)/shard_map/pallas_call | solution.py:55
  154.2 33.7 %all-gather.7.cloned.1.call-done.mixed = bf16[4,192,1152]{2,1,0:T(8,128)(2,1)} async-done(((bf16[1,192,1152]{2,1,0:T(8,128)(2,1)}), bf16[4,192,1152]{2,1,0:T(8,128)(2,1)}) %all-gather.7.cloned.1.call-update) | async-done | bytes 1769488 | tf_op jit(solution)/shard_map/all_gather | solution.py:329
  187.9 12.5 %shard_map.242 = (bf16[4,192,1152]{2,1,0:T(8,128)(2,1)}, bf16[4,192,1152]{2,1,0:T(8,128)(2,1)}, bf16[4,192,1152]{2,1,0:T(8,128)(2,1)}, f32[4,1,1152]{2,1,0:T(1,128)}) custom-call(bf16[4,192,1152]{2,1,0:T(8,128)(2,1)} %all-gather.7.cloned.1.call-done.mixed, f32[4,192,1152]{2,1,0:T(8,128)} %get-tuple-element.93.active_grad, bf16[1152,1152]{1,0:T(8,128)(2,1)} %up.1, ...), custom_call_target="tpu_custom_call" | custom-call | tf_op jit(solution)/shard_map/pallas_call | solution.py:55
  200.4 4.1 fusion.1
  204.5 2.5 fusion
  210.1 2.9 collective-permute-done.4
  220.6 13.8 %collective-permute-done.5 = bf16[288,1152]{1,0:T(8,128)(2,1)S(1)} collective-permute-done((bf16[288,1152]{1,0:T(8,128)(2,1)S(1)}, bf16[288,1152]{1,0:T(8,128)(2,1)S(1)}, u32[]{:S(2)}, u32[]{:S(2)}) %collective-permute-start.5) | collective-permute-done | bytes 663584 | tf_op jit(solution)/shard_map/ppermute | solution.py:270
  238.7 6.0 %collective-permute-done.8 = bf16[144,1152]{1,0:T(8,128)(2,1)S(1)} collective-permute-done((bf16[144,1152]{1,0:T(8,128)(2,1)S(1)}, bf16[144,1152]{1,0:T(8,128)(2,1)S(1)}, u32[]{:S(2)}, u32[]{:S(2)}) %collective-permute-start.8) | collective-permute-done | bytes 331808 | tf_op jit(solution)/shard_map/ppermute | solution.py:270
  248.6 4.5 %collective-permute-done.10 = bf16[144,1152]{1,0:T(8,128)(2,1)S(1)} collective-permute-done((bf16[144,1152]{1,0:T(8,128)(2,1)S(1)}, bf16[144,1152]{1,0:T(8,128)(2,1)S(1)}, u32[]{:S(2)}, u32[]{:S(2)}) %collective-permute-start.10) | collective-permute-done | bytes 331808 | tf_op jit(solution)/shard_map/ppermute | solution.py:278
  257.3 11.4 %collective-permute-done.12 = bf16[288,1152]{1,0:T(8,128)(2,1)S(1)} collective-permute-done((bf16[288,1152]{1,0:T(8,128)(2,1)S(1)}, bf16[288,1152]{1,0:T(8,128)(2,1)S(1)}, u32[]{:S(2)}, u32[]{:S(2)}) %collective-permute-start.12) | collective-permute-done | bytes 663584 | tf_op jit(solution)/shard_map/ppermute | solution.py:278
  272.0 6.9 %shard_map.243 = (bf16[4,192,1152]{2,1,0:T(8,128)(2,1)}, f32[4,1,1152]{2,1,0:T(1,128)}) custom-call(bf16[4,192,1152]{2,1,0:T(8,128)(2,1)} %get-tuple-element.94.active, bf16[4,192,1152]{2,1,0:T(8,128)(2,1)} %all-gather.9.cloned.1.call-done.grad_two, f32[4,1,128]{2,1,0:T(1,128)} %bitcast.141, bf16[1152,1152]{1,0:T(8,128)(2,1)} %down.3, f32[1,1152]{1,0:T(1,128)} %select_n.206.bias), custom_call_target="tpu_custom_call" | custom-call | tf_op jit(solution)/shard_map/pallas_call | solution.py:55
  279.5 3.2 shard_map.247
  282.8 4.7 %fusion.2 = f32[1152,1152]{1,0:T(8,128)} fusion(bf16[576,1152]{1,0:T(8,128)(2,1)} %collective-permute-done.13, bf16[576,1152]{1,0:T(8,128)(2,1)S(1)} %maximum_select_fusion.2, pred[]{:T(512)S(6)} %eq.14), kind=kLoop, calls=%fused_computation.7 | loop fusion | flops 13271040 | bytes 7962625 | tf_op jit(solution)/shard_map/convert_element_type | solution.py:450
  287.5 4.7 %fusion.3 = f32[1152,1152]{1,0:T(8,128)} fusion(bf16[576,1152]{1,0:T(8,128)(2,1)} %collective-permute-done.14, bf16[576,1152]{1,0:T(8,128)(2,1)S(1)} %maximum_select_fusion.3, pred[]{:T(512)S(6)} %eq.14), kind=kLoop, calls=%fused_computation.9 | loop fusion | flops 13271040 | bytes 7962625 | tf_op jit(solution)/shard_map/convert_element_type | solution.py:450
  292.2 28.0 %all-gather.11.cloned.1.call-done.grad = bf16[4,192,1152]{2,1,0:T(8,128)(2,1)} async-done(((bf16[1,192,1152]{2,1,0:T(8,128)(2,1)}), bf16[4,192,1152]{2,1,0:T(8,128)(2,1)}) %all-gather.11.cloned.1.call-update) | async-done | bytes 1769488 | tf_op jit(solution)/shard_map/all_gather | solution.py:329
  320.2 22.7 %shard_map.244 = (bf16[4,192,1152]{2,1,0:T(8,128)(2,1)}, f32[4,3,1152]{2,1,0:T(4,128)}, f32[4,2,288]{2,1,0:T(2,128)}, bf16[4,288,1152]{2,1,0:T(8,128)(2,1)}) custom-call(bf16[4,192,1152]{2,1,0:T(8,128)(2,1)} %all-gather.11.cloned.1.call-done.grad, bf16[4,3,192,288]{3,2,1,0:T(8,128)(2,1)} %get-tuple-element.112.qkv, ...), custom_call_target="tpu_custom_call" | custom-call | tf_op jit(solution)/shard_map/pallas_call | solution.py:55
  353.0 6.6 %collective-permute-done.20 = bf16[144,1152]{1,0:T(8,128)(2,1)S(1)} collective-permute-done((bf16[144,1152]{1,0:T(8,128)(2,1)S(1)}, bf16[144,1152]{1,0:T(8,128)(2,1)S(1)}, u32[]{:S(2)}, u32[]{:S(2)}) %collective-permute-start.20) | collective-permute-done | bytes 331808 | tf_op jit(solution)/shard_map/ppermute | solution.py:270
  364.1 2.5 collective-permute-done.22
  369.8 3.9 collective-permute-done.25
  381.8 2.4 reduce-scatter.7.cloned.1.call-done.branch
  384.2 2.8 shard_map.245
  388.2 9.7 %all_gather.19 = bf16[8,128,128]{2,1,0:T(8,128)(2,1)S(1)} all-gather(bf16[1,128,128]{2,1,0:T(8,128)(2,1)S(1)} %pad_bitcast_fusion), channel_id=1, replica_groups=mesh['dp'=8,'mp'=4] {'dp'}, dimensions={0}, use_global_device_ids=true | all-gather | bytes 294912 | tf_op jit(solution)/shard_map/all_gather | solution.py:502
  406.7 18.3 %reduce-scatter.11.cloned.1.call-done.mixed_grad = bf16[1,192,1152]{2,1,0:T(8,128)(2,1)} async-done(((bf16[4,192,1152]{2,1,0:T(8,128)(2,1)}), bf16[1,192,1152]{2,1,0:T(8,128)(2,1)}) %reduce-scatter.11.cloned.1.call-update) | async-done | bytes 442384 | tf_op jit(solution)/shard_map/reduce_scatter | solution.py:333
  425.0 3.3 shard_map.246
  (188 shorter events, 76.1 us)
Async XLA Ops:
  7.2 47.8 %all-gather.5.cloned.1.call-start = ((), (), s32[]{:S(2)}) async-start(), calls=%async_computation.4 | async-start | bytes 2211840 | tf_op jit(solution)/shard_map/all_gather | solution.py:329
  11.9 93.5 %reduce-scatter.5.cloned.1.call-start = ((), (), s32[]{:S(2)}) async-start(), calls=%async_computation.5 | async-start | bytes 2211840 | tf_op jit(solution)/shard_map/reduce_scatter | solution.py:333
  12.6 8.6 %collective-permute-start.1 = (bf16[1,1280]{1,0:T(2,128)(2,1)S(1)}, bf16[1,1280]{1,0:T(2,128)(2,1)S(1)}, u32[]{:S(2)}, u32[]{:S(2)}) collective-permute-start(bf16[1,1280]{1,0:T(2,128)(2,1)S(1)} %get-tuple-element.206), channel_id=1, source_target_pairs={{0,2},{1,3},{2,0},{3,1},{4,6},{5,7},{6,4},{7,5},{8,10},{9,11},{10,... | collective-permute-start | bytes 7688 | tf_op jit(solution)/shard_map/ppermute | solution.py:310
  16.7 5.4 %collective-permute-start = (bf16[1,1280]{1,0:T(2,128)(2,1)S(1)}, bf16[1,1280]{1,0:T(2,128)(2,1)S(1)}, u32[]{:S(2)}, u32[]{:S(2)}) collective-permute-start(bf16[1,1280]{1,0:T(2,128)(2,1)S(1)} %get-tuple-element.206), channel_id=1, source_target_pairs={{0,1},{1,2},{2,3},{3,0},{4,5},{5,6},{6,7},{7,4},{8,9},{9,10},{10,1... | collective-permute-start | bytes 7688 | tf_op jit(solution)/shard_map/ppermute | solution.py:310
  67.9 78.9 %all-gather.9.cloned.1.call-start = ((), (), s32[]{:S(2)}) async-start(), calls=%async_computation.7 | async-start | bytes 2211840 | tf_op jit(solution)/shard_map/all_gather | solution.py:329
  68.6 119.3 %all-gather.7.cloned.1.call-start = ((), (), s32[]{:S(2)}) async-start(), calls=%async_computation.6 | async-start | bytes 2211840 | tf_op jit(solution)/shard_map/all_gather | solution.py:329
  108.4 170.5 %reduce-scatter.9.cloned.1.call-start = ((), (), s32[]{:S(2)}) async-start(), calls=%async_computation.9 | async-start | bytes 2211840 | tf_op jit(solution)/shard_map/reduce_scatter | solution.py:333
  217.4 17.0 %collective-permute-start.5 = (bf16[288,1152]{1,0:T(8,128)(2,1)S(1)}, bf16[288,1152]{1,0:T(8,128)(2,1)S(1)}, u32[]{:S(2)}, u32[]{:S(2)}) collective-permute-start(bf16[288,1152]{1,0:T(8,128)(2,1)S(1)} %get-tuple-element.187), channel_id=1, source_target_pairs={{0,8},{4,12},{8,0},{12,4},{16,24},{20,28},{24,16},{28,20},{1,9},{5... | collective-permute-start | bytes 1990664 | tf_op jit(solution)/shard_map/ppermute | solution.py:270
  219.0 16.7 %collective-permute-start.6 = (bf16[288,1152]{1,0:T(8,128)(2,1)S(1)}, bf16[288,1152]{1,0:T(8,128)(2,1)S(1)}, u32[]{:S(2)}, u32[]{:S(2)}) collective-permute-start(bf16[288,1152]{1,0:T(8,128)(2,1)S(1)} %get-tuple-element.185), channel_id=1, source_target_pairs={{0,16},{4,20},{8,24},{12,28},{16,0},{20,4},{24,8},{28,12},{1,17},{... | collective-permute-start | bytes 1990664 | tf_op jit(solution)/shard_map/ppermute | solution.py:270
  236.0 8.8 %collective-permute-start.8 = (bf16[144,1152]{1,0:T(8,128)(2,1)S(1)}, bf16[144,1152]{1,0:T(8,128)(2,1)S(1)}, u32[]{:S(2)}, u32[]{:S(2)}) collective-permute-start(bf16[144,1152]{1,0:T(8,128)(2,1)S(1)} %get-tuple-element.193), channel_id=1, source_target_pairs={{0,8},{4,12},{8,0},{12,4},{16,24},{20,28},{24,16},{28,20},{1,9},{5... | collective-permute-start | bytes 995336 | tf_op jit(solution)/shard_map/ppermute | solution.py:270
  236.9 8.5 %collective-permute-start.7 = (bf16[144,1152]{1,0:T(8,128)(2,1)S(1)}, bf16[144,1152]{1,0:T(8,128)(2,1)S(1)}, u32[]{:S(2)}, u32[]{:S(2)}) collective-permute-start(bf16[144,1152]{1,0:T(8,128)(2,1)S(1)} %get-tuple-element.195), channel_id=1, source_target_pairs={{0,16},{4,20},{8,24},{12,28},{16,0},{20,4},{24,8},{28,12},{1,17},{... | collective-permute-start | bytes 995336 | tf_op jit(solution)/shard_map/ppermute | solution.py:270
  238.5 81.7 %all-gather.11.cloned.1.call-start = ((), (), s32[]{:S(2)}) async-start(), calls=%async_computation.10 | async-start | bytes 2211840 | tf_op jit(solution)/shard_map/all_gather | solution.py:329
  245.5 7.6 %collective-permute-start.10 = (bf16[144,1152]{1,0:T(8,128)(2,1)S(1)}, bf16[144,1152]{1,0:T(8,128)(2,1)S(1)}, u32[]{:S(2)}, u32[]{:S(2)}) collective-permute-start(bf16[144,1152]{1,0:T(8,128)(2,1)S(1)} %add_convert_fusion.8), channel_id=1, source_target_pairs={{0,8},{4,12},{8,0},{12,4},{16,24},{20,28},{24,16},{28,20},{1,9},{5... | collective-permute-start | bytes 995336 | tf_op jit(solution)/shard_map/ppermute | solution.py:278
  247.1 7.7 %collective-permute-start.9 = (bf16[144,1152]{1,0:T(8,128)(2,1)S(1)}, bf16[144,1152]{1,0:T(8,128)(2,1)S(1)}, u32[]{:S(2)}, u32[]{:S(2)}) collective-permute-start(bf16[144,1152]{1,0:T(8,128)(2,1)S(1)} %add_convert_fusion.9), channel_id=1, source_target_pairs={{0,16},{4,20},{8,24},{12,28},{16,0},{20,4},{24,8},{28,12},{1,17},{... | collective-permute-start | bytes 995336 | tf_op jit(solution)/shard_map/ppermute | solution.py:278
  254.9 13.7 %collective-permute-start.12 = (bf16[288,1152]{1,0:T(8,128)(2,1)S(1)}, bf16[288,1152]{1,0:T(8,128)(2,1)S(1)}, u32[]{:S(2)}, u32[]{:S(2)}) collective-permute-start(bf16[288,1152]{1,0:T(8,128)(2,1)S(1)} %maximum_select_fusion.7), channel_id=1, source_target_pairs={{0,16},{4,20},{8,24},{12,28},{16,0},{20,4},{24,8},{28,12},{1,17},{... | collective-permute-start | bytes 1990664 | tf_op jit(solution)/shard_map/ppermute | solution.py:278
  256.6 13.1 %collective-permute-start.11 = (bf16[288,1152]{1,0:T(8,128)(2,1)S(1)}, bf16[288,1152]{1,0:T(8,128)(2,1)S(1)}, u32[]{:S(2)}, u32[]{:S(2)}) collective-permute-start(bf16[288,1152]{1,0:T(8,128)(2,1)S(1)} %maximum_select_fusion.6), channel_id=1, source_target_pairs={{0,8},{4,12},{8,0},{12,4},{16,24},{20,28},{24,16},{28,20},{1,9},{5... | collective-permute-start | bytes 1990664 | tf_op jit(solution)/shard_map/ppermute | solution.py:278
  270.2 12.6 %collective-permute-start.14 = (bf16[576,1152]{1,0:T(8,128)(2,1)S(1)}, bf16[576,1152]{1,0:T(8,128)(2,1)}, u32[]{:S(2)}, u32[]{:S(2)}) collective-permute-start(bf16[576,1152]{1,0:T(8,128)(2,1)S(1)} %maximum_select_fusion.3), channel_id=1, source_target_pairs={{0,4},{4,0},{8,12},{12,8},{16,20},{20,16},{24,28},{28,24},{1,5},{5... | collective-permute-start | bytes 3981320 | tf_op jit(solution)/shard_map/ppermute | solution.py:278
  270.8 12.0 %collective-permute-start.13 = (bf16[576,1152]{1,0:T(8,128)(2,1)S(1)}, bf16[576,1152]{1,0:T(8,128)(2,1)}, u32[]{:S(2)}, u32[]{:S(2)}) collective-permute-start(bf16[576,1152]{1,0:T(8,128)(2,1)S(1)} %maximum_select_fusion.2), channel_id=1, source_target_pairs={{0,4},{4,0},{8,12},{12,8},{16,20},{20,16},{24,28},{28,24},{1,5},{5... | collective-permute-start | bytes 3981320 | tf_op jit(solution)/shard_map/ppermute | solution.py:278
  282.7 101.4 %reduce-scatter.7.cloned.1.call-start = ((), (), s32[]{:S(2)}) async-start(), calls=%async_computation.8 | async-start | bytes 2211840 | tf_op jit(solution)/shard_map/reduce_scatter | solution.py:333
  345.6 79.4 %reduce-scatter.11.cloned.1.call-start = ((), (), s32[]{:S(2)}) async-start(), calls=%async_computation.11 | async-start | bytes 2211840 | tf_op jit(solution)/shard_map/reduce_scatter | solution.py:333
  349.6 9.9 %collective-permute-start.20 = (bf16[144,1152]{1,0:T(8,128)(2,1)S(1)}, bf16[144,1152]{1,0:T(8,128)(2,1)S(1)}, u32[]{:S(2)}, u32[]{:S(2)}) collective-permute-start(bf16[144,1152]{1,0:T(8,128)(2,1)S(1)} %get-tuple-element.191), channel_id=1, source_target_pairs={{0,8},{4,12},{8,0},{12,4},{16,24},{20,28},{24,16},{28,20},{1,9},{5... | collective-permute-start | bytes 995336 | tf_op jit(solution)/shard_map/ppermute | solution.py:270
  351.4 9.6 %collective-permute-start.21 = (bf16[144,1152]{1,0:T(8,128)(2,1)S(1)}, bf16[144,1152]{1,0:T(8,128)(2,1)S(1)}, u32[]{:S(2)}, u32[]{:S(2)}) collective-permute-start(bf16[144,1152]{1,0:T(8,128)(2,1)S(1)} %get-tuple-element.189), channel_id=1, source_target_pairs={{0,16},{4,20},{8,24},{12,28},{16,0},{20,4},{24,8},{28,12},{1,17},{... | collective-permute-start | bytes 995336 | tf_op jit(solution)/shard_map/ppermute | solution.py:270
  362.9 5.4 %collective-permute-start.23 = (bf16[72,1152]{1,0:T(8,128)(2,1)S(1)}, bf16[72,1152]{1,0:T(8,128)(2,1)S(1)}, u32[]{:S(2)}, u32[]{:S(2)}) collective-permute-start(bf16[72,1152]{1,0:T(8,128)(2,1)S(1)} %get-tuple-element.197), channel_id=1, source_target_pairs={{0,8},{4,12},{8,0},{12,4},{16,24},{20,28},{24,16},{28,20},{1,9},{5... | collective-permute-start | bytes 497672 | tf_op jit(solution)/shard_map/ppermute | solution.py:270
  368.4 5.4 %collective-permute-start.25 = (bf16[72,1152]{1,0:T(8,128)(2,1)S(1)}, bf16[72,1152]{1,0:T(8,128)(2,1)S(1)}, u32[]{:S(2)}, u32[]{:S(2)}) collective-permute-start(bf16[72,1152]{1,0:T(8,128)(2,1)S(1)} %add_convert_fusion.10), channel_id=1, source_target_pairs={{0,8},{4,12},{8,0},{12,4},{16,24},{20,28},{24,16},{28,20},{1,9},{5... | collective-permute-start | bytes 497672 | tf_op jit(solution)/shard_map/ppermute | solution.py:278
  369.0 5.6 %collective-permute-start.24 = (bf16[72,1152]{1,0:T(8,128)(2,1)S(1)}, bf16[72,1152]{1,0:T(8,128)(2,1)S(1)}, u32[]{:S(2)}, u32[]{:S(2)}) collective-permute-start(bf16[72,1152]{1,0:T(8,128)(2,1)S(1)} %add_convert_fusion.11), channel_id=1, source_target_pairs={{0,16},{4,20},{8,24},{12,28},{16,0},{20,4},{24,8},{28,12},{1,17},{... | collective-permute-start | bytes 497672 | tf_op jit(solution)/shard_map/ppermute | solution.py:278
  374.7 12.3 %collective-permute-start.27 = (bf16[144,1152]{1,0:T(8,128)(2,1)S(1)}, bf16[144,1152]{1,0:T(8,128)(2,1)S(1)}, u32[]{:S(2)}, u32[]{:S(2)}) collective-permute-start(bf16[144,1152]{1,0:T(8,128)(2,1)S(1)} %maximum_select_fusion.11), channel_id=1, source_target_pairs={{0,16},{4,20},{8,24},{12,28},{16,0},{20,4},{24,8},{28,12},{1,17},{... | collective-permute-start | bytes 995336 | tf_op jit(solution)/shard_map/ppermute | solution.py:278
  375.4 11.6 %collective-permute-start.26 = (bf16[144,1152]{1,0:T(8,128)(2,1)S(1)}, bf16[144,1152]{1,0:T(8,128)(2,1)S(1)}, u32[]{:S(2)}, u32[]{:S(2)}) collective-permute-start(bf16[144,1152]{1,0:T(8,128)(2,1)S(1)} %maximum_select_fusion.10), channel_id=1, source_target_pairs={{0,8},{4,12},{8,0},{12,4},{16,24},{20,28},{24,16},{28,20},{1,9},{5... | collective-permute-start | bytes 995336 | tf_op jit(solution)/shard_map/ppermute | solution.py:278
  377.5 10.5 %collective-permute-start.15 = (f32[4,8,216]{2,1,0:T(8,128)S(1)}, f32[4,8,216]{2,1,0:T(8,128)S(1)}, u32[]{:S(2)}, u32[]{:S(2)}) collective-permute-start(f32[4,8,216]{2,1,0:T(8,128)S(1)} %bitcast.145), channel_id=1, source_target_pairs={{0,1},{1,2},{2,3},{3,0},{4,5},{5,6},{6,7},{7,4},{8,9},{9,10},{10,1... | collective-permute-start | bytes 82952 | tf_op jit(solution)/shard_map/ppermute | solution.py:310
  378.0 10.0 %collective-permute-start.16 = (f32[4,8,216]{2,1,0:T(8,128)S(1)}, f32[4,8,216]{2,1,0:T(8,128)S(1)}, u32[]{:S(2)}, u32[]{:S(2)}) collective-permute-start(f32[4,8,216]{2,1,0:T(8,128)S(1)} %bitcast.144), channel_id=1, source_target_pairs={{0,2},{1,3},{2,0},{3,1},{4,6},{5,7},{6,4},{7,5},{8,10},{9,11},{10,... | collective-permute-start | bytes 82952 | tf_op jit(solution)/shard_map/ppermute | solution.py:310
  379.4 8.6 %collective-permute-start.17 = (f32[4,8,216]{2,1,0:T(8,128)S(1)}, f32[4,8,216]{2,1,0:T(8,128)S(1)}, u32[]{:S(2)}, u32[]{:S(2)}) collective-permute-start(f32[4,8,216]{2,1,0:T(8,128)S(1)} %bitcast.143), channel_id=1, source_target_pairs={{0,3},{1,0},{2,1},{3,2},{4,7},{5,4},{6,5},{7,6},{8,11},{9,8},{10,9... | collective-permute-start | bytes 82952 | tf_op jit(solution)/shard_map/ppermute | solution.py:310
  387.2 14.8 %collective-permute-start.29 = (bf16[288,1152]{1,0:T(8,128)(2,1)S(1)}, bf16[288,1152]{1,0:T(8,128)(2,1)S(1)}, u32[]{:S(2)}, u32[]{:S(2)}) collective-permute-start(bf16[288,1152]{1,0:T(8,128)(2,1)S(1)} %maximum_select_fusion.9), channel_id=1, source_target_pairs={{0,4},{4,0},{8,12},{12,8},{16,20},{20,16},{24,28},{28,24},{1,5},{5... | collective-permute-start | bytes 1990664 | tf_op jit(solution)/shard_map/ppermute | solution.py:278
  387.4 14.6 %collective-permute-start.28 = (bf16[288,1152]{1,0:T(8,128)(2,1)S(1)}, bf16[288,1152]{1,0:T(8,128)(2,1)S(1)}, u32[]{:S(2)}, u32[]{:S(2)}) collective-permute-start(bf16[288,1152]{1,0:T(8,128)(2,1)S(1)} %maximum_select_fusion.8), channel_id=1, source_target_pairs={{0,4},{4,0},{8,12},{12,8},{16,20},{20,16},{24,28},{28,24},{1,5},{5... | collective-permute-start | bytes 1990664 | tf_op jit(solution)/shard_map/ppermute | solution.py:278
  (22 other events, 178.1 us)
Sparse Core Ops, SparseCore 0:
  12.0 42.9 all-gather.4
  68.0 37.3 reduce-scatter.4
  107.5 39.2 all-gather.8
  148.7 39.0 all-gather.6
  238.6 36.3 reduce-scatter.8
  282.9 37.2 all-gather.10
  345.8 38.3 reduce-scatter.6
  386.5 38.4 reduce-scatter.10

commit v4 on v3

--- a/solution.py
+++ b/solution.py
@@ -293,11 +293,75 @@
     return [add_low(own, got) for own, got in lax.optimization_barrier(flights)]
 
 
-def join_all(parts, level):
-    ways = orders()
-    flights = [double(part, way[level]) for part, way in zip(parts, ways)]
-    flights = lax.optimization_barrier(flights)
-    return [join(own, got, way[level]) for (own, got), way in zip(flights, ways)]
+def double_all(parts, level):
+    flights = [double(part, way[level]) for part, way in zip(parts, orders())]
+    return lax.optimization_barrier(flights)
+
+
+def join_all(flights, level):
+    return [join(own, got, way[level]) for (own, got), way in zip(flights, orders())]
+
+
+def trade(part):
+    count, mine = lax.axis_size("dp") // 2, lax.axis_index("dp") >> 1
+    blocks = part.reshape(count, part.shape[0] // count, part.shape[1])
+    own = lax.dynamic_index_in_dim(blocks, mine, 0, keepdims=False)
+    sends = [
+        lax.dynamic_index_in_dim(blocks, mine ^ step, 0, keepdims=False) for step in range(1, count)
+    ]
+    return [own] + far(sends)
+
+
+def far(sends):
+    every = range(lax.axis_size("dp"))
+    return [
+        lax.ppermute(send, "dp", [(i, i ^ (2 * step)) for i in every])
+        for step, send in enumerate(sends, 1)
+    ]
+
+
+def spread(block):
+    return [block] + far([block] * (lax.axis_size("dp") // 2 - 1))
+
+
+def finish_body(places, own, got, first, second):
+    count, rows = own.shape[0], first.shape[1]
+    cut = first.shape[0]
+    side, mine = places[0], places[1]
+
+    def block(step):
+        place = (step % count) ^ mine
+        left, right = own[place, :rows, :], got[place, :rows, :]
+        return jnp.where(step // count == side, left, right).astype(F32)
+
+    def fill_first(step, carry):
+        first[step] = block(step)
+        return carry
+
+    def fill_second(step, carry):
+        second[step] = block(step + cut)
+        return carry
+
+    lax.fori_loop(0, cut, fill_first, 0)
+    lax.fori_loop(0, 2 * count - cut, fill_second, 0)
+
+
+def finish(own, got, rows):
+    count, _, width = own.shape
+    index = lax.axis_index("dp")
+    places = jnp.stack([index & 1, index >> 1]).astype(jnp.int32)
+    cut = 3 * count // 2
+    vmem = pl.BlockSpec(memory_space=pltpu.VMEM)
+    return pl.pallas_call(
+        finish_body,
+        in_specs=[pl.BlockSpec(memory_space=pltpu.SMEM), vmem, vmem],
+        out_specs=[vmem, vmem],
+        out_shape=[
+            jax.ShapeDtypeStruct((cut, rows, width), F32),
+            jax.ShapeDtypeStruct((2 * count - cut, rows, width), F32),
+        ],
+        name="finish",
+    )(places, own, got)
 
 
 def orders():
@@ -446,13 +510,13 @@
     for level in range(2, levels):
         sums = halve_all(sums, level)
     for level in reversed(range(1, levels)):
-        sums = join_all(sums, level)
-    up_weight_grad, down_weight_grad = [part.astype(F32) for part in join_all(sums, 0)]
+        sums = join_all(double_all(sums, level), level)
+    last = double_all(sums, 0)
     mixed_grad, attend_stats, bias_sums, part = call(
         functools.partial(attend_back_body, head_dim), group,
         [
             (group_grad, True), (qkv, True), (group_routed, True), (mixed_one, True),
-            (attended, True), (after(keep, up_weight_grad, down_weight_grad), True),
+            (attended, True), (after(keep, last), True),
             (qkv_weight, False), (out_weight, False),
         ],
         [
@@ -471,15 +535,9 @@
         [((images, patches, width), BF16)],
     )
     mixed_one_grad = own_sum(mixed_grad)
-    part = part.reshape(2, 2 * cols, width)
-    firsts = [part[0], part[1]]
-    for level in range(levels):
-        firsts = halve_all(firsts, level)
-    for level in reversed(range(levels)):
-        firsts = join_all(firsts, level)
-    part = jnp.concatenate(firsts, axis=0).astype(F32)
-    qkv_weight_grad = part[: 3 * cols].reshape(3, cols, width)
-    out_weight_grad = part[3 * cols :]
+    half = add_low(*halve(part.reshape(4 * cols, width), 0))
+    last = after(last, half)
+    blocks = trade(half)
 
     placed = lax.dynamic_update_slice(
         jnp.zeros((group, 3, width), F32), middle_stats, (here * images, 0, 0)
@@ -498,8 +556,23 @@
     ]
     sizes = [piece.shape[0] for piece in pieces]
     packed = jnp.concatenate(pieces)
-    packed = jnp.pad(packed, (0, -packed.shape[0] % 2048)).reshape(-1, 128)
-    packed = lax.all_gather(packed, "dp", axis=0, tiled=False).reshape(groups, -1)
+    packed = jnp.pad(packed, (0, -packed.shape[0] % (16 * width))).reshape(-1, width)
+    blocks = after(blocks, packed)
+    block_sum = sum(one.astype(F32) for one in blocks).astype(BF16)
+    rows = block_sum.shape[0]
+    last = after(last, block_sum)
+    up_weight_grad, down_weight_grad = [one.astype(F32) for one in join_all(last, 0)]
+    pieces = spread(jnp.concatenate([block_sum, packed]))
+    own = jnp.stack(after(pieces, up_weight_grad, down_weight_grad, layer_out))
+    own, got = double(own, 0)
+    qkv_weight_grad, out_weight_grad = finish(own, got, rows)
+    qkv_weight_grad = qkv_weight_grad.reshape(3, cols, width)
+    out_weight_grad = out_weight_grad.reshape(cols, width)
+
+    packed = jnp.stack([own[:, rows:], got[:, rows:]]).reshape(2, groups // 2, -1)
+    place = lax.axis_index("dp")
+    order = jnp.arange(groups) ^ place
+    packed = packed[order & 1, order >> 1]
     starts = [sum(sizes[:i]) for i in range(len(sizes))]
     views = [packed[:, s : s + n] for s, n in zip(starts, sizes)]
     mod_all = views[0].reshape(groups, group, groups, each)

time: 436 us -> 410 us (0.940)
  waiting for transfers between devices: 242 us -> 224 us
  blocking collectives: 9.71 us -> 0 us
  starting transfers between devices: 34.7 us -> 28.3 us
  Pallas kernels: 73.5 us -> 78.1 us
    ppermute x12 -> x7, waiting for transfers between devices: 41.2 us -> 19.1 us  [halve(): return (own, lax.ppermute(other, 'dp', partner(bit)))]
    all_gather x4, waiting for transfers between devices: 120 us -> 98.5 us  [all_rows(): return lax.all_gather(rows, 'mp', axis=0, tiled=True)]
    ppermute x0 -> x6, waiting for transfers between devices: none -> 10.4 us  [far(): lax.ppermute(send, 'dp', [(i, i ^ 2 * step) for i in every])]
    all_gather x1 -> x0, blocking collectives: 9.71 us -> none  [per_device(): lax.all_gather(packed, 'dp', axis=0, tiled=False).reshape(groups, -1)]
    reduce_scatter x4, waiting for transfers between devices: 55.4 us -> 63.7 us  [own_sum(): return lax.psum_scatter(rows, 'mp', scatter_dimension=0, tiled=True)]
    ppermute x0 -> x6, starting transfers between devices: none -> 7.04 us  [far(): lax.ppermute(send, 'dp', [(i, i ^ 2 * step) for i in every])]
    ppermute x12 -> x7, starting transfers between devices: 11.6 us -> 5.18 us  [halve(): return (own, lax.ppermute(other, 'dp', partner(bit)))]
    pallas_call x0 -> x1, Pallas kernels: none -> 4.64 us  [finish(): pl.pallas_call(finish_body, in_specs=[pl.BlockSpec(memory_space=pltpu.SME...]
  transfers between devices with their start and end apart: 38 -> 34, of which waited for: 26 -> 23; matrix products, arithmetic and copies ran while one was open for 10% -> 13% of each run, Pallas kernels for 5% -> 11%
where the time goes in v4:
time: 410 us; the launch traced here: 409 us
  waiting for transfers between devices  224 us (55%)
  Pallas kernels  78.1 us (19%)
  starting transfers between devices  28.3 us (7%)
  other arithmetic  23.4 us (6%)
  local copies, waits for them, and re-layouts  22.4 us (5%)
  matrix products  17.5 us (4%)
  between operations  15.4 us (4%)
    all_gather x4, waiting for transfers between devices, all_rows(): return lax.all_gather(rows, 'mp', axis=0, tiled=True)  98.5 us
    pallas_call x9, Pallas kernels, call(): pl.pallas_call(body, grid=(grid,), in_specs=[block(a.shape) if step else...  73.5 us
    reduce_scatter x4, waiting for transfers between devices, own_sum(): return lax.psum_scatter(rows, 'mp', scatter_dimension=0, tiled=True)  63.7 us
    ppermute x7, waiting for transfers between devices, double(): return (part, lax.ppermute(part, 'dp', partner(bit)))  27.6 us
    ppermute x7, waiting for transfers between devices, halve(): return (own, lax.ppermute(other, 'dp', partner(bit)))  19.1 us
    dot_general x4, matrix products, mm(): lax.dot_general(left, right, (dims, ((), ())), preferred_element_type=F32)  17.5 us
    ppermute x6, waiting for transfers between devices, far(): lax.ppermute(send, 'dp', [(i, i ^ 2 * step) for i in every])  10.4 us
    ppermute x6, starting transfers between devices, shift(): lax.ppermute(value, 'mp', [(i, (i + step) % count) for i in range(count)])  9.47 us
  transfers between devices with their start and end apart: 34, of which 23 were waited for; matrix products, arithmetic and copies ran while one was open for 13% of the time, Pallas kernels for 11%

profile of v4, /device:TPU:0, one launch (start us, length us, event | category | flops | bytes accessed | tf_op | source)
XLA Modules:
  0.0 409.2 jit_solution(627605988561181194)
XLA Ops:
  9.3 2.5 shard_map.238
  12.6 5.1 %collective-permute-start.2 = (bf16[1,1280]{1,0:T(2,128)(2,1)S(1)}, bf16[1,1280]{1,0:T(2,128)(2,1)S(1)}, u32[]{:S(2)}, u32[]{:S(2)}) collective-permute-start(bf16[1,1280]{1,0:T(2,128)(2,1)S(1)} %get-tuple-element.186), channel_id=1, source_target_pairs={{0,3},{1,0},{2,1},{3,2},{4,7},{5,4},{6,5},{7,6},{8,11},{9,8},{10,9... | collective-permute-start | bytes 7688 | tf_op jit(solution)/shard_map/ppermute | solution.py:374
  19.4 2.8 collective-permute-done.1
  23.8 9.7 %convolution_add_fusion = f32[4,6912]{1,0:T(4,128)S(1)} fusion(bf16[6912,1152]{1,0:T(8,128)(2,1)} %param.20, f32[6912]{0:T(1024)S(1)} %convert_element_type.167, bf16[4,1280]{1,0:T(4,128)(2,1)S(1)} %broadcast_select_fusion), kind=kOutput, calls=%fused_computation.4 | convolution fusion | flops 63756288 | bytes 16073728 | tf_op jit(solution)/shard_map/dot_general | solution.py:36
  34.9 20.2 %all-gather.5.cloned.1.call-done.routed = bf16[4,192,1152]{2,1,0:T(8,128)(2,1)} async-done(((bf16[1,192,1152]{2,1,0:T(8,128)(2,1)}), bf16[4,192,1152]{2,1,0:T(8,128)(2,1)}) %all-gather.5.cloned.1.call-update) | async-done | bytes 1769488 | tf_op jit(solution)/shard_map/all_gather | solution.py:393
  55.1 12.8 %shard_map.239 = (bf16[4,192,1152]{2,1,0:T(8,128)(2,1)}, bf16[4,3,192,288]{3,2,1,0:T(8,128)(2,1)}, bf16[4,192,288]{2,1,0:T(8,128)(2,1)}, bf16[4,192,1152]{2,1,0:T(8,128)(2,1)}) custom-call(bf16[4,192,1152]{2,1,0:T(8,128)(2,1)} %all-gather.5.cloned.1.call-done.routed, f32[4,6,1152]{2,1,0:T(8,128)} %reshape.239.mod, f32[4,1,128]{2,1,0:T(1,128)} %bitcast.128, ...), custom_call_target="tpu_custom_call" | custom-call | tf_op jit(solution)/shard_map/pallas_call | solution.py:55
  70.7 34.7 %reduce-scatter.5.cloned.1.call-done.branch = bf16[1,192,1152]{2,1,0:T(8,128)(2,1)} async-done(((bf16[4,192,1152]{2,1,0:T(8,128)(2,1)}), bf16[1,192,1152]{2,1,0:T(8,128)(2,1)}) %reduce-scatter.5.cloned.1.call-update) | async-done | bytes 442384 | tf_op jit(solution)/shard_map/reduce_scatter | solution.py:397
  105.9 2.5 shard_map.240
  109.2 37.5 %all-gather.9.cloned.1.call-done.grad_two = bf16[4,192,1152]{2,1,0:T(8,128)(2,1)} async-done(((bf16[1,192,1152]{2,1,0:T(8,128)(2,1)}), bf16[4,192,1152]{2,1,0:T(8,128)(2,1)}) %all-gather.9.cloned.1.call-update) | async-done | bytes 1769488 | tf_op jit(solution)/shard_map/all_gather | solution.py:393
  146.7 7.4 %shard_map.241 = (bf16[4,192,1152]{2,1,0:T(8,128)(2,1)}, f32[4,192,1152]{2,1,0:T(8,128)}, f32[4,1,1152]{2,1,0:T(1,128)}) custom-call(bf16[4,192,1152]{2,1,0:T(8,128)(2,1)} %all-gather.9.cloned.1.call-done.grad_two, f32[4,6,1152]{2,1,0:T(8,128)} %reshape.239.mod, f32[4,1,128]{2,1,0:T(1,128)} %bitcast.129, bf16[1152,1152]{1,0:T(8,128)(2,1)} %down.3), custom_call_target="tpu_custom_call" | custom-call | tf_op jit(solution)/shard_map/pallas_call | solution.py:55
  154.2 33.7 %all-gather.7.cloned.1.call-done.mixed = bf16[4,192,1152]{2,1,0:T(8,128)(2,1)} async-done(((bf16[1,192,1152]{2,1,0:T(8,128)(2,1)}), bf16[4,192,1152]{2,1,0:T(8,128)(2,1)}) %all-gather.7.cloned.1.call-update) | async-done | bytes 1769488 | tf_op jit(solution)/shard_map/all_gather | solution.py:393
  187.9 12.5 %shard_map.242 = (bf16[4,192,1152]{2,1,0:T(8,128)(2,1)}, bf16[4,192,1152]{2,1,0:T(8,128)(2,1)}, bf16[4,192,1152]{2,1,0:T(8,128)(2,1)}, f32[4,1,1152]{2,1,0:T(1,128)}) custom-call(bf16[4,192,1152]{2,1,0:T(8,128)(2,1)} %all-gather.7.cloned.1.call-done.mixed, f32[4,192,1152]{2,1,0:T(8,128)} %get-tuple-element.87.active_grad, bf16[1152,1152]{1,0:T(8,128)(2,1)} %up.1, ...), custom_call_target="tpu_custom_call" | custom-call | tf_op jit(solution)/shard_map/pallas_call | solution.py:55
  200.4 4.0 fusion
  206.8 2.5 fusion.1
  210.7 3.3 collective-permute-done.4
  219.7 13.8 %collective-permute-done.5 = bf16[288,1152]{1,0:T(8,128)(2,1)S(1)} collective-permute-done((bf16[288,1152]{1,0:T(8,128)(2,1)S(1)}, bf16[288,1152]{1,0:T(8,128)(2,1)S(1)}, u32[]{:S(2)}, u32[]{:S(2)}) %collective-permute-start.5) | collective-permute-done | bytes 663584 | tf_op jit(solution)/shard_map/ppermute | solution.py:270
  238.9 6.9 %shard_map.243 = (bf16[4,192,1152]{2,1,0:T(8,128)(2,1)}, f32[4,1,1152]{2,1,0:T(1,128)}) custom-call(bf16[4,192,1152]{2,1,0:T(8,128)(2,1)} %get-tuple-element.88.active, bf16[4,192,1152]{2,1,0:T(8,128)(2,1)} %all-gather.9.cloned.1.call-done.grad_two, f32[4,1,128]{2,1,0:T(1,128)} %bitcast.130, bf16[1152,1152]{1,0:T(8,128)(2,1)} %down.3, f32[1,1152]{1,0:T(1,128)} %select_n.196.bias), custom_call_target="tpu_custom_call" | custom-call | tf_op jit(solution)/shard_map/pallas_call | solution.py:55
  248.4 2.9 shard_map.247
  255.3 5.6 %collective-permute-done.10 = bf16[144,1152]{1,0:T(8,128)(2,1)S(1)} collective-permute-done((bf16[144,1152]{1,0:T(8,128)(2,1)S(1)}, bf16[144,1152]{1,0:T(8,128)(2,1)S(1)}, u32[]{:S(2)}, u32[]{:S(2)}) %collective-permute-start.10) | collective-permute-done | bytes 331808 | tf_op jit(solution)/shard_map/ppermute | solution.py:278
  264.3 12.2 %collective-permute-done.11 = bf16[288,1152]{1,0:T(8,128)(2,1)S(1)} collective-permute-done((bf16[288,1152]{1,0:T(8,128)(2,1)S(1)}, bf16[288,1152]{1,0:T(8,128)(2,1)S(1)}, u32[]{:S(2)}, u32[]{:S(2)}) %collective-permute-start.11) | collective-permute-done | bytes 663584 | tf_op jit(solution)/shard_map/ppermute | solution.py:278
  283.6 7.1 %all-gather.11.cloned.1.call-done.grad = bf16[4,192,1152]{2,1,0:T(8,128)(2,1)} async-done(((bf16[1,192,1152]{2,1,0:T(8,128)(2,1)}), bf16[4,192,1152]{2,1,0:T(8,128)(2,1)}) %all-gather.11.cloned.1.call-update) | async-done | bytes 1769488 | tf_op jit(solution)/shard_map/all_gather | solution.py:393
  290.7 22.7 %shard_map.244 = (bf16[4,192,1152]{2,1,0:T(8,128)(2,1)}, f32[4,3,1152]{2,1,0:T(4,128)}, f32[4,2,288]{2,1,0:T(2,128)}, bf16[4,288,1152]{2,1,0:T(8,128)(2,1)}) custom-call(bf16[4,192,1152]{2,1,0:T(8,128)(2,1)} %all-gather.11.cloned.1.call-done.grad, bf16[4,3,192,288]{3,2,1,0:T(8,128)(2,1)} %get-tuple-element.106.qkv, ...), custom_call_target="tpu_custom_call" | custom-call | tf_op jit(solution)/shard_map/pallas_call | solution.py:55
  313.4 2.5 dynamic-slice_bitcast_fusion
  327.9 4.6 %reduce-scatter.7.cloned.1.call-done.branch = bf16[1,192,1152]{2,1,0:T(8,128)(2,1)} async-done(((bf16[4,192,1152]{2,1,0:T(8,128)(2,1)}), bf16[1,192,1152]{2,1,0:T(8,128)(2,1)}) %reduce-scatter.7.cloned.1.call-update) | async-done | bytes 442384 | tf_op jit(solution)/shard_map/reduce_scatter | solution.py:397
  332.5 2.8 shard_map.245
  336.4 5.1 %collective-permute-done.17 = bf16[144,1152]{1,0:T(8,128)(2,1)} collective-permute-done((bf16[144,1152]{1,0:T(8,128)(2,1)}, bf16[144,1152]{1,0:T(8,128)(2,1)}, u32[]{:S(2)}, u32[]{:S(2)}) %collective-permute-start.17) | collective-permute-done | bytes 331808 | tf_op jit(solution)/shard_map/ppermute | solution.py:318
  346.5 4.7 %fusion.2 = f32[1152,1152]{1,0:T(8,128)} fusion(bf16[576,1152]{1,0:T(8,128)(2,1)} %collective-permute-done.13, bf16[576,1152]{1,0:T(8,128)(2,1)S(1)} %maximum_select_fusion.2, pred[]{:T(512)S(6)} %eq.24), kind=kLoop, calls=%fused_computation.8 | loop fusion | flops 13271040 | bytes 7962625 | tf_op jit(solution)/shard_map/convert_element_type | solution.py:564
  351.2 4.6 %fusion.3 = f32[1152,1152]{1,0:T(8,128)} fusion(bf16[576,1152]{1,0:T(8,128)(2,1)} %collective-permute-done.14, bf16[576,1152]{1,0:T(8,128)(2,1)S(1)} %maximum_select_fusion.3, pred[]{:T(512)S(6)} %eq.24), kind=kLoop, calls=%fused_computation.10 | loop fusion | flops 13271040 | bytes 7962625 | tf_op jit(solution)/shard_map/convert_element_type | solution.py:564
  355.8 5.3 %collective-permute-done.23 = bf16[160,1152]{1,0:T(8,128)(2,1)S(1)} collective-permute-done((bf16[160,1152]{1,0:T(8,128)(2,1)S(1)}, bf16[160,1152]{1,0:T(8,128)(2,1)S(1)}, u32[]{:S(2)}, u32[]{:S(2)}) %collective-permute-start.23) | collective-permute-done | bytes 368672 | tf_op jit(solution)/shard_map/ppermute | solution.py:318
  369.4 4.6 %finish.1 = (f32[6,144,1152]{2,1,0:T(8,128)}, f32[2,144,1152]{2,1,0:T(8,128)}) custom-call(s32[2]{0:T(128)} %pad_add_fusion.places, bf16[4,160,1152]{2,1,0:T(8,128)(2,1)} %copy-done, bf16[4,160,1152]{2,1,0:T(8,128)(2,1)} %copy-done.2), custom_call_target="tpu_custom_call" | custom-call | tf_op jit(solution)/shard_map/finish/pallas_call | solution.py:355
  374.8 24.2 %reduce-scatter.11.cloned.1.call-done.mixed_grad = bf16[1,192,1152]{2,1,0:T(8,128)(2,1)} async-done(((bf16[4,192,1152]{2,1,0:T(8,128)(2,1)}), bf16[1,192,1152]{2,1,0:T(8,128)(2,1)}) %reduce-scatter.11.cloned.1.call-update) | async-done | bytes 442384 | tf_op jit(solution)/shard_map/reduce_scatter | solution.py:397
  399.0 3.3 shard_map.246
  (182 shorter events, 69.2 us)
Async XLA Ops:
  7.2 47.8 %all-gather.5.cloned.1.call-start = ((), (), s32[]{:S(2)}) async-start(), calls=%async_computation.4 | async-start | bytes 2211840 | tf_op jit(solution)/shard_map/all_gather | solution.py:393
  11.9 93.5 %reduce-scatter.5.cloned.1.call-start = ((), (), s32[]{:S(2)}) async-start(), calls=%async_computation.5 | async-start | bytes 2211840 | tf_op jit(solution)/shard_map/reduce_scatter | solution.py:397
  12.6 6.8 %collective-permute-start.2 = (bf16[1,1280]{1,0:T(2,128)(2,1)S(1)}, bf16[1,1280]{1,0:T(2,128)(2,1)S(1)}, u32[]{:S(2)}, u32[]{:S(2)}) collective-permute-start(bf16[1,1280]{1,0:T(2,128)(2,1)S(1)} %get-tuple-element.186), channel_id=1, source_target_pairs={{0,3},{1,0},{2,1},{3,2},{4,7},{5,4},{6,5},{7,6},{8,11},{9,8},{10,9... | collective-permute-start | bytes 7688 | tf_op jit(solution)/shard_map/ppermute | solution.py:374
  17.7 4.5 %collective-permute-start.1 = (bf16[1,1280]{1,0:T(2,128)(2,1)S(1)}, bf16[1,1280]{1,0:T(2,128)(2,1)S(1)}, u32[]{:S(2)}, u32[]{:S(2)}) collective-permute-start(bf16[1,1280]{1,0:T(2,128)(2,1)S(1)} %get-tuple-element.186), channel_id=1, source_target_pairs={{0,2},{1,3},{2,0},{3,1},{4,6},{5,7},{6,4},{7,5},{8,10},{9,11},{10,... | collective-permute-start | bytes 7688 | tf_op jit(solution)/shard_map/ppermute | solution.py:374
  17.7 5.4 %collective-permute-start = (bf16[1,1280]{1,0:T(2,128)(2,1)S(1)}, bf16[1,1280]{1,0:T(2,128)(2,1)S(1)}, u32[]{:S(2)}, u32[]{:S(2)}) collective-permute-start(bf16[1,1280]{1,0:T(2,128)(2,1)S(1)} %get-tuple-element.186), channel_id=1, source_target_pairs={{0,1},{1,2},{2,3},{3,0},{4,5},{5,6},{6,7},{7,4},{8,9},{9,10},{10,1... | collective-permute-start | bytes 7688 | tf_op jit(solution)/shard_map/ppermute | solution.py:374
  67.9 78.8 %all-gather.9.cloned.1.call-start = ((), (), s32[]{:S(2)}) async-start(), calls=%async_computation.7 | async-start | bytes 2211840 | tf_op jit(solution)/shard_map/all_gather | solution.py:393
  68.7 119.2 %all-gather.7.cloned.1.call-start = ((), (), s32[]{:S(2)}) async-start(), calls=%async_computation.6 | async-start | bytes 2211840 | tf_op jit(solution)/shard_map/all_gather | solution.py:393
  108.4 139.9 %reduce-scatter.9.cloned.1.call-start = ((), (), s32[]{:S(2)}) async-start(), calls=%async_computation.9 | async-start | bytes 2211840 | tf_op jit(solution)/shard_map/reduce_scatter | solution.py:397
  205.6 5.1 %collective-permute-start.3 = (bf16[576,1152]{1,0:T(8,128)(2,1)}, bf16[576,1152]{1,0:T(8,128)(2,1)}, u32[]{:S(2)}, u32[]{:S(2)}) collective-permute-start(bf16[576,1152]{1,0:T(8,128)(2,1)} %get-tuple-element.167), channel_id=1, source_target_pairs={{0,4},{4,0},{8,12},{12,8},{16,20},{20,16},{24,28},{28,24},{1,5},{5... | collective-permute-start | bytes 3981320 | tf_op jit(solution)/shard_map/ppermute | solution.py:270
  210.6 3.4 collective-permute-start.4
  210.7 80.1 %all-gather.11.cloned.1.call-start = ((), (), s32[]{:S(2)}) async-start(), calls=%async_computation.10 | async-start | bytes 2211840 | tf_op jit(solution)/shard_map/all_gather | solution.py:393
  216.5 17.0 %collective-permute-start.5 = (bf16[288,1152]{1,0:T(8,128)(2,1)S(1)}, bf16[288,1152]{1,0:T(8,128)(2,1)S(1)}, u32[]{:S(2)}, u32[]{:S(2)}) collective-permute-start(bf16[288,1152]{1,0:T(8,128)(2,1)S(1)} %get-tuple-element.175), channel_id=1, source_target_pairs={{0,8},{4,12},{8,0},{12,4},{16,24},{20,28},{24,16},{28,20},{1,9},{5... | collective-permute-start | bytes 1990664 | tf_op jit(solution)/shard_map/ppermute | solution.py:270
  218.2 16.7 %collective-permute-start.6 = (bf16[288,1152]{1,0:T(8,128)(2,1)S(1)}, bf16[288,1152]{1,0:T(8,128)(2,1)S(1)}, u32[]{:S(2)}, u32[]{:S(2)}) collective-permute-start(bf16[288,1152]{1,0:T(8,128)(2,1)S(1)} %get-tuple-element.173), channel_id=1, source_target_pairs={{0,16},{4,20},{8,24},{12,28},{16,0},{20,4},{24,8},{28,12},{1,17},{... | collective-permute-start | bytes 1990664 | tf_op jit(solution)/shard_map/ppermute | solution.py:270
  235.2 10.7 %collective-permute-start.7 = (bf16[144,1152]{1,0:T(8,128)(2,1)S(1)}, bf16[144,1152]{1,0:T(8,128)(2,1)}, u32[]{:S(2)}, u32[]{:S(2)}) collective-permute-start(bf16[144,1152]{1,0:T(8,128)(2,1)S(1)} %get-tuple-element.179), channel_id=1, source_target_pairs={{0,16},{4,20},{8,24},{12,28},{16,0},{20,4},{24,8},{28,12},{1,17},{... | collective-permute-start | bytes 995336 | tf_op jit(solution)/shard_map/ppermute | solution.py:270
  237.7 8.7 %collective-permute-start.8 = (bf16[144,1152]{1,0:T(8,128)(2,1)}, bf16[144,1152]{1,0:T(8,128)(2,1)S(1)}, u32[]{:S(2)}, u32[]{:S(2)}) collective-permute-start(bf16[144,1152]{1,0:T(8,128)(2,1)} %get-tuple-element.177), channel_id=1, source_target_pairs={{0,8},{4,12},{8,0},{12,4},{16,24},{20,28},{24,16},{28,20},{1,9},{5... | collective-permute-start | bytes 995336 | tf_op jit(solution)/shard_map/ppermute | solution.py:270
  247.5 7.8 %collective-permute-start.9 = (bf16[144,1152]{1,0:T(8,128)(2,1)S(1)}, bf16[144,1152]{1,0:T(8,128)(2,1)S(1)}, u32[]{:S(2)}, u32[]{:S(2)}) collective-permute-start(bf16[144,1152]{1,0:T(8,128)(2,1)S(1)} %add_convert_fusion.6), channel_id=1, source_target_pairs={{0,16},{4,20},{8,24},{12,28},{16,0},{20,4},{24,8},{28,12},{1,17},{... | collective-permute-start | bytes 995336 | tf_op jit(solution)/shard_map/ppermute | solution.py:278
  251.3 81.2 %reduce-scatter.7.cloned.1.call-start = ((), (), s32[]{:S(2)}) async-start(), calls=%async_computation.8 | async-start | bytes 2211840 | tf_op jit(solution)/shard_map/reduce_scatter | solution.py:397
  251.7 9.2 %collective-permute-start.10 = (bf16[144,1152]{1,0:T(8,128)(2,1)S(1)}, bf16[144,1152]{1,0:T(8,128)(2,1)S(1)}, u32[]{:S(2)}, u32[]{:S(2)}) collective-permute-start(bf16[144,1152]{1,0:T(8,128)(2,1)S(1)} %add_convert_fusion.5), channel_id=1, source_target_pairs={{0,8},{4,12},{8,0},{12,4},{16,24},{20,28},{24,16},{28,20},{1,9},{5... | collective-permute-start | bytes 995336 | tf_op jit(solution)/shard_map/ppermute | solution.py:278
  261.0 15.5 %collective-permute-start.11 = (bf16[288,1152]{1,0:T(8,128)(2,1)S(1)}, bf16[288,1152]{1,0:T(8,128)(2,1)S(1)}, u32[]{:S(2)}, u32[]{:S(2)}) collective-permute-start(bf16[288,1152]{1,0:T(8,128)(2,1)S(1)} %maximum_select_fusion.4), channel_id=1, source_target_pairs={{0,8},{4,12},{8,0},{12,4},{16,24},{20,28},{24,16},{28,20},{1,9},{5... | collective-permute-start | bytes 1990664 | tf_op jit(solution)/shard_map/ppermute | solution.py:278
  262.7 15.2 %collective-permute-start.12 = (bf16[288,1152]{1,0:T(8,128)(2,1)S(1)}, bf16[288,1152]{1,0:T(8,128)(2,1)S(1)}, u32[]{:S(2)}, u32[]{:S(2)}) collective-permute-start(bf16[288,1152]{1,0:T(8,128)(2,1)S(1)} %maximum_select_fusion.5), channel_id=1, source_target_pairs={{0,16},{4,20},{8,24},{12,28},{16,0},{20,4},{24,8},{28,12},{1,17},{... | collective-permute-start | bytes 1990664 | tf_op jit(solution)/shard_map/ppermute | solution.py:278
  279.0 4.6 %collective-permute-start.14 = (bf16[576,1152]{1,0:T(8,128)(2,1)S(1)}, bf16[576,1152]{1,0:T(8,128)(2,1)}, u32[]{:S(2)}, u32[]{:S(2)}) collective-permute-start(bf16[576,1152]{1,0:T(8,128)(2,1)S(1)} %maximum_select_fusion.3), channel_id=1, source_target_pairs={{0,4},{4,0},{8,12},{12,8},{16,20},{20,16},{24,28},{28,24},{1,5},{5... | collective-permute-start | bytes 3981320 | tf_op jit(solution)/shard_map/ppermute | solution.py:278
  279.6 119.4 %reduce-scatter.11.cloned.1.call-start = ((), (), s32[]{:S(2)}) async-start(), calls=%async_computation.11 | async-start | bytes 2211840 | tf_op jit(solution)/shard_map/reduce_scatter | solution.py:397
  316.0 4.5 %collective-permute-start.15 = (bf16[576,1152]{1,0:T(8,128)(2,1)}, bf16[576,1152]{1,0:T(8,128)(2,1)}, u32[]{:S(2)}, u32[]{:S(2)}) collective-permute-start(bf16[576,1152]{1,0:T(8,128)(2,1)} %dynamic-slice_bitcast_fusion), channel_id=1, source_target_pairs={{0,4},{4,0},{8,12},{12,8},{16,20},{20,16},{24,28},{28,24},{1,5},{5... | collective-permute-start | bytes 3981320 | tf_op jit(solution)/shard_map/ppermute | solution.py:270
  317.2 9.3 %collective-permute-start.21 = (f32[4,8,216]{2,1,0:T(8,128)S(1)}, f32[4,8,216]{2,1,0:T(8,128)S(1)}, u32[]{:S(2)}, u32[]{:S(2)}) collective-permute-start(f32[4,8,216]{2,1,0:T(8,128)S(1)} %bitcast.134), channel_id=1, source_target_pairs={{0,3},{1,0},{2,1},{3,2},{4,7},{5,4},{6,5},{7,6},{8,11},{9,8},{10,9... | collective-permute-start | bytes 82952 | tf_op jit(solution)/shard_map/ppermute | solution.py:374
  318.5 16.8 %collective-permute-start.20 = (f32[4,8,216]{2,1,0:T(8,128)S(1)}, f32[4,8,216]{2,1,0:T(8,128)}, u32[]{:S(2)}, u32[]{:S(2)}) collective-permute-start(f32[4,8,216]{2,1,0:T(8,128)S(1)} %bitcast.132), channel_id=1, source_target_pairs={{0,2},{1,3},{2,0},{3,1},{4,6},{5,7},{6,4},{7,5},{8,10},{9,11},{10,... | collective-permute-start | bytes 82952 | tf_op jit(solution)/shard_map/ppermute | solution.py:374
  319.1 16.2 %collective-permute-start.19 = (f32[4,8,216]{2,1,0:T(8,128)S(1)}, f32[4,8,216]{2,1,0:T(8,128)}, u32[]{:S(2)}, u32[]{:S(2)}) collective-permute-start(f32[4,8,216]{2,1,0:T(8,128)S(1)} %bitcast.133), channel_id=1, source_target_pairs={{0,1},{1,2},{2,3},{3,0},{4,5},{5,6},{6,7},{7,4},{8,9},{9,10},{10,1... | collective-permute-start | bytes 82952 | tf_op jit(solution)/shard_map/ppermute | solution.py:374
  323.5 12.9 %collective-permute-start.16 = (bf16[144,1152]{1,0:T(8,128)(2,1)}, bf16[144,1152]{1,0:T(8,128)(2,1)}, u32[]{:S(2)}, u32[]{:S(2)}) collective-permute-start(bf16[144,1152]{1,0:T(8,128)(2,1)} %get-tuple-element.171), channel_id=1, source_target_pairs={{0,8},{4,12},{8,0},{12,4},{16,24},{20,28},{24,16},{28,20},{1,9},{5... | collective-permute-start | bytes 995336 | tf_op jit(solution)/shard_map/ppermute | solution.py:318
  325.0 16.5 %collective-permute-start.17 = (bf16[144,1152]{1,0:T(8,128)(2,1)}, bf16[144,1152]{1,0:T(8,128)(2,1)}, u32[]{:S(2)}, u32[]{:S(2)}) collective-permute-start(bf16[144,1152]{1,0:T(8,128)(2,1)} %get-tuple-element.170), channel_id=1, source_target_pairs={{0,16},{4,20},{8,24},{12,28},{16,0},{20,4},{24,8},{28,12},{1,17},{... | collective-permute-start | bytes 995336 | tf_op jit(solution)/shard_map/ppermute | solution.py:318
  326.5 15.0 %collective-permute-start.18 = (bf16[144,1152]{1,0:T(8,128)(2,1)S(1)}, bf16[144,1152]{1,0:T(8,128)(2,1)}, u32[]{:S(2)}, u32[]{:S(2)}) collective-permute-start(bf16[144,1152]{1,0:T(8,128)(2,1)S(1)} %get-tuple-element.169), channel_id=1, source_target_pairs={{0,24},{4,28},{8,16},{12,20},{16,8},{20,12},{24,0},{28,4},{1,25},{... | collective-permute-start | bytes 995336 | tf_op jit(solution)/shard_map/ppermute | solution.py:318
  342.9 12.9 %collective-permute-start.22 = (bf16[160,1152]{1,0:T(8,128)(2,1)S(1)}, bf16[160,1152]{1,0:T(8,128)(2,1)S(1)}, u32[]{:S(2)}, u32[]{:S(2)}) collective-permute-start(bf16[160,1152]{1,0:T(8,128)(2,1)S(1)} %pad_maximum_fusion.1), channel_id=1, source_target_pairs={{0,8},{4,12},{8,0},{12,4},{16,24},{20,28},{24,16},{28,20},{1,9},{5... | collective-permute-start | bytes 1105928 | tf_op jit(solution)/shard_map/ppermute | solution.py:318
  344.2 16.9 %collective-permute-start.23 = (bf16[160,1152]{1,0:T(8,128)(2,1)S(1)}, bf16[160,1152]{1,0:T(8,128)(2,1)S(1)}, u32[]{:S(2)}, u32[]{:S(2)}) collective-permute-start(bf16[160,1152]{1,0:T(8,128)(2,1)S(1)} %pad_maximum_fusion.1), channel_id=1, source_target_pairs={{0,16},{4,20},{8,24},{12,28},{16,0},{20,4},{24,8},{28,12},{1,17},{... | collective-permute-start | bytes 1105928 | tf_op jit(solution)/shard_map/ppermute | solution.py:318
  345.0 16.1 %collective-permute-start.24 = (bf16[160,1152]{1,0:T(8,128)(2,1)S(1)}, bf16[160,1152]{1,0:T(8,128)(2,1)S(1)}, u32[]{:S(2)}, u32[]{:S(2)}) collective-permute-start(bf16[160,1152]{1,0:T(8,128)(2,1)S(1)} %pad_maximum_fusion.1), channel_id=1, source_target_pairs={{0,24},{4,28},{8,16},{12,20},{16,8},{20,12},{24,0},{28,4},{1,25},{... | collective-permute-start | bytes 1105928 | tf_op jit(solution)/shard_map/ppermute | solution.py:318
  (23 other events, 172.0 us)
Sparse Core Ops, SparseCore 0:
  12.0 43.0 all-gather.4
  68.0 37.2 reduce-scatter.4
  107.5 39.2 all-gather.8
  148.7 39.0 all-gather.6
  210.8 37.4 reduce-scatter.8
  251.4 39.2 all-gather.10
  293.0 39.4 reduce-scatter.6
  361.5 37.4 reduce-scatter.10

commit v5 on v4

--- a/solution.py
+++ b/solution.py
@@ -393,6 +393,29 @@
     return lax.all_gather(rows, "mp", axis=0, tiled=True)
 
 
+def chain_rows(rows):
+    count = lax.axis_size("mp")
+    up = down = rows
+    ups, downs = [], []
+    for hop in range(1, count):
+        up = lax.ppermute(up, "mp", [(i, i + 1) for i in range(hop - 1, count - 1)])
+        down = lax.ppermute(down, "mp", [(i, i - 1) for i in range(count - hop, 0, -1)])
+        ups.append(up)
+        downs.append(down)
+    return ups, downs
+
+
+def in_order(rows, ups, downs):
+    count, here = lax.axis_size("mp"), lax.axis_index("mp")
+    slots = [rows] + [
+        jnp.where(here > hop, up, down) for hop, (up, down) in enumerate(zip(ups, downs[::-1]))
+    ]
+    order = (here - jnp.arange(count)) % count
+    return jnp.concatenate(
+        [lax.dynamic_index_in_dim(jnp.stack(slots), order[i], 0, False) for i in range(count)]
+    )
+
+
 def own_sum(rows):
     return lax.psum_scatter(rows, "mp", scatter_dimension=0, tiled=True)
 
@@ -427,7 +450,11 @@
         [(rows_shape, BF16), (rows_shape, BF16)],
     )
     group_routed = all_rows(routed)
-    group_two = all_rows(grad_two)
+    near = members <= 4
+    if near:
+        hops = chain_rows(after(grad_two, group_routed))
+    else:
+        group_two = all_rows(grad_two)
 
     small = jnp.concatenate(
         [conditioning, jnp.broadcast_to(keep_count.astype(BF16)[:, None], (images, 128))], axis=1
@@ -463,6 +490,8 @@
         [(rows_shape, F32), (rows_shape, BF16)],
     )
     group_mixed = all_rows(mixed_two)
+    if near:
+        group_two = in_order(grad_two, *after(hops, mixed_two))
     unit_shape = (group, slots, hidden_units)
     down_grad, active_grad, down_sum = call(
         down_back_body, group,
@@ -501,7 +530,7 @@
         middle_back_body, images,
         [
             (mixed_two_grad, True), (hidden_one, True), (branch_one, True), (out_bias_row, False),
-            (grad_two, True), (own_mod, True), (after(own_keep, gate_grad, *sums), True),
+            (grad_two, True), (own_mod, True), (after(own_keep, gate_grad), True),
         ],
         [(rows_shape, F32), (rows_shape, BF16), ((images, 3, width), F32)],
     )

time: 410 us -> 389 us (0.949)
  waiting for transfers between devices: 224 us -> 183 us
  between operations: 15.4 us -> 23.2 us
  starting transfers between devices: 28.3 us -> 35.9 us
    all_gather x4 -> x3, waiting for transfers between devices: 98.5 us -> 27.5 us  [all_rows(): return lax.all_gather(rows, 'mp', axis=0, tiled=True)]
    ppermute x0 -> x6, waiting for transfers between devices: none -> 57.3 us  [the longest x3 41.3 us: chain_rows(): lax.ppermute(down, 'mp', [(i, i - 1) for i in range(count - hop, 0, -1)])]
    reduce_scatter x4, waiting for transfers between devices: 63.7 us -> 37.7 us  [own_sum(): return lax.psum_scatter(rows, 'mp', scatter_dimension=0, tiled=True)]
    ppermute x0 -> x6, starting transfers between devices: none -> 7.68 us  [the longest x3 4.03 us: chain_rows(): lax.ppermute(down, 'mp', [(i, i - 1) for i in range(count - hop, 0, -1)])]
  transfers between devices with their start and end apart: 34 -> 39, of which waited for: 23 -> 25; matrix products, arithmetic and copies ran while one was open for 13% -> 14% of each run, Pallas kernels for 11% -> 12%
where the time goes in v5:
time: 389 us; the launch traced here: 388 us
  waiting for transfers between devices  183 us (47%)
  Pallas kernels  78.2 us (20%)
  starting transfers between devices  35.9 us (9%)
  other arithmetic  25.3 us (7%)
  local copies, waits for them, and re-layouts  24.1 us (6%)
  between operations  23.2 us (6%)
  matrix products  17.5 us (4%)
    pallas_call x9, Pallas kernels, call(): pl.pallas_call(body, grid=(grid,), in_specs=[block(a.shape) if step else...  73.6 us
    ppermute x3, waiting for transfers between devices, chain_rows(): lax.ppermute(down, 'mp', [(i, i - 1) for i in range(count - hop, 0, -1)])  41.3 us
    reduce_scatter x4, waiting for transfers between devices, own_sum(): return lax.psum_scatter(rows, 'mp', scatter_dimension=0, tiled=True)  37.7 us
    ppermute x7, waiting for transfers between devices, double(): return (part, lax.ppermute(part, 'dp', partner(bit)))  27.6 us
    all_gather x3, waiting for transfers between devices, all_rows(): return lax.all_gather(rows, 'mp', axis=0, tiled=True)  27.5 us
    ppermute x7, waiting for transfers between devices, halve(): return (own, lax.ppermute(other, 'dp', partner(bit)))  18.8 us
    dot_general x4, matrix products, mm(): lax.dot_general(left, right, (dims, ((), ())), preferred_element_type=F32)  17.5 us
    ppermute x3, waiting for transfers between devices, chain_rows(): up = lax.ppermute(up, 'mp', [(i, i + 1) for i in range(hop - 1, count - 1)])  16 us
  transfers between devices with their start and end apart: 39, of which 25 were waited for; matrix products, arithmetic and copies ran while one was open for 14% of the time, Pallas kernels for 12%

profile of v5, /device:TPU:0, one launch (start us, length us, event | category | flops | bytes accessed | tf_op | source)
XLA Modules:
  0.0 387.6 jit_solution(6276916618770698961)
XLA Ops:
  9.2 2.5 shard_map.238
  12.5 5.1 %collective-permute-start.2 = (bf16[1,1280]{1,0:T(2,128)(2,1)S(1)}, bf16[1,1280]{1,0:T(2,128)(2,1)S(1)}, u32[]{:S(2)}, u32[]{:S(2)}) collective-permute-start(bf16[1,1280]{1,0:T(2,128)(2,1)S(1)} %get-tuple-element.204), channel_id=1, source_target_pairs={{0,3},{1,0},{2,1},{3,2},{4,7},{5,4},{6,5},{7,6},{8,11},{9,8},{10,9... | collective-permute-start | bytes 7688 | tf_op jit(solution)/shard_map/ppermute | solution.py:374
  19.3 2.8 collective-permute-done.1
  23.8 9.7 %convolution_add_fusion = f32[4,6912]{1,0:T(4,128)S(1)} fusion(bf16[6912,1152]{1,0:T(8,128)(2,1)} %param.20, f32[6912]{0:T(1024)S(1)} %convert_element_type.167, bf16[4,1280]{1,0:T(4,128)(2,1)S(1)} %broadcast_select_fusion), kind=kOutput, calls=%fused_computation.4 | convolution fusion | flops 63756288 | bytes 16073728 | tf_op jit(solution)/shard_map/dot_general | solution.py:36
  34.8 20.2 %all-gather.4.cloned.1.call-done.routed = bf16[4,192,1152]{2,1,0:T(8,128)(2,1)} async-done(((bf16[1,192,1152]{2,1,0:T(8,128)(2,1)}), bf16[4,192,1152]{2,1,0:T(8,128)(2,1)}) %all-gather.4.cloned.1.call-update) | async-done | bytes 1769488 | tf_op jit(solution)/shard_map/all_gather | solution.py:393
  55.0 12.8 %shard_map.239 = (bf16[4,192,1152]{2,1,0:T(8,128)(2,1)}, bf16[4,3,192,288]{3,2,1,0:T(8,128)(2,1)}, bf16[4,192,288]{2,1,0:T(8,128)(2,1)}, bf16[4,192,1152]{2,1,0:T(8,128)(2,1)}) custom-call(bf16[4,192,1152]{2,1,0:T(8,128)(2,1)} %all-gather.4.cloned.1.call-done.routed, f32[4,6,1152]{2,1,0:T(8,128)} %reshape.239.mod, f32[4,1,128]{2,1,0:T(1,128)} %bitcast.148, ...), custom_call_target="tpu_custom_call" | custom-call | tf_op jit(solution)/shard_map/pallas_call | solution.py:55
  73.1 16.0 %collective-permute-done.3 = bf16[1,192,1152]{2,1,0:T(8,128)(2,1)S(1)} collective-permute-done((bf16[1,192,1152]{2,1,0:T(8,128)(2,1)S(1)}, bf16[1,192,1152]{2,1,0:T(8,128)(2,1)S(1)}, u32[]{:S(2)}, u32[]{:S(2)}) %collective-permute-start.3) | collective-permute-done | bytes 442400 | tf_op jit(solution)/shard_map/ppermute | solution.py:401
  89.8 14.5 %collective-permute-done.6 = bf16[1,192,1152]{2,1,0:T(8,128)(2,1)S(1)} collective-permute-done((bf16[1,192,1152]{2,1,0:T(8,128)(2,1)S(1)}, bf16[1,192,1152]{2,1,0:T(8,128)(2,1)S(1)}, u32[]{:S(2)}, u32[]{:S(2)}) %collective-permute-start.6) | collective-permute-done | bytes 442400 | tf_op jit(solution)/shard_map/ppermute | solution.py:402
  107.0 8.5 %reduce-scatter.5.cloned.1.call-done.branch = bf16[1,192,1152]{2,1,0:T(8,128)(2,1)} async-done(((bf16[4,192,1152]{2,1,0:T(8,128)(2,1)}), bf16[1,192,1152]{2,1,0:T(8,128)(2,1)}) %reduce-scatter.5.cloned.1.call-update) | async-done | bytes 442384 | tf_op jit(solution)/shard_map/reduce_scatter | solution.py:420
  119.3 2.8 collective-permute-done.7
  132.6 23.9 %collective-permute-done.8 = bf16[1,192,1152]{2,1,0:T(8,128)(2,1)S(1)} collective-permute-done((bf16[1,192,1152]{2,1,0:T(8,128)(2,1)S(1)}, bf16[1,192,1152]{2,1,0:T(8,128)(2,1)S(1)}, u32[]{:S(2)}, u32[]{:S(2)}) %collective-permute-start.8) | collective-permute-done | bytes 442400 | tf_op jit(solution)/shard_map/ppermute | solution.py:402
  158.6 7.5 %shard_map.241 = (bf16[4,192,1152]{2,1,0:T(8,128)(2,1)}, f32[4,192,1152]{2,1,0:T(8,128)}, f32[4,1,1152]{2,1,0:T(1,128)}) custom-call(bf16[4,192,1152]{2,1,0:T(8,128)(2,1)} %pad_maximum_fusion.1.grad_two, f32[4,6,1152]{2,1,0:T(8,128)} %reshape.239.mod, f32[4,1,128]{2,1,0:T(1,128)} %bitcast.149, bf16[1152,1152]{1,0:T(8,128)(2,1)} %down.3), custom_call_target="tpu_custom_call" | custom-call | tf_op jit(solution)/shard_map/pallas_call | solution.py:55
  166.0 12.5 %shard_map.242 = (bf16[4,192,1152]{2,1,0:T(8,128)(2,1)}, bf16[4,192,1152]{2,1,0:T(8,128)(2,1)}, bf16[4,192,1152]{2,1,0:T(8,128)(2,1)}, f32[4,1,1152]{2,1,0:T(1,128)}) custom-call(bf16[4,192,1152]{2,1,0:T(8,128)(2,1)} %all-gather.6.cloned.1.call-done.mixed, f32[4,192,1152]{2,1,0:T(8,128)} %get-tuple-element.101.active_grad, bf16[1152,1152]{1,0:T(8,128)(2,1)} %up.1, ...), custom_call_target="tpu_custom_call" | custom-call | tf_op jit(solution)/shard_map/pallas_call | solution.py:55
  178.5 4.0 %fusion = bf16[1152,1152]{1,0:T(8,128)(2,1)S(1)} fusion(bf16[4,192,1152]{2,1,0:T(8,128)(2,1)} %get-tuple-element.103, bf16[4,192,1152]{2,1,0:T(8,128)(2,1)S(1)} %copy-done.3), kind=kOutput, calls=%fused_computation.5 | convolution fusion | flops 2039758848 | bytes 6193152 | tf_op jit(solution)/shard_map/dot_general | solution.py:36
  189.1 3.1 collective-permute-done.10
  198.8 12.2 %collective-permute-done.11 = bf16[288,1152]{1,0:T(8,128)(2,1)S(1)} collective-permute-done((bf16[288,1152]{1,0:T(8,128)(2,1)S(1)}, bf16[288,1152]{1,0:T(8,128)(2,1)S(1)}, u32[]{:S(2)}, u32[]{:S(2)}) %collective-permute-start.11) | collective-permute-done | bytes 663584 | tf_op jit(solution)/shard_map/ppermute | solution.py:270
  211.0 3.0 collective-permute-done.12
  218.0 7.0 %shard_map.243 = (bf16[4,192,1152]{2,1,0:T(8,128)(2,1)}, f32[4,1,1152]{2,1,0:T(1,128)}) custom-call(bf16[4,192,1152]{2,1,0:T(8,128)(2,1)} %get-tuple-element.102.active, bf16[4,192,1152]{2,1,0:T(8,128)(2,1)} %pad_maximum_fusion.1.grad_two, f32[4,1,128]{2,1,0:T(1,128)} %bitcast.150, bf16[1152,1152]{1,0:T(8,128)(2,1)} %down.3, f32[1,1152]{1,0:T(1,128)} %select_n.241.bias), custom_call_target="tpu_custom_call" | custom-call | tf_op jit(solution)/shard_map/pallas_call | solution.py:55
  226.7 2.9 shard_map.247
  233.4 5.6 %collective-permute-done.16 = bf16[144,1152]{1,0:T(8,128)(2,1)S(1)} collective-permute-done((bf16[144,1152]{1,0:T(8,128)(2,1)S(1)}, bf16[144,1152]{1,0:T(8,128)(2,1)S(1)}, u32[]{:S(2)}, u32[]{:S(2)}) %collective-permute-start.16) | collective-permute-done | bytes 331808 | tf_op jit(solution)/shard_map/ppermute | solution.py:278
  242.4 12.2 %collective-permute-done.17 = bf16[288,1152]{1,0:T(8,128)(2,1)S(1)} collective-permute-done((bf16[288,1152]{1,0:T(8,128)(2,1)S(1)}, bf16[288,1152]{1,0:T(8,128)(2,1)S(1)}, u32[]{:S(2)}, u32[]{:S(2)}) %collective-permute-start.17) | collective-permute-done | bytes 663584 | tf_op jit(solution)/shard_map/ppermute | solution.py:278
  261.7 7.4 %all-gather.8.cloned.1.call-done.grad = bf16[4,192,1152]{2,1,0:T(8,128)(2,1)} async-done(((bf16[1,192,1152]{2,1,0:T(8,128)(2,1)}), bf16[4,192,1152]{2,1,0:T(8,128)(2,1)}) %all-gather.8.cloned.1.call-update) | async-done | bytes 1769488 | tf_op jit(solution)/shard_map/all_gather | solution.py:393
  269.1 22.7 %shard_map.244 = (bf16[4,192,1152]{2,1,0:T(8,128)(2,1)}, f32[4,3,1152]{2,1,0:T(4,128)}, f32[4,2,288]{2,1,0:T(2,128)}, bf16[4,288,1152]{2,1,0:T(8,128)(2,1)}) custom-call(bf16[4,192,1152]{2,1,0:T(8,128)(2,1)} %all-gather.8.cloned.1.call-done.grad, bf16[4,3,192,288]{3,2,1,0:T(8,128)(2,1)} %get-tuple-element.116.qkv, ...), custom_call_target="tpu_custom_call" | custom-call | tf_op jit(solution)/shard_map/pallas_call | solution.py:55
  306.2 4.5 %reduce-scatter.7.cloned.1.call-done.branch = bf16[1,192,1152]{2,1,0:T(8,128)(2,1)} async-done(((bf16[4,192,1152]{2,1,0:T(8,128)(2,1)}), bf16[1,192,1152]{2,1,0:T(8,128)(2,1)}) %reduce-scatter.7.cloned.1.call-update) | async-done | bytes 442384 | tf_op jit(solution)/shard_map/reduce_scatter | solution.py:420
  310.7 2.8 shard_map.245
  314.6 5.3 %collective-permute-done.23 = bf16[144,1152]{1,0:T(8,128)(2,1)} collective-permute-done((bf16[144,1152]{1,0:T(8,128)(2,1)}, bf16[144,1152]{1,0:T(8,128)(2,1)}, u32[]{:S(2)}, u32[]{:S(2)}) %collective-permute-start.23) | collective-permute-done | bytes 331808 | tf_op jit(solution)/shard_map/ppermute | solution.py:318
  324.8 4.7 %fusion.2 = f32[1152,1152]{1,0:T(8,128)} fusion(bf16[576,1152]{1,0:T(8,128)(2,1)} %collective-permute-done.19, bf16[576,1152]{1,0:T(8,128)(2,1)S(1)} %maximum_select_fusion.2, pred[]{:T(512)S(6)} %eq.25), kind=kLoop, calls=%fused_computation.8 | loop fusion | flops 13271040 | bytes 7962625 | tf_op jit(solution)/shard_map/convert_element_type | solution.py:593
  329.6 4.6 %fusion.3 = f32[1152,1152]{1,0:T(8,128)} fusion(bf16[576,1152]{1,0:T(8,128)(2,1)} %collective-permute-done.20, bf16[576,1152]{1,0:T(8,128)(2,1)S(1)} %maximum_select_fusion.3, pred[]{:T(512)S(6)} %eq.25), kind=kLoop, calls=%fused_computation.10 | loop fusion | flops 13271040 | bytes 7962625 | tf_op jit(solution)/shard_map/convert_element_type | solution.py:593
  334.2 5.3 %collective-permute-done.29 = bf16[160,1152]{1,0:T(8,128)(2,1)S(1)} collective-permute-done((bf16[160,1152]{1,0:T(8,128)(2,1)S(1)}, bf16[160,1152]{1,0:T(8,128)(2,1)S(1)}, u32[]{:S(2)}, u32[]{:S(2)}) %collective-permute-start.29) | collective-permute-done | bytes 368672 | tf_op jit(solution)/shard_map/ppermute | solution.py:318
  347.8 4.6 %finish.1 = (f32[6,144,1152]{2,1,0:T(8,128)}, f32[2,144,1152]{2,1,0:T(8,128)}) custom-call(s32[2]{0:T(128)} %pad_add_fusion.places, bf16[4,160,1152]{2,1,0:T(8,128)(2,1)} %copy-done, bf16[4,160,1152]{2,1,0:T(8,128)(2,1)} %copy-done.2), custom_call_target="tpu_custom_call" | custom-call | tf_op jit(solution)/shard_map/finish/pallas_call | solution.py:355
  353.2 24.2 %reduce-scatter.11.cloned.1.call-done.mixed_grad = bf16[1,192,1152]{2,1,0:T(8,128)(2,1)} async-done(((bf16[4,192,1152]{2,1,0:T(8,128)(2,1)}), bf16[1,192,1152]{2,1,0:T(8,128)(2,1)}) %reduce-scatter.11.cloned.1.call-update) | async-done | bytes 442384 | tf_op jit(solution)/shard_map/reduce_scatter | solution.py:420
  377.4 3.3 shard_map.246
  (199 shorter events, 86.0 us)
Async XLA Ops:
  7.2 47.8 %all-gather.4.cloned.1.call-start = ((), (), s32[]{:S(2)}) async-start(), calls=%async_computation.4 | async-start | bytes 2211840 | tf_op jit(solution)/shard_map/all_gather | solution.py:393
  11.8 103.7 %reduce-scatter.5.cloned.1.call-start = ((), (), s32[]{:S(2)}) async-start(), calls=%async_computation.5 | async-start | bytes 2211840 | tf_op jit(solution)/shard_map/reduce_scatter | solution.py:420
  12.5 6.8 %collective-permute-start.2 = (bf16[1,1280]{1,0:T(2,128)(2,1)S(1)}, bf16[1,1280]{1,0:T(2,128)(2,1)S(1)}, u32[]{:S(2)}, u32[]{:S(2)}) collective-permute-start(bf16[1,1280]{1,0:T(2,128)(2,1)S(1)} %get-tuple-element.204), channel_id=1, source_target_pairs={{0,3},{1,0},{2,1},{3,2},{4,7},{5,4},{6,5},{7,6},{8,11},{9,8},{10,9... | collective-permute-start | bytes 7688 | tf_op jit(solution)/shard_map/ppermute | solution.py:374
  17.7 5.4 %collective-permute-start = (bf16[1,1280]{1,0:T(2,128)(2,1)S(1)}, bf16[1,1280]{1,0:T(2,128)(2,1)S(1)}, u32[]{:S(2)}, u32[]{:S(2)}) collective-permute-start(bf16[1,1280]{1,0:T(2,128)(2,1)S(1)} %get-tuple-element.204), channel_id=1, source_target_pairs={{0,1},{1,2},{2,3},{3,0},{4,5},{5,6},{6,7},{7,4},{8,9},{9,10},{10,1... | collective-permute-start | bytes 7688 | tf_op jit(solution)/shard_map/ppermute | solution.py:374
  67.9 98.1 %all-gather.6.cloned.1.call-start = ((), (), s32[]{:S(2)}) async-start(), calls=%async_computation.6 | async-start | bytes 2211840 | tf_op jit(solution)/shard_map/all_gather | solution.py:393
  68.9 20.2 %collective-permute-start.3 = (bf16[1,192,1152]{2,1,0:T(8,128)(2,1)S(1)}, bf16[1,192,1152]{2,1,0:T(8,128)(2,1)S(1)}, u32[]{:S(2)}, u32[]{:S(2)}) collective-permute-start(bf16[1,192,1152]{2,1,0:T(8,128)(2,1)S(1)} %copy-done.5), channel_id=1, source_target_pairs={{0,1},{1,2},{2,3},{4,5},{5,6},{6,7},{8,9},{9,10},{10,11},{12,13},{... | collective-permute-start | bytes 1327112 | tf_op jit(solution)/shard_map/ppermute | solution.py:401
  71.1 33.1 %collective-permute-start.6 = (bf16[1,192,1152]{2,1,0:T(8,128)(2,1)S(1)}, bf16[1,192,1152]{2,1,0:T(8,128)(2,1)S(1)}, u32[]{:S(2)}, u32[]{:S(2)}) collective-permute-start(bf16[1,192,1152]{2,1,0:T(8,128)(2,1)S(1)} %copy-done.5), channel_id=1, source_target_pairs={{3,2},{2,1},{1,0},{7,6},{6,5},{5,4},{11,10},{10,9},{9,8},{15,14},{... | collective-permute-start | bytes 1327112 | tf_op jit(solution)/shard_map/ppermute | solution.py:402
  89.1 29.5 %collective-permute-start.4 = (bf16[1,192,1152]{2,1,0:T(8,128)(2,1)S(1)}, bf16[1,192,1152]{2,1,0:T(8,128)(2,1)S(1)}, u32[]{:S(2)}, u32[]{:S(2)}) collective-permute-start(bf16[1,192,1152]{2,1,0:T(8,128)(2,1)S(1)} %collective-permute-done.3), channel_id=1, source_target_pairs={{1,2},{2,3},{5,6},{6,7},{9,10},{10,11},{13,14},{14,15},{17,18},{18... | collective-permute-start | bytes 1327112 | tf_op jit(solution)/shard_map/ppermute | solution.py:401
  104.3 17.8 %collective-permute-start.7 = (bf16[1,192,1152]{2,1,0:T(8,128)(2,1)S(1)}, bf16[1,192,1152]{2,1,0:T(8,128)(2,1)S(1)}, u32[]{:S(2)}, u32[]{:S(2)}) collective-permute-start(bf16[1,192,1152]{2,1,0:T(8,128)(2,1)S(1)} %collective-permute-done.6), channel_id=1, source_target_pairs={{2,1},{1,0},{6,5},{5,4},{10,9},{9,8},{14,13},{13,12},{18,17},{17,1... | collective-permute-start | bytes 1327112 | tf_op jit(solution)/shard_map/ppermute | solution.py:402
  118.5 108.2 %reduce-scatter.9.cloned.1.call-start = ((), (), s32[]{:S(2)}) async-start(), calls=%async_computation.8 | async-start | bytes 2211840 | tf_op jit(solution)/shard_map/reduce_scatter | solution.py:420
  118.6 14.0 %collective-permute-start.5 = (bf16[1,192,1152]{2,1,0:T(8,128)(2,1)S(1)}, bf16[1,192,1152]{2,1,0:T(8,128)(2,1)S(1)}, u32[]{:S(2)}, u32[]{:S(2)}) collective-permute-start(bf16[1,192,1152]{2,1,0:T(8,128)(2,1)S(1)} %collective-permute-done.4), channel_id=1, source_target_pairs={{2,3},{6,7},{10,11},{14,15},{18,19},{22,23},{26,27},{30,31}} | collective-permute-start | bytes 1327112 | tf_op jit(solution)/shard_map/ppermute | solution.py:401
  122.1 34.4 %collective-permute-start.8 = (bf16[1,192,1152]{2,1,0:T(8,128)(2,1)S(1)}, bf16[1,192,1152]{2,1,0:T(8,128)(2,1)S(1)}, u32[]{:S(2)}, u32[]{:S(2)}) collective-permute-start(bf16[1,192,1152]{2,1,0:T(8,128)(2,1)S(1)} %collective-permute-done.7), channel_id=1, source_target_pairs={{1,0},{5,4},{9,8},{13,12},{17,16},{21,20},{25,24},{29,28}} | collective-permute-start | bytes 1327112 | tf_op jit(solution)/shard_map/ppermute | solution.py:402
  188.8 80.3 %all-gather.8.cloned.1.call-start = ((), (), s32[]{:S(2)}) async-start(), calls=%async_computation.9 | async-start | bytes 2211840 | tf_op jit(solution)/shard_map/all_gather | solution.py:393
  194.0 17.0 %collective-permute-start.11 = (bf16[288,1152]{1,0:T(8,128)(2,1)S(1)}, bf16[288,1152]{1,0:T(8,128)(2,1)S(1)}, u32[]{:S(2)}, u32[]{:S(2)}) collective-permute-start(bf16[288,1152]{1,0:T(8,128)(2,1)S(1)} %get-tuple-element.193), channel_id=1, source_target_pairs={{0,8},{4,12},{8,0},{12,4},{16,24},{20,28},{24,16},{28,20},{1,9},{5... | collective-permute-start | bytes 1990664 | tf_op jit(solution)/shard_map/ppermute | solution.py:270
  197.2 16.7 %collective-permute-start.12 = (bf16[288,1152]{1,0:T(8,128)(2,1)S(1)}, bf16[288,1152]{1,0:T(8,128)(2,1)S(1)}, u32[]{:S(2)}, u32[]{:S(2)}) collective-permute-start(bf16[288,1152]{1,0:T(8,128)(2,1)S(1)} %get-tuple-element.191), channel_id=1, source_target_pairs={{0,16},{4,20},{8,24},{12,28},{16,0},{20,4},{24,8},{28,12},{1,17},{... | collective-permute-start | bytes 1990664 | tf_op jit(solution)/shard_map/ppermute | solution.py:270
  214.2 10.7 %collective-permute-start.13 = (bf16[144,1152]{1,0:T(8,128)(2,1)S(1)}, bf16[144,1152]{1,0:T(8,128)(2,1)S(1)}, u32[]{:S(2)}, u32[]{:S(2)}) collective-permute-start(bf16[144,1152]{1,0:T(8,128)(2,1)S(1)} %get-tuple-element.197), channel_id=1, source_target_pairs={{0,16},{4,20},{8,24},{12,28},{16,0},{20,4},{24,8},{28,12},{1,17},{... | collective-permute-start | bytes 995336 | tf_op jit(solution)/shard_map/ppermute | solution.py:270
  216.7 8.7 %collective-permute-start.14 = (bf16[144,1152]{1,0:T(8,128)(2,1)}, bf16[144,1152]{1,0:T(8,128)(2,1)S(1)}, u32[]{:S(2)}, u32[]{:S(2)}) collective-permute-start(bf16[144,1152]{1,0:T(8,128)(2,1)} %get-tuple-element.195), channel_id=1, source_target_pairs={{0,8},{4,12},{8,0},{12,4},{16,24},{20,28},{24,16},{28,20},{1,9},{5... | collective-permute-start | bytes 995336 | tf_op jit(solution)/shard_map/ppermute | solution.py:270
  225.6 7.8 %collective-permute-start.15 = (bf16[144,1152]{1,0:T(8,128)(2,1)S(1)}, bf16[144,1152]{1,0:T(8,128)(2,1)S(1)}, u32[]{:S(2)}, u32[]{:S(2)}) collective-permute-start(bf16[144,1152]{1,0:T(8,128)(2,1)S(1)} %add_convert_fusion.6), channel_id=1, source_target_pairs={{0,16},{4,20},{8,24},{12,28},{16,0},{20,4},{24,8},{28,12},{1,17},{... | collective-permute-start | bytes 995336 | tf_op jit(solution)/shard_map/ppermute | solution.py:278
  229.7 81.0 %reduce-scatter.7.cloned.1.call-start = ((), (), s32[]{:S(2)}) async-start(), calls=%async_computation.7 | async-start | bytes 2211840 | tf_op jit(solution)/shard_map/reduce_scatter | solution.py:420
  229.8 9.2 %collective-permute-start.16 = (bf16[144,1152]{1,0:T(8,128)(2,1)S(1)}, bf16[144,1152]{1,0:T(8,128)(2,1)S(1)}, u32[]{:S(2)}, u32[]{:S(2)}) collective-permute-start(bf16[144,1152]{1,0:T(8,128)(2,1)S(1)} %add_convert_fusion.5), channel_id=1, source_target_pairs={{0,8},{4,12},{8,0},{12,4},{16,24},{20,28},{24,16},{28,20},{1,9},{5... | collective-permute-start | bytes 995336 | tf_op jit(solution)/shard_map/ppermute | solution.py:278
  239.2 15.5 %collective-permute-start.17 = (bf16[288,1152]{1,0:T(8,128)(2,1)S(1)}, bf16[288,1152]{1,0:T(8,128)(2,1)S(1)}, u32[]{:S(2)}, u32[]{:S(2)}) collective-permute-start(bf16[288,1152]{1,0:T(8,128)(2,1)S(1)} %maximum_select_fusion.4), channel_id=1, source_target_pairs={{0,8},{4,12},{8,0},{12,4},{16,24},{20,28},{24,16},{28,20},{1,9},{5... | collective-permute-start | bytes 1990664 | tf_op jit(solution)/shard_map/ppermute | solution.py:278
  240.9 15.2 %collective-permute-start.18 = (bf16[288,1152]{1,0:T(8,128)(2,1)S(1)}, bf16[288,1152]{1,0:T(8,128)(2,1)S(1)}, u32[]{:S(2)}, u32[]{:S(2)}) collective-permute-start(bf16[288,1152]{1,0:T(8,128)(2,1)S(1)} %maximum_select_fusion.5), channel_id=1, source_target_pairs={{0,16},{4,20},{8,24},{12,28},{16,0},{20,4},{24,8},{28,12},{1,17},{... | collective-permute-start | bytes 1990664 | tf_op jit(solution)/shard_map/ppermute | solution.py:278
  257.7 119.7 %reduce-scatter.11.cloned.1.call-start = ((), (), s32[]{:S(2)}) async-start(), calls=%async_computation.10 | async-start | bytes 2211840 | tf_op jit(solution)/shard_map/reduce_scatter | solution.py:420
  295.5 9.3 %collective-permute-start.27 = (f32[4,8,216]{2,1,0:T(8,128)S(1)}, f32[4,8,216]{2,1,0:T(8,128)S(1)}, u32[]{:S(2)}, u32[]{:S(2)}) collective-permute-start(f32[4,8,216]{2,1,0:T(8,128)S(1)} %bitcast.154), channel_id=1, source_target_pairs={{0,3},{1,0},{2,1},{3,2},{4,7},{5,4},{6,5},{7,6},{8,11},{9,8},{10,9... | collective-permute-start | bytes 82952 | tf_op jit(solution)/shard_map/ppermute | solution.py:374
  296.8 16.7 %collective-permute-start.26 = (f32[4,8,216]{2,1,0:T(8,128)S(1)}, f32[4,8,216]{2,1,0:T(8,128)}, u32[]{:S(2)}, u32[]{:S(2)}) collective-permute-start(f32[4,8,216]{2,1,0:T(8,128)S(1)} %bitcast.152), channel_id=1, source_target_pairs={{0,2},{1,3},{2,0},{3,1},{4,6},{5,7},{6,4},{7,5},{8,10},{9,11},{10,... | collective-permute-start | bytes 82952 | tf_op jit(solution)/shard_map/ppermute | solution.py:374
  297.5 16.0 %collective-permute-start.25 = (f32[4,8,216]{2,1,0:T(8,128)S(1)}, f32[4,8,216]{2,1,0:T(8,128)}, u32[]{:S(2)}, u32[]{:S(2)}) collective-permute-start(f32[4,8,216]{2,1,0:T(8,128)S(1)} %bitcast.153), channel_id=1, source_target_pairs={{0,1},{1,2},{2,3},{3,0},{4,5},{5,6},{6,7},{7,4},{8,9},{9,10},{10,1... | collective-permute-start | bytes 82952 | tf_op jit(solution)/shard_map/ppermute | solution.py:374
  301.9 12.7 %collective-permute-start.22 = (bf16[144,1152]{1,0:T(8,128)(2,1)}, bf16[144,1152]{1,0:T(8,128)(2,1)}, u32[]{:S(2)}, u32[]{:S(2)}) collective-permute-start(bf16[144,1152]{1,0:T(8,128)(2,1)} %get-tuple-element.189), channel_id=1, source_target_pairs={{0,8},{4,12},{8,0},{12,4},{16,24},{20,28},{24,16},{28,20},{1,9},{5... | collective-permute-start | bytes 995336 | tf_op jit(solution)/shard_map/ppermute | solution.py:318
  303.4 16.5 %collective-permute-start.23 = (bf16[144,1152]{1,0:T(8,128)(2,1)}, bf16[144,1152]{1,0:T(8,128)(2,1)}, u32[]{:S(2)}, u32[]{:S(2)}) collective-permute-start(bf16[144,1152]{1,0:T(8,128)(2,1)} %get-tuple-element.188), channel_id=1, source_target_pairs={{0,16},{4,20},{8,24},{12,28},{16,0},{20,4},{24,8},{28,12},{1,17},{... | collective-permute-start | bytes 995336 | tf_op jit(solution)/shard_map/ppermute | solution.py:318
  304.8 15.0 %collective-permute-start.24 = (bf16[144,1152]{1,0:T(8,128)(2,1)S(1)}, bf16[144,1152]{1,0:T(8,128)(2,1)}, u32[]{:S(2)}, u32[]{:S(2)}) collective-permute-start(bf16[144,1152]{1,0:T(8,128)(2,1)S(1)} %get-tuple-element.187), channel_id=1, source_target_pairs={{0,24},{4,28},{8,16},{12,20},{16,8},{20,12},{24,0},{28,4},{1,25},{... | collective-permute-start | bytes 995336 | tf_op jit(solution)/shard_map/ppermute | solution.py:318
  321.3 12.9 %collective-permute-start.28 = (bf16[160,1152]{1,0:T(8,128)(2,1)S(1)}, bf16[160,1152]{1,0:T(8,128)(2,1)S(1)}, u32[]{:S(2)}, u32[]{:S(2)}) collective-permute-start(bf16[160,1152]{1,0:T(8,128)(2,1)S(1)} %pad_maximum_fusion.3), channel_id=1, source_target_pairs={{0,8},{4,12},{8,0},{12,4},{16,24},{20,28},{24,16},{28,20},{1,9},{5... | collective-permute-start | bytes 1105928 | tf_op jit(solution)/shard_map/ppermute | solution.py:318
  322.5 16.9 %collective-permute-start.29 = (bf16[160,1152]{1,0:T(8,128)(2,1)S(1)}, bf16[160,1152]{1,0:T(8,128)(2,1)S(1)}, u32[]{:S(2)}, u32[]{:S(2)}) collective-permute-start(bf16[160,1152]{1,0:T(8,128)(2,1)S(1)} %pad_maximum_fusion.3), channel_id=1, source_target_pairs={{0,16},{4,20},{8,24},{12,28},{16,0},{20,4},{24,8},{28,12},{1,17},{... | collective-permute-start | bytes 1105928 | tf_op jit(solution)/shard_map/ppermute | solution.py:318
  323.3 16.1 %collective-permute-start.30 = (bf16[160,1152]{1,0:T(8,128)(2,1)S(1)}, bf16[160,1152]{1,0:T(8,128)(2,1)S(1)}, u32[]{:S(2)}, u32[]{:S(2)}) collective-permute-start(bf16[160,1152]{1,0:T(8,128)(2,1)S(1)} %pad_maximum_fusion.3), channel_id=1, source_target_pairs={{0,24},{4,28},{8,16},{12,20},{16,8},{20,12},{24,0},{28,4},{1,25},{... | collective-permute-start | bytes 1105928 | tf_op jit(solution)/shard_map/ppermute | solution.py:318
  (28 other events, 206.8 us)
Sparse Core Ops, SparseCore 0:
  11.9 43.0 all-gather.3
  68.0 47.4 reduce-scatter.4
  118.6 45.9 all-gather.5
  188.9 37.6 reduce-scatter.8
  229.8 39.2 all-gather.7
  271.3 39.4 reduce-scatter.6
  339.9 37.4 reduce-scatter.10

commit v6 on v5

--- a/solution.py
+++ b/solution.py
@@ -61,6 +61,46 @@
         scratch_shapes=list(scratch),
         out_shape=[jax.ShapeDtypeStruct(shape, dtype) for shape, dtype in outs],
     )(*[a for a, _ in ins])
+
+
+def split_call(body, start, images, group, own_ins, group_ins, outs, fixed=(), scratch=()):
+    start = jnp.full((1,), start, jnp.int32)
+    shapes = [jax.ShapeDtypeStruct(shape, dtype) for shape, dtype in outs]
+    apart = [jax.ShapeDtypeStruct(shape, dtype) for shape, dtype in fixed]
+
+    def at(shape, first, moving):
+        rest = (0,) * (len(shape) - 1)
+
+        def place(i, p):
+            return ((p[0] + first + i) % group if moving else i,) + rest
+
+        return pl.BlockSpec((1,) + tuple(shape[1:]), place)
+
+    def full(shape):
+        return pl.BlockSpec(tuple(shape), lambda i, p: (0,) * len(shape))
+
+    def run(ins, first, count, filled, moving):
+        def step(index, *refs):
+            body(*refs[: len(ins)], *refs[len(ins) + len(filled) :])
+
+        return pl.pallas_call(
+            step,
+            grid_spec=pltpu.PrefetchScalarGridSpec(
+                num_scalar_prefetch=1,
+                grid=(count,),
+                in_specs=[at(a.shape, first, moving) if by else full(a.shape) for a, by in ins]
+                + [pl.BlockSpec(memory_space=pl.ANY)] * len(filled),
+                out_specs=[at(one.shape, first, True) for one in shapes]
+                + [full(one.shape) for one in apart],
+                scratch_shapes=list(scratch),
+            ),
+            out_shape=shapes + apart,
+            input_output_aliases={1 + len(ins) + i: i for i in range(len(filled))},
+        )(start, *[a for a, _ in ins], *filled)
+
+    own = run(own_ins, 0, images, [], False)
+    rest = run(group_ins, images, group - images, own[: len(shapes)], True)
+    return list(rest[: len(shapes)]) + [(a, b) for a, b in zip(own[len(shapes) :], rest[len(shapes) :])]
 
 
 def gather_body(picks, tokens, cotangent, routed, grad_two):
@@ -121,11 +161,12 @@
 
 def attend_back_body(
     head_dim, grad, qkv, routed, mixed, attended, keep, weight, out_weight,
-    mixed_grad, stats, bias_sums, part, total,
+    mixed_grad, stats, bias_sums, part, kept,
 ):
     slots, cols = routed.shape[1], weight.shape[1]
     scale = 1.0 / math.sqrt(head_dim)
-    rows_grad = grad[0]
+    here = pl.ds(pl.multiple_of(pl.program_id(0) * slots, slots), slots)
+    rows_grad = grad[here, :]
     attended_grad = mm(rows_grad, out_weight[...], NT).astype(BF16)
     query, key, value = qkv[0, 0], qkv[0, 1], qkv[0, 2]
     alive = live_keys(keep, slots)
@@ -146,21 +187,8 @@
     query_grad = (query_grad * scale).astype(BF16)
     key_grad = (key_grad * scale).astype(BF16)
     value_grad = value_grad.astype(BF16)
-    step = pl.program_id(0)
-
-    @pl.when(step == 0)
-    def _():
-        total[...] = jnp.zeros_like(total)
-
-    total[0] += mm(query_grad, mixed[0], TN)
-    total[1] += mm(key_grad, mixed[0], TN)
-    total[2] += mm(value_grad, mixed[0], TN)
-    total[3] += mm(attended[0], rows_grad, TN)
-
-    @pl.when(step == pl.num_programs(0) - 1)
-    def _():
-        part[...] = total[...].astype(BF16)
-
+    for index, one in enumerate((query_grad, key_grad, value_grad)):
+        kept[index, here, :] = one
     rows = mm(query_grad, weight[0]) + mm(key_grad, weight[1]) + mm(value_grad, weight[2])
     mixed_grad[0] = rows.astype(BF16)
     normed, _ = norm_rows(routed[0].astype(F32))
@@ -169,6 +197,12 @@
     stats[0, 2:3, :] = jnp.sum(rows_grad.astype(F32), axis=0, keepdims=True)
     bias_sums[0, 0:1, :] = jnp.sum(query_grad.astype(F32), axis=0, keepdims=True)
     bias_sums[0, 1:2, :] = jnp.sum(value_grad.astype(F32), axis=0, keepdims=True)
+
+    @pl.when(pl.program_id(0) == pl.num_programs(0) - 1)
+    def _():
+        for index in range(3):
+            part[index] = mm(kept[index], mixed[...], TN).astype(BF16)
+        part[3] = mm(attended[...], grad[...], TN).astype(BF16)
 
 
 def down_back_body(grad_two, mod, keep, down, down_grad, active_grad, down_sum):
@@ -469,12 +503,12 @@
     out_bias_row = out_bias.astype(F32)[None]
     down_bias_row = down_bias.astype(F32)[None]
 
-    mixed_one, qkv, attended, branch = call(
-        functools.partial(attend_body, head_dim), group,
-        [
-            (group_routed, True), (modulation, True), (keep, True), (qkv_weight, False),
-            (qv_bias.astype(F32), False), (out_weight, False),
-        ],
+    first_image = here * images
+    fixed_ins = [(qkv_weight, False), (qv_bias.astype(F32), False), (out_weight, False)]
+    mixed_one, qkv, attended, branch = split_call(
+        functools.partial(attend_body, head_dim), first_image, images, group,
+        [(routed, True), (own_mod, True), (own_keep, True)] + fixed_ins,
+        [(group_routed, True), (modulation, True), (keep, True)] + fixed_ins,
         [
             (group_shape, BF16), ((group, 3, slots, cols), BF16), ((group, slots, cols), BF16),
             (group_shape, BF16),
@@ -498,12 +532,12 @@
         [(group_two, True), (modulation, True), (keep, True), (down_weight, False)],
         [(group_shape, BF16), (unit_shape, F32), ((group, 1, width), F32)],
     )
-    active, before_grad, mixed_grad, up_sum = call(
-        forward_body, group,
-        [
-            (group_mixed, True), (active_grad, True), (up_weight, False),
-            (up_bias.astype(F32)[None], False),
-        ],
+    own_active_grad = lax.dynamic_slice_in_dim(active_grad, first_image, images, 0)
+    fixed_ins = [(up_weight, False), (up_bias.astype(F32)[None], False)]
+    active, before_grad, mixed_grad, up_sum = split_call(
+        forward_body, first_image, images, group,
+        [(mixed_two, True), (own_active_grad, True)] + fixed_ins,
+        [(group_mixed, True), (active_grad, True)] + fixed_ins,
         [
             (unit_shape, BF16), (unit_shape, BF16), (group_shape, BF16),
             ((group, 1, hidden_units), F32),
@@ -544,16 +578,16 @@
     mixed_grad, attend_stats, bias_sums, part = call(
         functools.partial(attend_back_body, head_dim), group,
         [
-            (group_grad, True), (qkv, True), (group_routed, True), (mixed_one, True),
-            (attended, True), (after(keep, last), True),
-            (qkv_weight, False), (out_weight, False),
+            (group_grad.reshape(wide), False), (qkv, True), (group_routed, True),
+            (mixed_one.reshape(wide), False), (attended.reshape(-1, cols), False),
+            (after(keep, last), True), (qkv_weight, False), (out_weight, False),
         ],
         [
             (group_shape, BF16), ((group, 3, width), F32), ((group, 2, cols), F32),
             ((4, cols, width), BF16),
         ],
         fixed=1,
-        scratch=[pltpu.VMEM((4, cols, width), F32)],
+        scratch=[pltpu.VMEM((3, group * slots, cols), BF16)],
     )
     (layer_out,) = call(
         out_body, images,

time: 389 us -> 391 us (level); the launches traced: 388 us -> 384 us
  waiting for transfers between devices: 183 us -> 171 us
  Pallas kernels: 78.2 us -> 83.4 us
    pallas_call x0 -> x4, Pallas kernels: none -> 31.1 us  [run(): pl.pallas_call(step, grid_spec=pltpu.PrefetchScalarGridSpec(num_scalar_pr...]
    pallas_call x9 -> x7, Pallas kernels: 73.6 us -> 47.7 us  [call(): pl.pallas_call(body, grid=(grid,), in_specs=[block(a.shape) if step else...]
    ppermute x3, waiting for transfers between devices: 41.3 us -> 30.4 us  [chain_rows(): lax.ppermute(down, 'mp', [(i, i - 1) for i in range(count - hop, 0, -1)])]
    reduce_scatter x4, waiting for transfers between devices: 37.7 us -> 27.4 us  [own_sum(): return lax.psum_scatter(rows, 'mp', scatter_dimension=0, tiled=True)]
    all_gather x3, waiting for transfers between devices: 27.5 us -> 37.6 us  [all_rows(): return lax.all_gather(rows, 'mp', axis=0, tiled=True)]
  transfers between devices with their start and end apart: 39 -> 39, of which waited for: 25 -> 22; matrix products, arithmetic and copies ran while one was open for 14% -> 15% of each run, Pallas kernels for 12% -> 15%
where the time goes in v6:
time: 391 us; the launch traced here: 384 us
  waiting for transfers between devices  171 us (44%)
  Pallas kernels  83.4 us (21%)
  starting transfers between devices  37.5 us (10%)
  other arithmetic  26.3 us (7%)
  local copies, waits for them, and re-layouts  24.9 us (6%)
  between operations  23.3 us (6%)
  matrix products  17.6 us (5%)
    pallas_call x7, Pallas kernels, call(): pl.pallas_call(body, grid=(grid,), in_specs=[block(a.shape) if step else...  47.7 us
    all_gather x3, waiting for transfers between devices, all_rows(): return lax.all_gather(rows, 'mp', axis=0, tiled=True)  37.6 us
    pallas_call x4, Pallas kernels, run(): pl.pallas_call(step, grid_spec=pltpu.PrefetchScalarGridSpec(num_scalar_pr...  31.1 us
    ppermute x3, waiting for transfers between devices, chain_rows(): lax.ppermute(down, 'mp', [(i, i - 1) for i in range(count - hop, 0, -1)])  30.4 us
    reduce_scatter x4, waiting for transfers between devices, own_sum(): return lax.psum_scatter(rows, 'mp', scatter_dimension=0, tiled=True)  27.4 us
    ppermute x7, waiting for transfers between devices, double(): return (part, lax.ppermute(part, 'dp', partner(bit)))  27.3 us
    ppermute x7, waiting for transfers between devices, halve(): return (own, lax.ppermute(other, 'dp', partner(bit)))  18.9 us
    dot_general x4, matrix products, mm(): lax.dot_general(left, right, (dims, ((), ())), preferred_element_type=F32)  17.6 us
  transfers between devices with their start and end apart: 39, of which 22 were waited for; matrix products, arithmetic and copies ran while one was open for 15% of the time, Pallas kernels for 15%

profile of v6, /device:TPU:0, one launch (start us, length us, event | category | flops | bytes accessed | tf_op | source)
XLA Modules:
  0.0 383.9 jit_solution(6698200567174251305)
XLA Ops:
  12.6 3.1 collective-permute-start
  22.6 9.8 %convolution_add_fusion = f32[4,6912]{1,0:T(4,128)S(1)} fusion(bf16[6912,1152]{1,0:T(8,128)(2,1)} %param.20, f32[6912]{0:T(1024)S(1)} %convert_element_type.167, bf16[4,1280]{1,0:T(4,128)(2,1)S(1)} %broadcast_select_fusion), kind=kOutput, calls=%fused_computation.4 | convolution fusion | flops 63756288 | bytes 16073728 | tf_op jit(solution)/shard_map/dot_general | solution.py:36
  33.7 5.2 %shard_map.239 = (bf16[4,192,1152]{2,1,0:T(8,128)(2,1)}, bf16[4,3,192,288]{3,2,1,0:T(8,128)(2,1)}, bf16[4,192,288]{2,1,0:T(8,128)(2,1)}, bf16[4,192,1152]{2,1,0:T(8,128)(2,1)}) custom-call(s32[1]{0:T(128)} %bitcast.index, bf16[1,192,1152]{2,1,0:T(8,128)(2,1)} %get-tuple-element.98.refs_0_.routed, f32[1,6,1152]{2,1,0:T(8,128)} %constant_dynamic-slice_fusion.6.refs_1_.mod, ...), custom_call_target="tpu_custom_call" | custom-call | tf_op jit(solution)/shard_map/pallas_call | solution.py:86
  39.5 15.5 %all-gather.4.cloned.1.call-done.refs_0_.routed = bf16[4,192,1152]{2,1,0:T(8,128)(2,1)} async-done(((bf16[1,192,1152]{2,1,0:T(8,128)(2,1)}), bf16[4,192,1152]{2,1,0:T(8,128)(2,1)}) %all-gather.4.cloned.1.call-update) | async-done | bytes 1769488 | tf_op jit(solution)/shard_map/all_gather | solution.py:427
  55.0 10.4 %shard_map.240 = (bf16[4,192,1152]{2,1,0:T(8,128)(2,1)}, bf16[4,3,192,288]{3,2,1,0:T(8,128)(2,1)}, bf16[4,192,288]{2,1,0:T(8,128)(2,1)}, bf16[4,192,1152]{2,1,0:T(8,128)(2,1)}) custom-call(s32[1]{0:T(128)} %bitcast.index, ...), custom_call_target="tpu_custom_call", output_to_operand_aliasing={{0}: (7, {}), {1}: (8, {}), {2}: (9, {}), {3}: (10, {})} | custom-call | tf_op jit(solution)/shard_map/pallas_call | solution.py:86
  70.1 16.6 %collective-permute-done.3 = bf16[1,192,1152]{2,1,0:T(8,128)(2,1)S(1)} collective-permute-done((bf16[1,192,1152]{2,1,0:T(8,128)(2,1)S(1)}, bf16[1,192,1152]{2,1,0:T(8,128)(2,1)S(1)}, u32[]{:S(2)}, u32[]{:S(2)}) %collective-permute-start.3) | collective-permute-done | bytes 442400 | tf_op jit(solution)/shard_map/ppermute | solution.py:435
  87.4 14.6 %collective-permute-done.6 = bf16[1,192,1152]{2,1,0:T(8,128)(2,1)S(1)} collective-permute-done((bf16[1,192,1152]{2,1,0:T(8,128)(2,1)S(1)}, bf16[1,192,1152]{2,1,0:T(8,128)(2,1)S(1)}, u32[]{:S(2)}, u32[]{:S(2)}) %collective-permute-start.6) | collective-permute-done | bytes 442400 | tf_op jit(solution)/shard_map/ppermute | solution.py:436
  103.9 15.8 %collective-permute-done.7 = bf16[1,192,1152]{2,1,0:T(8,128)(2,1)S(1)} collective-permute-done((bf16[1,192,1152]{2,1,0:T(8,128)(2,1)S(1)}, bf16[1,192,1152]{2,1,0:T(8,128)(2,1)S(1)}, u32[]{:S(2)}, u32[]{:S(2)}) %collective-permute-start.7) | collective-permute-done | bytes 442400 | tf_op jit(solution)/shard_map/ppermute | solution.py:436
  135.5 7.4 %shard_map.242 = (bf16[4,192,1152]{2,1,0:T(8,128)(2,1)}, f32[4,192,1152]{2,1,0:T(8,128)}, f32[4,1,1152]{2,1,0:T(1,128)}) custom-call(bf16[4,192,1152]{2,1,0:T(8,128)(2,1)} %pad_maximum_fusion.1.grad_two, f32[4,6,1152]{2,1,0:T(8,128)} %copy-done.7, f32[4,1,128]{2,1,0:T(1,128)} %bitcast.156, bf16[1152,1152]{1,0:T(8,128)(2,1)} %down.3), custom_call_target="tpu_custom_call" | custom-call | tf_op jit(solution)/shard_map/pallas_call | solution.py:55
  145.1 5.2 %shard_map.243 = (bf16[4,192,1152]{2,1,0:T(8,128)(2,1)}, bf16[4,192,1152]{2,1,0:T(8,128)(2,1)}, bf16[4,192,1152]{2,1,0:T(8,128)(2,1)}, f32[4,1,1152]{2,1,0:T(1,128)}) custom-call(s32[1]{0:T(128)} %bitcast.index, bf16[1,192,1152]{2,1,0:T(8,128)(2,1)} %get-tuple-element.104.refs_0_, f32[1,192,1152]{2,1,0:T(8,128)} %constant_dynamic-slice_fusion.5.refs_1_, ...), custom_call_target="tpu_custom_call" | custom-call | tf_op jit(solution)/shard_map/pallas_call | solution.py:86
  150.3 14.5 %all-gather.6.cloned.1.call-done.refs_0_ = bf16[4,192,1152]{2,1,0:T(8,128)(2,1)} async-done(((bf16[1,192,1152]{2,1,0:T(8,128)(2,1)}), bf16[4,192,1152]{2,1,0:T(8,128)(2,1)}) %all-gather.6.cloned.1.call-update) | async-done | bytes 1769488 | tf_op jit(solution)/shard_map/all_gather | solution.py:427
  164.8 10.2 %shard_map.244 = (bf16[4,192,1152]{2,1,0:T(8,128)(2,1)}, bf16[4,192,1152]{2,1,0:T(8,128)(2,1)}, bf16[4,192,1152]{2,1,0:T(8,128)(2,1)}, f32[4,1,1152]{2,1,0:T(1,128)}) custom-call(s32[1]{0:T(128)} %bitcast.index, bf16[4,192,1152]{2,1,0:T(8,128)(2,1)} %all-gather.6.cloned.1.call-done.refs_0_, ...), custom_call_target="tpu_custom_call", output_to_operand_aliasing={{0}: (5, {}), {1}: (6, {}), {2}: (7, {}), {3}: (8, {})} | custom-call | tf_op jit(solution)/shard_map/pallas_call | solution.py:86
  175.0 4.0 %fusion.1 = bf16[1152,1152]{1,0:T(8,128)(2,1)S(1)} fusion(bf16[4,192,1152]{2,1,0:T(8,128)(2,1)} %get-tuple-element.118.active, bf16[4,192,1152]{2,1,0:T(8,128)(2,1)S(1)} %copy-done.21), kind=kOutput, calls=%fused_computation.6 | convolution fusion | flops 2039758848 | bytes 6193152 | tf_op jit(solution)/shard_map/dot_general | solution.py:36
  185.6 3.1 collective-permute-done.9
  195.3 12.2 %collective-permute-done.12 = bf16[288,1152]{1,0:T(8,128)(2,1)S(1)} collective-permute-done((bf16[288,1152]{1,0:T(8,128)(2,1)S(1)}, bf16[288,1152]{1,0:T(8,128)(2,1)S(1)}, u32[]{:S(2)}, u32[]{:S(2)}) %collective-permute-start.12) | collective-permute-done | bytes 663584 | tf_op jit(solution)/shard_map/ppermute | solution.py:304
  207.5 3.0 collective-permute-done.11
  214.5 7.0 %shard_map.245 = (bf16[4,192,1152]{2,1,0:T(8,128)(2,1)}, f32[4,1,1152]{2,1,0:T(1,128)}) custom-call(bf16[4,192,1152]{2,1,0:T(8,128)(2,1)} %get-tuple-element.118.active, bf16[4,192,1152]{2,1,0:T(8,128)(2,1)} %pad_maximum_fusion.1.grad_two, f32[4,1,128]{2,1,0:T(1,128)} %bitcast.157, bf16[1152,1152]{1,0:T(8,128)(2,1)} %down.3, f32[1,1152]{1,0:T(1,128)} %select_n.242.bias), custom_call_target="tpu_custom_call" | custom-call | tf_op jit(solution)/shard_map/pallas_call | solution.py:55
  223.8 2.9 shard_map.249
  227.8 3.0 collective-permute-done.16
  230.8 4.5 %collective-permute-done.15 = bf16[144,1152]{1,0:T(8,128)(2,1)S(1)} collective-permute-done((bf16[144,1152]{1,0:T(8,128)(2,1)S(1)}, bf16[144,1152]{1,0:T(8,128)(2,1)S(1)}, u32[]{:S(2)}, u32[]{:S(2)}) %collective-permute-start.15) | collective-permute-done | bytes 331808 | tf_op jit(solution)/shard_map/ppermute | solution.py:312
  238.7 11.8 %collective-permute-done.18 = bf16[288,1152]{1,0:T(8,128)(2,1)S(1)} collective-permute-done((bf16[288,1152]{1,0:T(8,128)(2,1)S(1)}, bf16[288,1152]{1,0:T(8,128)(2,1)S(1)}, u32[]{:S(2)}, u32[]{:S(2)}) %collective-permute-start.18) | collective-permute-done | bytes 663584 | tf_op jit(solution)/shard_map/ppermute | solution.py:312
  257.8 7.6 %all-gather.8.cloned.1.call-done = bf16[4,192,1152]{2,1,0:T(8,128)(2,1)} async-done(((bf16[1,192,1152]{2,1,0:T(8,128)(2,1)}), bf16[4,192,1152]{2,1,0:T(8,128)(2,1)}) %all-gather.8.cloned.1.call-update) | async-done | bytes 1769488 | tf_op jit(solution)/shard_map/all_gather | solution.py:427
  265.4 22.1 %shard_map.246 = (bf16[4,192,1152]{2,1,0:T(8,128)(2,1)}, f32[4,3,1152]{2,1,0:T(4,128)}, f32[4,2,288]{2,1,0:T(2,128)}, bf16[4,288,1152]{2,1,0:T(8,128)(2,1)}) custom-call(bf16[768,1152]{1,0:T(8,128)(2,1)} %bitcast.148, bf16[4,3,192,288]{3,2,1,0:T(8,128)(2,1)} %get-tuple-element.132.qkv, bf16[4,192,1152]{2,1,0:T(8,128)(2,1)} %all-gather.4.cloned.1.call-done.refs_0_.routed, ...), custom_call_target="tpu_custom_call" | custom-call | tf_op jit(solution)/shard_map/pallas_call | solution.py:55
  303.1 4.0 %reduce-scatter.7.cloned.1.call-done.branch = bf16[1,192,1152]{2,1,0:T(8,128)(2,1)} async-done(((bf16[4,192,1152]{2,1,0:T(8,128)(2,1)}), bf16[1,192,1152]{2,1,0:T(8,128)(2,1)}) %reduce-scatter.7.cloned.1.call-update) | async-done | bytes 442384 | tf_op jit(solution)/shard_map/reduce_scatter | solution.py:454
  307.1 2.8 shard_map.247
  311.0 5.8 %collective-permute-done.23 = bf16[144,1152]{1,0:T(8,128)(2,1)} collective-permute-done((bf16[144,1152]{1,0:T(8,128)(2,1)}, bf16[144,1152]{1,0:T(8,128)(2,1)}, u32[]{:S(2)}, u32[]{:S(2)}) %collective-permute-start.23) | collective-permute-done | bytes 331808 | tf_op jit(solution)/shard_map/ppermute | solution.py:352
  321.7 4.6 %fusion.3 = f32[1152,1152]{1,0:T(8,128)} fusion(bf16[576,1152]{1,0:T(8,128)(2,1)} %collective-permute-done.20, bf16[576,1152]{1,0:T(8,128)(2,1)S(1)} %maximum_select_fusion.3, pred[]{:T(512)S(6)} %eq.25), kind=kLoop, calls=%fused_computation.10 | loop fusion | flops 13271040 | bytes 7962625 | tf_op jit(solution)/shard_map/convert_element_type | solution.py:627
  326.3 4.8 %fusion.2 = f32[1152,1152]{1,0:T(8,128)} fusion(bf16[576,1152]{1,0:T(8,128)(2,1)} %collective-permute-done.19, bf16[576,1152]{1,0:T(8,128)(2,1)S(1)} %maximum_select_fusion.2, pred[]{:T(512)S(6)} %eq.25), kind=kLoop, calls=%fused_computation.8 | loop fusion | flops 13271040 | bytes 7962625 | tf_op jit(solution)/shard_map/convert_element_type | solution.py:627
  331.1 5.2 %collective-permute-done.29 = bf16[160,1152]{1,0:T(8,128)(2,1)S(1)} collective-permute-done((bf16[160,1152]{1,0:T(8,128)(2,1)S(1)}, bf16[160,1152]{1,0:T(8,128)(2,1)S(1)}, u32[]{:S(2)}, u32[]{:S(2)}) %collective-permute-start.29) | collective-permute-done | bytes 368672 | tf_op jit(solution)/shard_map/ppermute | solution.py:352
  344.7 4.6 %finish.1 = (f32[6,144,1152]{2,1,0:T(8,128)}, f32[2,144,1152]{2,1,0:T(8,128)}) custom-call(s32[2]{0:T(128)} %pad_add_fusion.places, bf16[4,160,1152]{2,1,0:T(8,128)(2,1)} %copy-done, bf16[4,160,1152]{2,1,0:T(8,128)(2,1)} %copy-done.2), custom_call_target="tpu_custom_call" | custom-call | tf_op jit(solution)/shard_map/finish/pallas_call | solution.py:389
  350.1 23.4 %reduce-scatter.11.cloned.1.call-done.mixed_grad = bf16[1,192,1152]{2,1,0:T(8,128)(2,1)} async-done(((bf16[4,192,1152]{2,1,0:T(8,128)(2,1)}), bf16[1,192,1152]{2,1,0:T(8,128)(2,1)}) %reduce-scatter.11.cloned.1.call-update) | async-done | bytes 442384 | tf_op jit(solution)/shard_map/reduce_scatter | solution.py:454
  373.5 3.3 shard_map.248
  (204 shorter events, 92.5 us)
Async XLA Ops:
  7.2 47.8 %all-gather.4.cloned.1.call-start = ((), (), s32[]{:S(2)}) async-start(), calls=%async_computation.4 | async-start | bytes 2211840 | tf_op jit(solution)/shard_map/all_gather | solution.py:427
  11.8 109.8 %reduce-scatter.5.cloned.1.call-start = ((), (), s32[]{:S(2)}) async-start(), calls=%async_computation.5 | async-start | bytes 2211840 | tf_op jit(solution)/shard_map/reduce_scatter | solution.py:454
  12.6 7.7 %collective-permute-start = (bf16[1,1280]{1,0:T(2,128)(2,1)S(1)}, bf16[1,1280]{1,0:T(2,128)(2,1)S(1)}, u32[]{:S(2)}, u32[]{:S(2)}) collective-permute-start(bf16[1,1280]{1,0:T(2,128)(2,1)S(1)} %get-tuple-element.220), channel_id=1, source_target_pairs={{0,1},{1,2},{2,3},{3,0},{4,5},{5,6},{6,7},{7,4},{8,9},{9,10},{10,1... | collective-permute-start | bytes 7688 | tf_op jit(solution)/shard_map/ppermute | solution.py:408
  65.5 99.3 %all-gather.6.cloned.1.call-start = ((), (), s32[]{:S(2)}) async-start(), calls=%async_computation.6 | async-start | bytes 2211840 | tf_op jit(solution)/shard_map/all_gather | solution.py:427
  66.4 20.3 %collective-permute-start.3 = (bf16[1,192,1152]{2,1,0:T(8,128)(2,1)S(1)}, bf16[1,192,1152]{2,1,0:T(8,128)(2,1)S(1)}, u32[]{:S(2)}, u32[]{:S(2)}) collective-permute-start(bf16[1,192,1152]{2,1,0:T(8,128)(2,1)S(1)} %copy-done.3), channel_id=1, source_target_pairs={{0,1},{1,2},{2,3},{4,5},{5,6},{6,7},{8,9},{9,10},{10,11},{12,13},{... | collective-permute-start | bytes 1327112 | tf_op jit(solution)/shard_map/ppermute | solution.py:435
  68.8 33.2 %collective-permute-start.6 = (bf16[1,192,1152]{2,1,0:T(8,128)(2,1)S(1)}, bf16[1,192,1152]{2,1,0:T(8,128)(2,1)S(1)}, u32[]{:S(2)}, u32[]{:S(2)}) collective-permute-start(bf16[1,192,1152]{2,1,0:T(8,128)(2,1)S(1)} %copy-done.3), channel_id=1, source_target_pairs={{3,2},{2,1},{1,0},{7,6},{6,5},{5,4},{11,10},{10,9},{9,8},{15,14},{... | collective-permute-start | bytes 1327112 | tf_op jit(solution)/shard_map/ppermute | solution.py:436
  86.7 16.5 %collective-permute-start.4 = (bf16[1,192,1152]{2,1,0:T(8,128)(2,1)S(1)}, bf16[1,192,1152]{2,1,0:T(8,128)(2,1)S(1)}, u32[]{:S(2)}, u32[]{:S(2)}) collective-permute-start(bf16[1,192,1152]{2,1,0:T(8,128)(2,1)S(1)} %collective-permute-done.3), channel_id=1, source_target_pairs={{1,2},{2,3},{5,6},{6,7},{9,10},{10,11},{13,14},{14,15},{17,18},{18... | collective-permute-start | bytes 1327112 | tf_op jit(solution)/shard_map/ppermute | solution.py:435
  101.9 17.8 %collective-permute-start.7 = (bf16[1,192,1152]{2,1,0:T(8,128)(2,1)S(1)}, bf16[1,192,1152]{2,1,0:T(8,128)(2,1)S(1)}, u32[]{:S(2)}, u32[]{:S(2)}) collective-permute-start(bf16[1,192,1152]{2,1,0:T(8,128)(2,1)S(1)} %collective-permute-done.6), channel_id=1, source_target_pairs={{2,1},{1,0},{6,5},{5,4},{10,9},{9,8},{14,13},{13,12},{18,17},{17,1... | collective-permute-start | bytes 1327112 | tf_op jit(solution)/shard_map/ppermute | solution.py:436
  103.2 30.2 %collective-permute-start.5 = (bf16[1,192,1152]{2,1,0:T(8,128)(2,1)S(1)}, bf16[1,192,1152]{2,1,0:T(8,128)(2,1)S(1)}, u32[]{:S(2)}, u32[]{:S(2)}) collective-permute-start(bf16[1,192,1152]{2,1,0:T(8,128)(2,1)S(1)} %collective-permute-done.4), channel_id=1, source_target_pairs={{2,3},{6,7},{10,11},{14,15},{18,19},{22,23},{26,27},{30,31}} | collective-permute-start | bytes 1327112 | tf_op jit(solution)/shard_map/ppermute | solution.py:435
  119.7 13.7 %collective-permute-start.8 = (bf16[1,192,1152]{2,1,0:T(8,128)(2,1)S(1)}, bf16[1,192,1152]{2,1,0:T(8,128)(2,1)S(1)}, u32[]{:S(2)}, u32[]{:S(2)}) collective-permute-start(bf16[1,192,1152]{2,1,0:T(8,128)(2,1)S(1)} %collective-permute-done.7), channel_id=1, source_target_pairs={{1,0},{5,4},{9,8},{13,12},{17,16},{21,20},{25,24},{29,28}} | collective-permute-start | bytes 1327112 | tf_op jit(solution)/shard_map/ppermute | solution.py:436
  124.1 99.6 %reduce-scatter.9.cloned.1.call-start = ((), (), s32[]{:S(2)}) async-start(), calls=%async_computation.8 | async-start | bytes 2211840 | tf_op jit(solution)/shard_map/reduce_scatter | solution.py:454
  185.4 80.1 %all-gather.8.cloned.1.call-start = ((), (), s32[]{:S(2)}) async-start(), calls=%async_computation.9 | async-start | bytes 2211840 | tf_op jit(solution)/shard_map/all_gather | solution.py:427
  190.5 17.0 %collective-permute-start.12 = (bf16[288,1152]{1,0:T(8,128)(2,1)S(1)}, bf16[288,1152]{1,0:T(8,128)(2,1)S(1)}, u32[]{:S(2)}, u32[]{:S(2)}) collective-permute-start(bf16[288,1152]{1,0:T(8,128)(2,1)S(1)} %get-tuple-element.207), channel_id=1, source_target_pairs={{0,16},{4,20},{8,24},{12,28},{16,0},{20,4},{24,8},{28,12},{1,17},{... | collective-permute-start | bytes 1990664 | tf_op jit(solution)/shard_map/ppermute | solution.py:304
  193.8 16.7 %collective-permute-start.11 = (bf16[288,1152]{1,0:T(8,128)(2,1)S(1)}, bf16[288,1152]{1,0:T(8,128)(2,1)S(1)}, u32[]{:S(2)}, u32[]{:S(2)}) collective-permute-start(bf16[288,1152]{1,0:T(8,128)(2,1)S(1)} %get-tuple-element.209), channel_id=1, source_target_pairs={{0,8},{4,12},{8,0},{12,4},{16,24},{20,28},{24,16},{28,20},{1,9},{5... | collective-permute-start | bytes 1990664 | tf_op jit(solution)/shard_map/ppermute | solution.py:304
  210.8 10.7 %collective-permute-start.14 = (bf16[144,1152]{1,0:T(8,128)(2,1)S(1)}, bf16[144,1152]{1,0:T(8,128)(2,1)}, u32[]{:S(2)}, u32[]{:S(2)}) collective-permute-start(bf16[144,1152]{1,0:T(8,128)(2,1)S(1)} %get-tuple-element.211), channel_id=1, source_target_pairs={{0,8},{4,12},{8,0},{12,4},{16,24},{20,28},{24,16},{28,20},{1,9},{5... | collective-permute-start | bytes 995336 | tf_op jit(solution)/shard_map/ppermute | solution.py:304
  213.3 8.7 %collective-permute-start.13 = (bf16[144,1152]{1,0:T(8,128)(2,1)}, bf16[144,1152]{1,0:T(8,128)(2,1)S(1)}, u32[]{:S(2)}, u32[]{:S(2)}) collective-permute-start(bf16[144,1152]{1,0:T(8,128)(2,1)} %get-tuple-element.213), channel_id=1, source_target_pairs={{0,16},{4,20},{8,24},{12,28},{16,0},{20,4},{24,8},{28,12},{1,17},{... | collective-permute-start | bytes 995336 | tf_op jit(solution)/shard_map/ppermute | solution.py:304
  223.1 7.7 %collective-permute-start.16 = (bf16[144,1152]{1,0:T(8,128)(2,1)S(1)}, bf16[144,1152]{1,0:T(8,128)(2,1)S(1)}, u32[]{:S(2)}, u32[]{:S(2)}) collective-permute-start(bf16[144,1152]{1,0:T(8,128)(2,1)S(1)} %add_convert_fusion.5), channel_id=1, source_target_pairs={{0,8},{4,12},{8,0},{12,4},{16,24},{20,28},{24,16},{28,20},{1,9},{5... | collective-permute-start | bytes 995336 | tf_op jit(solution)/shard_map/ppermute | solution.py:312
  226.7 80.4 %reduce-scatter.7.cloned.1.call-start = ((), (), s32[]{:S(2)}) async-start(), calls=%async_computation.7 | async-start | bytes 2211840 | tf_op jit(solution)/shard_map/reduce_scatter | solution.py:454
  226.8 8.5 %collective-permute-start.15 = (bf16[144,1152]{1,0:T(8,128)(2,1)S(1)}, bf16[144,1152]{1,0:T(8,128)(2,1)S(1)}, u32[]{:S(2)}, u32[]{:S(2)}) collective-permute-start(bf16[144,1152]{1,0:T(8,128)(2,1)S(1)} %add_convert_fusion.6), channel_id=1, source_target_pairs={{0,16},{4,20},{8,24},{12,28},{16,0},{20,4},{24,8},{28,12},{1,17},{... | collective-permute-start | bytes 995336 | tf_op jit(solution)/shard_map/ppermute | solution.py:312
  235.5 15.0 %collective-permute-start.18 = (bf16[288,1152]{1,0:T(8,128)(2,1)S(1)}, bf16[288,1152]{1,0:T(8,128)(2,1)S(1)}, u32[]{:S(2)}, u32[]{:S(2)}) collective-permute-start(bf16[288,1152]{1,0:T(8,128)(2,1)S(1)} %maximum_select_fusion.5), channel_id=1, source_target_pairs={{0,16},{4,20},{8,24},{12,28},{16,0},{20,4},{24,8},{28,12},{1,17},{... | collective-permute-start | bytes 1990664 | tf_op jit(solution)/shard_map/ppermute | solution.py:312
  237.2 15.0 %collective-permute-start.17 = (bf16[288,1152]{1,0:T(8,128)(2,1)S(1)}, bf16[288,1152]{1,0:T(8,128)(2,1)S(1)}, u32[]{:S(2)}, u32[]{:S(2)}) collective-permute-start(bf16[288,1152]{1,0:T(8,128)(2,1)S(1)} %maximum_select_fusion.4), channel_id=1, source_target_pairs={{0,8},{4,12},{8,0},{12,4},{16,24},{20,28},{24,16},{28,20},{1,9},{5... | collective-permute-start | bytes 1990664 | tf_op jit(solution)/shard_map/ppermute | solution.py:312
  253.9 119.7 %reduce-scatter.11.cloned.1.call-start = ((), (), s32[]{:S(2)}) async-start(), calls=%async_computation.10 | async-start | bytes 2211840 | tf_op jit(solution)/shard_map/reduce_scatter | solution.py:454
  290.1 5.6 %collective-permute-start.21 = (bf16[576,1152]{1,0:T(8,128)(2,1)}, bf16[576,1152]{1,0:T(8,128)(2,1)}, u32[]{:S(2)}, u32[]{:S(2)}) collective-permute-start(bf16[576,1152]{1,0:T(8,128)(2,1)} %dynamic-slice_bitcast_fusion), channel_id=1, source_target_pairs={{0,4},{4,0},{8,12},{12,8},{16,20},{20,16},{24,28},{28,24},{1,5},{5... | collective-permute-start | bytes 3981320 | tf_op jit(solution)/shard_map/ppermute | solution.py:304
  291.4 10.4 %collective-permute-start.25 = (f32[4,8,216]{2,1,0:T(8,128)S(1)}, f32[4,8,216]{2,1,0:T(8,128)S(1)}, u32[]{:S(2)}, u32[]{:S(2)}) collective-permute-start(f32[4,8,216]{2,1,0:T(8,128)S(1)} %bitcast.161), channel_id=1, source_target_pairs={{0,1},{1,2},{2,3},{3,0},{4,5},{5,6},{6,7},{7,4},{8,9},{9,10},{10,1... | collective-permute-start | bytes 82952 | tf_op jit(solution)/shard_map/ppermute | solution.py:408
  291.8 18.1 %collective-permute-start.26 = (f32[4,8,216]{2,1,0:T(8,128)S(1)}, f32[4,8,216]{2,1,0:T(8,128)}, u32[]{:S(2)}, u32[]{:S(2)}) collective-permute-start(f32[4,8,216]{2,1,0:T(8,128)S(1)} %bitcast.159), channel_id=1, source_target_pairs={{0,2},{1,3},{2,0},{3,1},{4,6},{5,7},{6,4},{7,5},{8,10},{9,11},{10,... | collective-permute-start | bytes 82952 | tf_op jit(solution)/shard_map/ppermute | solution.py:408
  293.2 16.6 %collective-permute-start.27 = (f32[4,8,216]{2,1,0:T(8,128)S(1)}, f32[4,8,216]{2,1,0:T(8,128)}, u32[]{:S(2)}, u32[]{:S(2)}) collective-permute-start(f32[4,8,216]{2,1,0:T(8,128)S(1)} %bitcast.160), channel_id=1, source_target_pairs={{0,3},{1,0},{2,1},{3,2},{4,7},{5,4},{6,5},{7,6},{8,11},{9,8},{10,9... | collective-permute-start | bytes 82952 | tf_op jit(solution)/shard_map/ppermute | solution.py:408
  298.8 12.2 %collective-permute-start.22 = (bf16[144,1152]{1,0:T(8,128)(2,1)}, bf16[144,1152]{1,0:T(8,128)(2,1)}, u32[]{:S(2)}, u32[]{:S(2)}) collective-permute-start(bf16[144,1152]{1,0:T(8,128)(2,1)} %get-tuple-element.205), channel_id=1, source_target_pairs={{0,8},{4,12},{8,0},{12,4},{16,24},{20,28},{24,16},{28,20},{1,9},{5... | collective-permute-start | bytes 995336 | tf_op jit(solution)/shard_map/ppermute | solution.py:352
  300.3 16.5 %collective-permute-start.23 = (bf16[144,1152]{1,0:T(8,128)(2,1)}, bf16[144,1152]{1,0:T(8,128)(2,1)}, u32[]{:S(2)}, u32[]{:S(2)}) collective-permute-start(bf16[144,1152]{1,0:T(8,128)(2,1)} %get-tuple-element.204), channel_id=1, source_target_pairs={{0,16},{4,20},{8,24},{12,28},{16,0},{20,4},{24,8},{28,12},{1,17},{... | collective-permute-start | bytes 995336 | tf_op jit(solution)/shard_map/ppermute | solution.py:352
  301.7 15.1 %collective-permute-start.24 = (bf16[144,1152]{1,0:T(8,128)(2,1)S(1)}, bf16[144,1152]{1,0:T(8,128)(2,1)}, u32[]{:S(2)}, u32[]{:S(2)}) collective-permute-start(bf16[144,1152]{1,0:T(8,128)(2,1)S(1)} %get-tuple-element.203), channel_id=1, source_target_pairs={{0,24},{4,28},{8,16},{12,20},{16,8},{20,12},{24,0},{28,4},{1,25},{... | collective-permute-start | bytes 995336 | tf_op jit(solution)/shard_map/ppermute | solution.py:352
  318.2 12.9 %collective-permute-start.28 = (bf16[160,1152]{1,0:T(8,128)(2,1)S(1)}, bf16[160,1152]{1,0:T(8,128)(2,1)S(1)}, u32[]{:S(2)}, u32[]{:S(2)}) collective-permute-start(bf16[160,1152]{1,0:T(8,128)(2,1)S(1)} %pad_maximum_fusion.3), channel_id=1, source_target_pairs={{0,8},{4,12},{8,0},{12,4},{16,24},{20,28},{24,16},{28,20},{1,9},{5... | collective-permute-start | bytes 1105928 | tf_op jit(solution)/shard_map/ppermute | solution.py:352
  319.4 16.9 %collective-permute-start.29 = (bf16[160,1152]{1,0:T(8,128)(2,1)S(1)}, bf16[160,1152]{1,0:T(8,128)(2,1)S(1)}, u32[]{:S(2)}, u32[]{:S(2)}) collective-permute-start(bf16[160,1152]{1,0:T(8,128)(2,1)S(1)} %pad_maximum_fusion.3), channel_id=1, source_target_pairs={{0,16},{4,20},{8,24},{12,28},{16,0},{20,4},{24,8},{28,12},{1,17},{... | collective-permute-start | bytes 1105928 | tf_op jit(solution)/shard_map/ppermute | solution.py:352
  320.2 16.1 %collective-permute-start.30 = (bf16[160,1152]{1,0:T(8,128)(2,1)S(1)}, bf16[160,1152]{1,0:T(8,128)(2,1)S(1)}, u32[]{:S(2)}, u32[]{:S(2)}) collective-permute-start(bf16[160,1152]{1,0:T(8,128)(2,1)S(1)} %pad_maximum_fusion.3), channel_id=1, source_target_pairs={{0,24},{4,28},{8,16},{12,20},{16,8},{20,12},{24,0},{28,4},{1,25},{... | collective-permute-start | bytes 1105928 | tf_op jit(solution)/shard_map/ppermute | solution.py:352
  (29 other events, 284.8 us)
Sparse Core Ops, SparseCore 0:
  12.0 42.9 all-gather.3
  65.6 47.4 reduce-scatter.4
  124.3 40.4 all-gather.5
  185.5 37.4 reduce-scatter.8
  226.8 38.5 all-gather.7
  267.6 39.4 reduce-scatter.6
  336.8 36.6 reduce-scatter.10

commit v7 on v6

--- a/solution.py
+++ b/solution.py
@@ -55,12 +55,53 @@
     return pl.pallas_call(
         body,
         grid=(grid,),
-        in_specs=[block(a.shape) if step else whole(a.shape) for a, step in ins],
+        in_specs=[
+            pl.BlockSpec(memory_space=pltpu.SMEM)
+            if step is None
+            else block(a.shape) if step else whole(a.shape)
+            for a, step in ins
+        ],
         out_specs=[block(shape) for shape, _ in outs[:moving]]
         + [whole(shape) for shape, _ in outs[moving:]],
         scratch_shapes=list(scratch),
         out_shape=[jax.ShapeDtypeStruct(shape, dtype) for shape, dtype in outs],
     )(*[a for a, _ in ins])
+
+
+def halves_body(side, left, right, own, other, total):
+    step, half = left.shape[1], own.shape[0]
+    at = pl.multiple_of(pl.program_id(0) * step, step)
+    total[pl.ds(at, step), :] = mm(left[...], right[...], TN).astype(BF16)
+
+    @pl.when(pl.program_id(0) == pl.num_programs(0) - 1)
+    def _():
+        own[...] = total[pl.ds(pl.multiple_of(side[0] * half, half), half), :]
+        other[...] = total[pl.ds(pl.multiple_of((1 - side[0]) * half, half), half), :]
+
+
+def weight_halves(left, right):
+    rows, cols = left.shape
+    width = right.shape[1]
+    step = 384 if cols % 384 == 0 else cols
+    half = jax.ShapeDtypeStruct((cols // 2, width), BF16)
+    return pl.pallas_call(
+        halves_body,
+        grid_spec=pltpu.PrefetchScalarGridSpec(
+            num_scalar_prefetch=1,
+            grid=(cols // step,),
+            in_specs=[
+                pl.BlockSpec((rows, step), lambda i, p: (0, i)),
+                pl.BlockSpec((rows, width), lambda i, p: (0, 0)),
+            ],
+            out_specs=[pl.BlockSpec((cols // 2, width), lambda i, p: (0, 0))] * 2,
+            scratch_shapes=[pltpu.VMEM((cols, width), BF16)],
+        ),
+        out_shape=[half, half],
+    )(jnp.full((1,), lax.axis_index("dp") & 1, jnp.int32), left, right)
+
+
+def modulate_body(cond, weight, bias, out):
+    out[0] = mm(cond[...], weight[0], NT) + bias[0]
 
 
 def split_call(body, start, images, group, own_ins, group_ins, outs, fixed=(), scratch=()):
@@ -160,8 +201,8 @@
 
 
 def attend_back_body(
-    head_dim, grad, qkv, routed, mixed, attended, keep, weight, out_weight,
-    mixed_grad, stats, bias_sums, part, kept,
+    head_dim, side, grad, qkv, routed, mixed, attended, keep, weight, out_weight,
+    mixed_grad, stats, bias_sums, own_part, other_part, kept,
 ):
     slots, cols = routed.shape[1], weight.shape[1]
     scale = 1.0 / math.sqrt(head_dim)
@@ -200,9 +241,21 @@
 
     @pl.when(pl.program_id(0) == pl.num_programs(0) - 1)
     def _():
-        for index in range(3):
-            part[index] = mm(kept[index], mixed[...], TN).astype(BF16)
-        part[3] = mm(attended[...], grad[...], TN).astype(BF16)
+        def put(index, value):
+            @pl.when(side[0] == index // 2)
+            def _():
+                own_part[index % 2] = value
+
+            @pl.when(side[0] != index // 2)
+            def _():
+                other_part[index % 2] = value
+
+        def product(index, carry):
+            put(index, mm(kept[index], mixed[...], TN).astype(BF16))
+            return carry
+
+        lax.fori_loop(0, 3, product, 0)
+        put(3, mm(attended[...], grad[...], TN).astype(BF16))
 
 
 def down_back_body(grad_two, mod, keep, down, down_grad, active_grad, down_sum):
@@ -495,8 +548,15 @@
     )
     small = small_gather(small).reshape(group, width + 128)
     silu_cond = jax.nn.silu(small[:, :width].astype(F32)).astype(BF16)
-    modulation = mm(silu_cond, ada_weight, NT) + ada_bias.astype(F32)
-    modulation = modulation.reshape(group, 6, width)
+    (modulation,) = call(
+        modulate_body, 6,
+        [
+            (silu_cond, False), (ada_weight.reshape(6, width, width), True),
+            (ada_bias.astype(F32).reshape(6, 1, width), True),
+        ],
+        [((6, group, width), F32)],
+    )
+    modulation = modulation.transpose(1, 0, 2)
     keep = small[:, None, width:].astype(F32)
     own_mod = lax.dynamic_slice_in_dim(modulation, here * images, images, 0)
     own_keep = jnp.broadcast_to(keep_count.astype(F32)[:, None, None], (images, 1, 128))
@@ -546,10 +606,13 @@
     mixed_two_grad = own_sum(mixed_grad)
     flat = (group * slots, hidden_units)
     wide = (group * slots, width)
-    up_part = mm(before_grad.reshape(flat), group_mixed.reshape(wide), TN).astype(BF16)
-    down_part = mm(active.reshape(flat), down_grad.reshape(wide), TN).astype(BF16)
+    up_part = weight_halves(before_grad.reshape(flat), group_mixed.reshape(wide))
+    down_part = weight_halves(active.reshape(flat), down_grad.reshape(wide))
     levels = len(dp_bits())
-    sums = halve_all((up_part, down_part), 0)
+    flights = [
+        (own, lax.ppermute(other, "dp", partner(0))) for own, other in (up_part, down_part)
+    ]
+    sums = [add_low(own, got) for own, got in lax.optimization_barrier(flights)]
     branch, gate_grad = call(
         branch_body, group,
         [
@@ -575,18 +638,19 @@
     for level in reversed(range(1, levels)):
         sums = join_all(double_all(sums, level), level)
     last = double_all(sums, 0)
-    mixed_grad, attend_stats, bias_sums, part = call(
+    mixed_grad, attend_stats, bias_sums, own_part, other_part = call(
         functools.partial(attend_back_body, head_dim), group,
         [
+            (jnp.full((1,), lax.axis_index("dp") & 1, jnp.int32), None),
             (group_grad.reshape(wide), False), (qkv, True), (group_routed, True),
             (mixed_one.reshape(wide), False), (attended.reshape(-1, cols), False),
             (after(keep, last), True), (qkv_weight, False), (out_weight, False),
         ],
         [
             (group_shape, BF16), ((group, 3, width), F32), ((group, 2, cols), F32),
-            ((4, cols, width), BF16),
-        ],
-        fixed=1,
+            ((2, cols, width), BF16), ((2, cols, width), BF16),
+        ],
+        fixed=2,
         scratch=[pltpu.VMEM((3, group * slots, cols), BF16)],
     )
     (layer_out,) = call(
@@ -598,7 +662,8 @@
         [((images, patches, width), BF16)],
     )
     mixed_one_grad = own_sum(mixed_grad)
-    half = add_low(*halve(part.reshape(4 * cols, width), 0))
+    other_part = lax.ppermute(other_part.reshape(2 * cols, width), "dp", partner(0))
+    half = add_low(own_part.reshape(2 * cols, width), other_part)
     last = after(last, half)
     blocks = trade(half)
 

time: 391 us -> 387 us (0.990); the launches traced: 384 us -> 385 us
  Pallas kernels: 83.4 us -> 107 us
  matrix products: 17.6 us -> 1.28 us
    pallas_call x7 -> x10, Pallas kernels: 47.7 us -> 71 us  [the longest x8 58.2 us: call(): pl.pallas_call(body, grid=(grid,), in_specs=[pl.BlockSpec(memory_space=pl...]
    dot_general x4 -> x1, matrix products: 17.6 us -> 1.28 us  [mm(): lax.dot_general(left, right, (dims, ((), ())), preferred_element_type=F32)]
    squeeze x7 -> x4, local copies, waits for them, and re-layouts: 6.17 us -> 1.08 us  [halve(): other = lax.dynamic_index_in_dim(halves, 1 - side, 0, keepdims=False)]
    ppermute x7 -> x4, waiting for transfers between devices: 18.9 us -> 15.5 us  [halve(): return (own, lax.ppermute(other, 'dp', partner(bit)))]
  transfers between devices with their start and end apart: 39 -> 39, of which waited for: 22 -> 23; matrix products, arithmetic and copies ran while one was open for 15% -> 11% of each run, Pallas kernels for 15% -> 19%
where the time goes in v7:
time: 387 us; the launch traced here: 385 us
  waiting for transfers between devices  168 us (43%)
  Pallas kernels  107 us (28%)
  starting transfers between devices  39.2 us (10%)
  other arithmetic  25 us (6%)
  between operations  23.1 us (6%)
  local copies, waits for them, and re-layouts  22.5 us (6%)
    pallas_call x8, Pallas kernels, call(): pl.pallas_call(body, grid=(grid,), in_specs=[pl.BlockSpec(memory_space=pl...  58.2 us
    all_gather x3, waiting for transfers between devices, all_rows(): return lax.all_gather(rows, 'mp', axis=0, tiled=True)  34.4 us
    pallas_call x4, Pallas kernels, run(): pl.pallas_call(step, grid_spec=pltpu.PrefetchScalarGridSpec(num_scalar_pr...  30.9 us
    ppermute x3, waiting for transfers between devices, chain_rows(): lax.ppermute(down, 'mp', [(i, i - 1) for i in range(count - hop, 0, -1)])  30.5 us
    reduce_scatter x4, waiting for transfers between devices, own_sum(): return lax.psum_scatter(rows, 'mp', scatter_dimension=0, tiled=True)  28.3 us
    ppermute x7, waiting for transfers between devices, double(): return (part, lax.ppermute(part, 'dp', partner(bit)))  27.6 us
    ppermute x3, waiting for transfers between devices, chain_rows(): up = lax.ppermute(up, 'mp', [(i, i + 1) for i in range(hop - 1, count - 1)])  16.6 us
    ppermute x4, waiting for transfers between devices, halve(): return (own, lax.ppermute(other, 'dp', partner(bit)))  15.5 us
  transfers between devices with their start and end apart: 39, of which 23 were waited for; matrix products, arithmetic and copies ran while one was open for 11% of the time, Pallas kernels for 19%

profile of v7, /device:TPU:0, one launch (start us, length us, event | category | flops | bytes accessed | tf_op | source)
XLA Modules:
  0.0 385.4 jit_solution(9837104007461969517)
XLA Ops:
  12.6 3.1 collective-permute-start
  23.2 9.6 %shard_map.239 = f32[6,4,1152]{2,1,0:T(4,128)} custom-call(bf16[4,1152]{1,0:T(4,128)(2,1)} %fusion.8.cond, bf16[6,1152,1152]{2,1,0:T(8,128)(2,1)} %bitcast.117, f32[6,1,1152]{2,1,0:T(1,128)} %reshape.289.bias), custom_call_target="tpu_custom_call" | custom-call | tf_op jit(solution)/shard_map/pallas_call | solution.py:55
  36.5 5.2 %shard_map.240 = (bf16[4,192,1152]{2,1,0:T(8,128)(2,1)}, bf16[4,3,192,288]{3,2,1,0:T(8,128)(2,1)}, bf16[4,192,288]{2,1,0:T(8,128)(2,1)}, bf16[4,192,1152]{2,1,0:T(8,128)(2,1)}) custom-call(s32[1]{0:T(128)} %bitcast.index, bf16[1,192,1152]{2,1,0:T(8,128)(2,1)} %get-tuple-element.103.refs_0_.routed, f32[1,6,1152]{2,1,0:T(8,128)} %copy.46.refs_1_.mod, ...), custom_call_target="tpu_custom_call" | custom-call | tf_op jit(solution)/shard_map/pallas_call | solution.py:127
  42.2 12.8 %all-gather.4.cloned.1.call-done.refs_0_.routed = bf16[4,192,1152]{2,1,0:T(8,128)(2,1)} async-done(((bf16[1,192,1152]{2,1,0:T(8,128)(2,1)}), bf16[4,192,1152]{2,1,0:T(8,128)(2,1)}) %all-gather.4.cloned.1.call-update) | async-done | bytes 1769488 | tf_op jit(solution)/shard_map/all_gather | solution.py:480
  55.0 10.4 %shard_map.241 = (bf16[4,192,1152]{2,1,0:T(8,128)(2,1)}, bf16[4,3,192,288]{3,2,1,0:T(8,128)(2,1)}, bf16[4,192,288]{2,1,0:T(8,128)(2,1)}, bf16[4,192,1152]{2,1,0:T(8,128)(2,1)}) custom-call(s32[1]{0:T(128)} %bitcast.index, ...), custom_call_target="tpu_custom_call", output_to_operand_aliasing={{0}: (7, {}), {1}: (8, {}), {2}: (9, {}), {3}: (10, {})} | custom-call | tf_op jit(solution)/shard_map/pallas_call | solution.py:127
  70.0 16.6 %collective-permute-done.3 = bf16[1,192,1152]{2,1,0:T(8,128)(2,1)S(1)} collective-permute-done((bf16[1,192,1152]{2,1,0:T(8,128)(2,1)S(1)}, bf16[1,192,1152]{2,1,0:T(8,128)(2,1)S(1)}, u32[]{:S(2)}, u32[]{:S(2)}) %collective-permute-start.3) | collective-permute-done | bytes 442400 | tf_op jit(solution)/shard_map/ppermute | solution.py:488
  87.3 14.5 %collective-permute-done.6 = bf16[1,192,1152]{2,1,0:T(8,128)(2,1)S(1)} collective-permute-done((bf16[1,192,1152]{2,1,0:T(8,128)(2,1)S(1)}, bf16[1,192,1152]{2,1,0:T(8,128)(2,1)S(1)}, u32[]{:S(2)}, u32[]{:S(2)}) %collective-permute-start.6) | collective-permute-done | bytes 442400 | tf_op jit(solution)/shard_map/ppermute | solution.py:489
  103.9 15.8 %collective-permute-done.7 = bf16[1,192,1152]{2,1,0:T(8,128)(2,1)S(1)} collective-permute-done((bf16[1,192,1152]{2,1,0:T(8,128)(2,1)S(1)}, bf16[1,192,1152]{2,1,0:T(8,128)(2,1)S(1)}, u32[]{:S(2)}, u32[]{:S(2)}) %collective-permute-start.7) | collective-permute-done | bytes 442400 | tf_op jit(solution)/shard_map/ppermute | solution.py:489
  135.5 7.4 %shard_map.243 = (bf16[4,192,1152]{2,1,0:T(8,128)(2,1)}, f32[4,192,1152]{2,1,0:T(8,128)}, f32[4,1,1152]{2,1,0:T(1,128)}) custom-call(bf16[4,192,1152]{2,1,0:T(8,128)(2,1)} %pad_maximum_fusion.1.grad_two, f32[4,6,1152]{2,1,0:T(8,128)} %bitcast.137, f32[4,1,128]{2,1,0:T(1,128)} %bitcast.144, bf16[1152,1152]{1,0:T(8,128)(2,1)} %down.3), custom_call_target="tpu_custom_call" | custom-call | tf_op jit(solution)/shard_map/pallas_call | solution.py:55
  145.0 5.3 %shard_map.244 = (bf16[4,192,1152]{2,1,0:T(8,128)(2,1)}, bf16[4,192,1152]{2,1,0:T(8,128)(2,1)}, bf16[4,192,1152]{2,1,0:T(8,128)(2,1)}, f32[4,1,1152]{2,1,0:T(1,128)}) custom-call(s32[1]{0:T(128)} %bitcast.index, bf16[1,192,1152]{2,1,0:T(8,128)(2,1)} %get-tuple-element.109.refs_0_, f32[1,192,1152]{2,1,0:T(8,128)} %constant_dynamic-slice_fusion.5.refs_1_, ...), custom_call_target="tpu_custom_call" | custom-call | tf_op jit(solution)/shard_map/pallas_call | solution.py:127
  150.3 14.5 %all-gather.6.cloned.1.call-done.refs_0_ = bf16[4,192,1152]{2,1,0:T(8,128)(2,1)} async-done(((bf16[1,192,1152]{2,1,0:T(8,128)(2,1)}), bf16[4,192,1152]{2,1,0:T(8,128)(2,1)}) %all-gather.6.cloned.1.call-update) | async-done | bytes 1769488 | tf_op jit(solution)/shard_map/all_gather | solution.py:480
  164.7 10.1 %shard_map.245 = (bf16[4,192,1152]{2,1,0:T(8,128)(2,1)}, bf16[4,192,1152]{2,1,0:T(8,128)(2,1)}, bf16[4,192,1152]{2,1,0:T(8,128)(2,1)}, f32[4,1,1152]{2,1,0:T(1,128)}) custom-call(s32[1]{0:T(128)} %bitcast.index, bf16[4,192,1152]{2,1,0:T(8,128)(2,1)} %all-gather.6.cloned.1.call-done.refs_0_, ...), custom_call_target="tpu_custom_call", output_to_operand_aliasing={{0}: (5, {}), {1}: (6, {}), {2}: (7, {}), {3}: (8, {})} | custom-call | tf_op jit(solution)/shard_map/pallas_call | solution.py:127
  174.8 6.4 %shard_map.247 = (bf16[576,1152]{1,0:T(8,128)(2,1)}, bf16[576,1152]{1,0:T(8,128)(2,1)}) custom-call(s32[1]{0:T(128)} %bitcast.28.side, bf16[768,1152]{1,0:T(8,128)(2,1)} %bitcast.118, bf16[768,1152]{1,0:T(8,128)(2,1)} %bitcast.132), custom_call_target="tpu_custom_call" | custom-call | tf_op jit(solution)/shard_map/pallas_call | solution.py:87
  181.2 6.4 %shard_map.246 = (bf16[576,1152]{1,0:T(8,128)(2,1)}, bf16[576,1152]{1,0:T(8,128)(2,1)}) custom-call(s32[1]{0:T(128)} %bitcast.28.side, bf16[768,1152]{1,0:T(8,128)(2,1)} %bitcast.121, bf16[768,1152]{1,0:T(8,128)(2,1)} %bitcast.120), custom_call_target="tpu_custom_call" | custom-call | tf_op jit(solution)/shard_map/pallas_call | solution.py:87
  188.2 2.8 collective-permute-done.9
  196.3 13.7 %collective-permute-done.12 = bf16[288,1152]{1,0:T(8,128)(2,1)S(1)} collective-permute-done((bf16[288,1152]{1,0:T(8,128)(2,1)S(1)}, bf16[288,1152]{1,0:T(8,128)(2,1)S(1)}, u32[]{:S(2)}, u32[]{:S(2)}) %collective-permute-start.12) | collective-permute-done | bytes 663584 | tf_op jit(solution)/shard_map/ppermute | solution.py:357
  216.7 6.9 %shard_map.248 = (bf16[4,192,1152]{2,1,0:T(8,128)(2,1)}, f32[4,1,1152]{2,1,0:T(1,128)}) custom-call(bf16[4,192,1152]{2,1,0:T(8,128)(2,1)} %get-tuple-element.123.active, bf16[4,192,1152]{2,1,0:T(8,128)(2,1)} %pad_maximum_fusion.1.grad_two, f32[4,1,128]{2,1,0:T(1,128)} %bitcast.145, bf16[1152,1152]{1,0:T(8,128)(2,1)} %down.3, f32[1,1152]{1,0:T(1,128)} %select_n.229.bias), custom_call_target="tpu_custom_call" | custom-call | tf_op jit(solution)/shard_map/pallas_call | solution.py:55
  225.7 2.9 shard_map.252
  230.5 3.0 collective-permute-done.16
  233.5 4.7 %collective-permute-done.15 = bf16[144,1152]{1,0:T(8,128)(2,1)S(1)} collective-permute-done((bf16[144,1152]{1,0:T(8,128)(2,1)S(1)}, bf16[144,1152]{1,0:T(8,128)(2,1)S(1)}, u32[]{:S(2)}, u32[]{:S(2)}) %collective-permute-start.15) | collective-permute-done | bytes 331808 | tf_op jit(solution)/shard_map/ppermute | solution.py:365
  241.6 12.2 %collective-permute-done.18 = bf16[288,1152]{1,0:T(8,128)(2,1)S(1)} collective-permute-done((bf16[288,1152]{1,0:T(8,128)(2,1)S(1)}, bf16[288,1152]{1,0:T(8,128)(2,1)S(1)}, u32[]{:S(2)}, u32[]{:S(2)}) %collective-permute-start.18) | collective-permute-done | bytes 663584 | tf_op jit(solution)/shard_map/ppermute | solution.py:365
  260.9 7.2 %all-gather.8.cloned.1.call-done = bf16[4,192,1152]{2,1,0:T(8,128)(2,1)} async-done(((bf16[1,192,1152]{2,1,0:T(8,128)(2,1)}), bf16[4,192,1152]{2,1,0:T(8,128)(2,1)}) %all-gather.8.cloned.1.call-update) | async-done | bytes 1769488 | tf_op jit(solution)/shard_map/all_gather | solution.py:480
  268.0 23.1 %shard_map.249 = (bf16[4,192,1152]{2,1,0:T(8,128)(2,1)}, f32[4,3,1152]{2,1,0:T(4,128)}, f32[4,2,288]{2,1,0:T(2,128)}, bf16[2,288,1152]{2,1,0:T(8,128)(2,1)}, bf16[2,288,1152]{2,1,0:T(8,128)(2,1)}) custom-call(s32[1]{0:T(128)} %bitcast.28.side, bf16[768,1152]{1,0:T(8,128)(2,1)} %bitcast.134, bf16[4,3,192,288]{3,2,1,0:T(8,128)(2,1)} %get-tuple-element.141.qkv, ...), custom_call_target="tpu_custom_call" | custom-call | tf_op jit(solution)/shard_map/pallas_call | solution.py:55
  305.1 5.1 %reduce-scatter.7.cloned.1.call-done.branch = bf16[1,192,1152]{2,1,0:T(8,128)(2,1)} async-done(((bf16[4,192,1152]{2,1,0:T(8,128)(2,1)}), bf16[1,192,1152]{2,1,0:T(8,128)(2,1)}) %reduce-scatter.7.cloned.1.call-update) | async-done | bytes 442384 | tf_op jit(solution)/shard_map/reduce_scatter | solution.py:507
  310.2 2.8 shard_map.250
  313.4 5.4 %collective-permute-done.23 = bf16[144,1152]{1,0:T(8,128)(2,1)} collective-permute-done((bf16[144,1152]{1,0:T(8,128)(2,1)}, bf16[144,1152]{1,0:T(8,128)(2,1)}, u32[]{:S(2)}, u32[]{:S(2)}) %collective-permute-start.23) | collective-permute-done | bytes 331808 | tf_op jit(solution)/shard_map/ppermute | solution.py:405
  323.7 4.8 %fusion.1 = f32[1152,1152]{1,0:T(8,128)} fusion(bf16[576,1152]{1,0:T(8,128)(2,1)} %collective-permute-done.20, bf16[576,1152]{1,0:T(8,128)(2,1)S(1)} %maximum_select_fusion.3, pred[]{:T(512)S(6)} %eq.25), kind=kLoop, calls=%fused_computation.5 | loop fusion | flops 13271040 | bytes 7962625 | tf_op jit(solution)/shard_map/convert_element_type | solution.py:692
  328.5 4.7 %fusion = f32[1152,1152]{1,0:T(8,128)} fusion(bf16[576,1152]{1,0:T(8,128)(2,1)} %collective-permute-done.19, bf16[576,1152]{1,0:T(8,128)(2,1)S(1)} %maximum_select_fusion.2, pred[]{:T(512)S(6)} %eq.25), kind=kLoop, calls=%fused_computation.3 | loop fusion | flops 13271040 | bytes 7962625 | tf_op jit(solution)/shard_map/convert_element_type | solution.py:692
  333.2 5.3 %collective-permute-done.29 = bf16[160,1152]{1,0:T(8,128)(2,1)S(1)} collective-permute-done((bf16[160,1152]{1,0:T(8,128)(2,1)S(1)}, bf16[160,1152]{1,0:T(8,128)(2,1)S(1)}, u32[]{:S(2)}, u32[]{:S(2)}) %collective-permute-start.29) | collective-permute-done | bytes 368672 | tf_op jit(solution)/shard_map/ppermute | solution.py:405
  346.9 4.6 %finish.1 = (f32[6,144,1152]{2,1,0:T(8,128)}, f32[2,144,1152]{2,1,0:T(8,128)}) custom-call(s32[2]{0:T(128)} %pad_add_fusion.places, bf16[4,160,1152]{2,1,0:T(8,128)(2,1)} %copy-done, bf16[4,160,1152]{2,1,0:T(8,128)(2,1)} %copy-done.2), custom_call_target="tpu_custom_call" | custom-call | tf_op jit(solution)/shard_map/finish/pallas_call | solution.py:442
  352.2 23.0 %reduce-scatter.11.cloned.1.call-done.mixed_grad = bf16[1,192,1152]{2,1,0:T(8,128)(2,1)} async-done(((bf16[4,192,1152]{2,1,0:T(8,128)(2,1)}), bf16[1,192,1152]{2,1,0:T(8,128)(2,1)}) %reduce-scatter.11.cloned.1.call-update) | async-done | bytes 442384 | tf_op jit(solution)/shard_map/reduce_scatter | solution.py:507
  375.2 3.3 shard_map.251
  (200 shorter events, 88.6 us)
Async XLA Ops:
  7.2 47.8 %all-gather.4.cloned.1.call-start = ((), (), s32[]{:S(2)}) async-start(), calls=%async_computation.4 | async-start | bytes 2211840 | tf_op jit(solution)/shard_map/all_gather | solution.py:480
  11.9 109.7 %reduce-scatter.5.cloned.1.call-start = ((), (), s32[]{:S(2)}) async-start(), calls=%async_computation.5 | async-start | bytes 2211840 | tf_op jit(solution)/shard_map/reduce_scatter | solution.py:507
  12.6 8.3 %collective-permute-start = (bf16[1,1280]{1,0:T(2,128)(2,1)S(1)}, bf16[1,1280]{1,0:T(2,128)(2,1)S(1)}, u32[]{:S(2)}, u32[]{:S(2)}) collective-permute-start(bf16[1,1280]{1,0:T(2,128)(2,1)S(1)} %get-tuple-element.226), channel_id=1, source_target_pairs={{0,1},{1,2},{2,3},{3,0},{4,5},{5,6},{6,7},{7,4},{8,9},{9,10},{10,1... | collective-permute-start | bytes 7688 | tf_op jit(solution)/shard_map/ppermute | solution.py:461
  65.4 99.3 %all-gather.6.cloned.1.call-start = ((), (), s32[]{:S(2)}) async-start(), calls=%async_computation.6 | async-start | bytes 2211840 | tf_op jit(solution)/shard_map/all_gather | solution.py:480
  66.4 20.3 %collective-permute-start.3 = (bf16[1,192,1152]{2,1,0:T(8,128)(2,1)S(1)}, bf16[1,192,1152]{2,1,0:T(8,128)(2,1)S(1)}, u32[]{:S(2)}, u32[]{:S(2)}) collective-permute-start(bf16[1,192,1152]{2,1,0:T(8,128)(2,1)S(1)} %copy-done.3), channel_id=1, source_target_pairs={{0,1},{1,2},{2,3},{4,5},{5,6},{6,7},{8,9},{9,10},{10,11},{12,13},{... | collective-permute-start | bytes 1327112 | tf_op jit(solution)/shard_map/ppermute | solution.py:488
  68.7 33.2 %collective-permute-start.6 = (bf16[1,192,1152]{2,1,0:T(8,128)(2,1)S(1)}, bf16[1,192,1152]{2,1,0:T(8,128)(2,1)S(1)}, u32[]{:S(2)}, u32[]{:S(2)}) collective-permute-start(bf16[1,192,1152]{2,1,0:T(8,128)(2,1)S(1)} %copy-done.3), channel_id=1, source_target_pairs={{3,2},{2,1},{1,0},{7,6},{6,5},{5,4},{11,10},{10,9},{9,8},{15,14},{... | collective-permute-start | bytes 1327112 | tf_op jit(solution)/shard_map/ppermute | solution.py:489
  86.7 16.5 %collective-permute-start.4 = (bf16[1,192,1152]{2,1,0:T(8,128)(2,1)S(1)}, bf16[1,192,1152]{2,1,0:T(8,128)(2,1)S(1)}, u32[]{:S(2)}, u32[]{:S(2)}) collective-permute-start(bf16[1,192,1152]{2,1,0:T(8,128)(2,1)S(1)} %collective-permute-done.3), channel_id=1, source_target_pairs={{1,2},{2,3},{5,6},{6,7},{9,10},{10,11},{13,14},{14,15},{17,18},{18... | collective-permute-start | bytes 1327112 | tf_op jit(solution)/shard_map/ppermute | solution.py:488
  101.9 17.8 %collective-permute-start.7 = (bf16[1,192,1152]{2,1,0:T(8,128)(2,1)S(1)}, bf16[1,192,1152]{2,1,0:T(8,128)(2,1)S(1)}, u32[]{:S(2)}, u32[]{:S(2)}) collective-permute-start(bf16[1,192,1152]{2,1,0:T(8,128)(2,1)S(1)} %collective-permute-done.6), channel_id=1, source_target_pairs={{2,1},{1,0},{6,5},{5,4},{10,9},{9,8},{14,13},{13,12},{18,17},{17,1... | collective-permute-start | bytes 1327112 | tf_op jit(solution)/shard_map/ppermute | solution.py:489
  103.2 30.1 %collective-permute-start.5 = (bf16[1,192,1152]{2,1,0:T(8,128)(2,1)S(1)}, bf16[1,192,1152]{2,1,0:T(8,128)(2,1)S(1)}, u32[]{:S(2)}, u32[]{:S(2)}) collective-permute-start(bf16[1,192,1152]{2,1,0:T(8,128)(2,1)S(1)} %collective-permute-done.4), channel_id=1, source_target_pairs={{2,3},{6,7},{10,11},{14,15},{18,19},{22,23},{26,27},{30,31}} | collective-permute-start | bytes 1327112 | tf_op jit(solution)/shard_map/ppermute | solution.py:488
  119.7 13.7 %collective-permute-start.8 = (bf16[1,192,1152]{2,1,0:T(8,128)(2,1)S(1)}, bf16[1,192,1152]{2,1,0:T(8,128)(2,1)S(1)}, u32[]{:S(2)}, u32[]{:S(2)}) collective-permute-start(bf16[1,192,1152]{2,1,0:T(8,128)(2,1)S(1)} %collective-permute-done.7), channel_id=1, source_target_pairs={{1,0},{5,4},{9,8},{13,12},{17,16},{21,20},{25,24},{29,28}} | collective-permute-start | bytes 1327112 | tf_op jit(solution)/shard_map/ppermute | solution.py:489
  124.1 101.5 %reduce-scatter.9.cloned.1.call-start = ((), (), s32[]{:S(2)}) async-start(), calls=%async_computation.8 | async-start | bytes 2211840 | tf_op jit(solution)/shard_map/reduce_scatter | solution.py:507
  181.2 7.0 %collective-permute-start.10 = (bf16[576,1152]{1,0:T(8,128)(2,1)}, bf16[576,1152]{1,0:T(8,128)(2,1)}, u32[]{:S(2)}, u32[]{:S(2)}) collective-permute-start(bf16[576,1152]{1,0:T(8,128)(2,1)} %get-tuple-element.129), channel_id=1, source_target_pairs={{0,4},{4,0},{8,12},{12,8},{16,20},{20,16},{24,28},{28,24},{1,5},{5... | collective-permute-start | bytes 3981320 | tf_op jit(solution)/shard_map/ppermute | solution.py:613
  188.2 79.9 %all-gather.8.cloned.1.call-start = ((), (), s32[]{:S(2)}) async-start(), calls=%async_computation.9 | async-start | bytes 2211840 | tf_op jit(solution)/shard_map/all_gather | solution.py:480
  192.8 17.3 %collective-permute-start.12 = (bf16[288,1152]{1,0:T(8,128)(2,1)S(1)}, bf16[288,1152]{1,0:T(8,128)(2,1)S(1)}, u32[]{:S(2)}, u32[]{:S(2)}) collective-permute-start(bf16[288,1152]{1,0:T(8,128)(2,1)S(1)} %get-tuple-element.213), channel_id=1, source_target_pairs={{0,16},{4,20},{8,24},{12,28},{16,0},{20,4},{24,8},{28,12},{1,17},{... | collective-permute-start | bytes 1990664 | tf_op jit(solution)/shard_map/ppermute | solution.py:357
  194.8 17.0 %collective-permute-start.11 = (bf16[288,1152]{1,0:T(8,128)(2,1)S(1)}, bf16[288,1152]{1,0:T(8,128)(2,1)S(1)}, u32[]{:S(2)}, u32[]{:S(2)}) collective-permute-start(bf16[288,1152]{1,0:T(8,128)(2,1)S(1)} %get-tuple-element.215), channel_id=1, source_target_pairs={{0,8},{4,12},{8,0},{12,4},{16,24},{20,28},{24,16},{28,20},{1,9},{5... | collective-permute-start | bytes 1990664 | tf_op jit(solution)/shard_map/ppermute | solution.py:357
  212.0 11.6 %collective-permute-start.14 = (bf16[144,1152]{1,0:T(8,128)(2,1)S(1)}, bf16[144,1152]{1,0:T(8,128)(2,1)}, u32[]{:S(2)}, u32[]{:S(2)}) collective-permute-start(bf16[144,1152]{1,0:T(8,128)(2,1)S(1)} %get-tuple-element.217), channel_id=1, source_target_pairs={{0,8},{4,12},{8,0},{12,4},{16,24},{20,28},{24,16},{28,20},{1,9},{5... | collective-permute-start | bytes 995336 | tf_op jit(solution)/shard_map/ppermute | solution.py:357
  214.6 9.1 %collective-permute-start.13 = (bf16[144,1152]{1,0:T(8,128)(2,1)}, bf16[144,1152]{1,0:T(8,128)(2,1)S(1)}, u32[]{:S(2)}, u32[]{:S(2)}) collective-permute-start(bf16[144,1152]{1,0:T(8,128)(2,1)} %get-tuple-element.219), channel_id=1, source_target_pairs={{0,16},{4,20},{8,24},{12,28},{16,0},{20,4},{24,8},{28,12},{1,17},{... | collective-permute-start | bytes 995336 | tf_op jit(solution)/shard_map/ppermute | solution.py:357
  224.8 8.7 %collective-permute-start.16 = (bf16[144,1152]{1,0:T(8,128)(2,1)S(1)}, bf16[144,1152]{1,0:T(8,128)(2,1)S(1)}, u32[]{:S(2)}, u32[]{:S(2)}) collective-permute-start(bf16[144,1152]{1,0:T(8,128)(2,1)S(1)} %add_convert_fusion.5), channel_id=1, source_target_pairs={{0,8},{4,12},{8,0},{12,4},{16,24},{20,28},{24,16},{28,20},{1,9},{5... | collective-permute-start | bytes 995336 | tf_op jit(solution)/shard_map/ppermute | solution.py:365
  228.6 81.6 %reduce-scatter.7.cloned.1.call-start = ((), (), s32[]{:S(2)}) async-start(), calls=%async_computation.7 | async-start | bytes 2211840 | tf_op jit(solution)/shard_map/reduce_scatter | solution.py:507
  229.0 9.2 %collective-permute-start.15 = (bf16[144,1152]{1,0:T(8,128)(2,1)S(1)}, bf16[144,1152]{1,0:T(8,128)(2,1)S(1)}, u32[]{:S(2)}, u32[]{:S(2)}) collective-permute-start(bf16[144,1152]{1,0:T(8,128)(2,1)S(1)} %add_convert_fusion.6), channel_id=1, source_target_pairs={{0,16},{4,20},{8,24},{12,28},{16,0},{20,4},{24,8},{28,12},{1,17},{... | collective-permute-start | bytes 995336 | tf_op jit(solution)/shard_map/ppermute | solution.py:365
  238.3 15.5 %collective-permute-start.18 = (bf16[288,1152]{1,0:T(8,128)(2,1)S(1)}, bf16[288,1152]{1,0:T(8,128)(2,1)S(1)}, u32[]{:S(2)}, u32[]{:S(2)}) collective-permute-start(bf16[288,1152]{1,0:T(8,128)(2,1)S(1)} %maximum_select_fusion.5), channel_id=1, source_target_pairs={{0,16},{4,20},{8,24},{12,28},{16,0},{20,4},{24,8},{28,12},{1,17},{... | collective-permute-start | bytes 1990664 | tf_op jit(solution)/shard_map/ppermute | solution.py:365
  240.1 15.2 %collective-permute-start.17 = (bf16[288,1152]{1,0:T(8,128)(2,1)S(1)}, bf16[288,1152]{1,0:T(8,128)(2,1)S(1)}, u32[]{:S(2)}, u32[]{:S(2)}) collective-permute-start(bf16[288,1152]{1,0:T(8,128)(2,1)S(1)} %maximum_select_fusion.4), channel_id=1, source_target_pairs={{0,8},{4,12},{8,0},{12,4},{16,24},{20,28},{24,16},{28,20},{1,9},{5... | collective-permute-start | bytes 1990664 | tf_op jit(solution)/shard_map/ppermute | solution.py:365
  256.9 118.3 %reduce-scatter.11.cloned.1.call-start = ((), (), s32[]{:S(2)}) async-start(), calls=%async_computation.10 | async-start | bytes 2211840 | tf_op jit(solution)/shard_map/reduce_scatter | solution.py:507
  293.3 10.2 %collective-permute-start.25 = (f32[4,8,216]{2,1,0:T(8,128)S(1)}, f32[4,8,216]{2,1,0:T(8,128)S(1)}, u32[]{:S(2)}, u32[]{:S(2)}) collective-permute-start(f32[4,8,216]{2,1,0:T(8,128)S(1)} %bitcast.149), channel_id=1, source_target_pairs={{0,1},{1,2},{2,3},{3,0},{4,5},{5,6},{6,7},{7,4},{8,9},{9,10},{10,1... | collective-permute-start | bytes 82952 | tf_op jit(solution)/shard_map/ppermute | solution.py:461
  293.8 19.2 %collective-permute-start.26 = (f32[4,8,216]{2,1,0:T(8,128)S(1)}, f32[4,8,216]{2,1,0:T(8,128)S(1)}, u32[]{:S(2)}, u32[]{:S(2)}) collective-permute-start(f32[4,8,216]{2,1,0:T(8,128)S(1)} %bitcast.147), channel_id=1, source_target_pairs={{0,2},{1,3},{2,0},{3,1},{4,6},{5,7},{6,4},{7,5},{8,10},{9,11},{10,... | collective-permute-start | bytes 82952 | tf_op jit(solution)/shard_map/ppermute | solution.py:461
  295.2 17.8 %collective-permute-start.27 = (f32[4,8,216]{2,1,0:T(8,128)S(1)}, f32[4,8,216]{2,1,0:T(8,128)S(1)}, u32[]{:S(2)}, u32[]{:S(2)}) collective-permute-start(f32[4,8,216]{2,1,0:T(8,128)S(1)} %bitcast.148), channel_id=1, source_target_pairs={{0,3},{1,0},{2,1},{3,2},{4,7},{5,4},{6,5},{7,6},{8,11},{9,8},{10,9... | collective-permute-start | bytes 82952 | tf_op jit(solution)/shard_map/ppermute | solution.py:461
  300.6 12.8 %collective-permute-start.22 = (bf16[144,1152]{1,0:T(8,128)(2,1)}, bf16[144,1152]{1,0:T(8,128)(2,1)}, u32[]{:S(2)}, u32[]{:S(2)}) collective-permute-start(bf16[144,1152]{1,0:T(8,128)(2,1)} %get-tuple-element.211), channel_id=1, source_target_pairs={{0,8},{4,12},{8,0},{12,4},{16,24},{20,28},{24,16},{28,20},{1,9},{5... | collective-permute-start | bytes 995336 | tf_op jit(solution)/shard_map/ppermute | solution.py:405
  302.1 16.7 %collective-permute-start.23 = (bf16[144,1152]{1,0:T(8,128)(2,1)}, bf16[144,1152]{1,0:T(8,128)(2,1)}, u32[]{:S(2)}, u32[]{:S(2)}) collective-permute-start(bf16[144,1152]{1,0:T(8,128)(2,1)} %get-tuple-element.210), channel_id=1, source_target_pairs={{0,16},{4,20},{8,24},{12,28},{16,0},{20,4},{24,8},{28,12},{1,17},{... | collective-permute-start | bytes 995336 | tf_op jit(solution)/shard_map/ppermute | solution.py:405
  303.6 15.2 %collective-permute-start.24 = (bf16[144,1152]{1,0:T(8,128)(2,1)S(1)}, bf16[144,1152]{1,0:T(8,128)(2,1)}, u32[]{:S(2)}, u32[]{:S(2)}) collective-permute-start(bf16[144,1152]{1,0:T(8,128)(2,1)S(1)} %get-tuple-element.209), channel_id=1, source_target_pairs={{0,24},{4,28},{8,16},{12,20},{16,8},{20,12},{24,0},{28,4},{1,25},{... | collective-permute-start | bytes 995336 | tf_op jit(solution)/shard_map/ppermute | solution.py:405
  320.1 13.0 %collective-permute-start.28 = (bf16[160,1152]{1,0:T(8,128)(2,1)S(1)}, bf16[160,1152]{1,0:T(8,128)(2,1)S(1)}, u32[]{:S(2)}, u32[]{:S(2)}) collective-permute-start(bf16[160,1152]{1,0:T(8,128)(2,1)S(1)} %pad_maximum_fusion.3), channel_id=1, source_target_pairs={{0,8},{4,12},{8,0},{12,4},{16,24},{20,28},{24,16},{28,20},{1,9},{5... | collective-permute-start | bytes 1105928 | tf_op jit(solution)/shard_map/ppermute | solution.py:405
  321.4 17.1 %collective-permute-start.29 = (bf16[160,1152]{1,0:T(8,128)(2,1)S(1)}, bf16[160,1152]{1,0:T(8,128)(2,1)S(1)}, u32[]{:S(2)}, u32[]{:S(2)}) collective-permute-start(bf16[160,1152]{1,0:T(8,128)(2,1)S(1)} %pad_maximum_fusion.3), channel_id=1, source_target_pairs={{0,16},{4,20},{8,24},{12,28},{16,0},{20,4},{24,8},{28,12},{1,17},{... | collective-permute-start | bytes 1105928 | tf_op jit(solution)/shard_map/ppermute | solution.py:405
  322.2 16.3 %collective-permute-start.30 = (bf16[160,1152]{1,0:T(8,128)(2,1)S(1)}, bf16[160,1152]{1,0:T(8,128)(2,1)S(1)}, u32[]{:S(2)}, u32[]{:S(2)}) collective-permute-start(bf16[160,1152]{1,0:T(8,128)(2,1)S(1)} %pad_maximum_fusion.3), channel_id=1, source_target_pairs={{0,24},{4,28},{8,16},{12,20},{16,8},{20,12},{24,0},{28,4},{1,25},{... | collective-permute-start | bytes 1105928 | tf_op jit(solution)/shard_map/ppermute | solution.py:405
  (28 other events, 343.1 us)
Sparse Core Ops, SparseCore 0:
  12.0 42.9 all-gather.3
  65.5 47.4 reduce-scatter.4
  124.2 40.4 all-gather.5
  188.3 37.2 reduce-scatter.8
  228.7 39.2 all-gather.7
  270.8 39.4 reduce-scatter.6
  339.0 36.1 reduce-scatter.10
